TPU v7x, 32 devices: a whole 2x2x4 slice. The times are simulated.
32 devices in a mesh: batch: 8 (over y, x, core), mp: 4 (over z).
Axes of the slice: x: 2, y: 2, z: 4, core: 2. Of those that a mesh axis runs over, the one named last changes fastest.
Arguments:
- hidden_in: bfloat16 [16, 512, 768], P('batch', 'mp'), may hold values from -6 to 6
- memory: bfloat16 [16, 1024, 768], P('batch', 'mp'), may hold values from -6 to 6
- tgt_len: int32 [16], P('batch'), may hold values from 256 to 512, as said below
- src_len: int32 [16], P('batch'), may hold values from 128 to 1024, as said below
- target_ids: int32 [16, 512], P('batch'), may hold values from 0 to 32127
- task_ids: int32 [16], P('batch'), may hold values from 0 to 2
- task_weight: float32 [3], replicated, may hold values from 3 to 30
- gain_self: bfloat16 [768], P('batch'), may hold values from 0.25 to 1.75
- q_self: bfloat16 [768, 768], P('batch', 'mp'), may hold values from -0.0546875 to 0.0546875
- k_self: bfloat16 [768, 768], P('batch', 'mp'), may hold values from -0.21875 to 0.21875
- v_self: bfloat16 [768, 768], P('batch', 'mp'), may hold values from -0.21875 to 0.21875
- o_self: bfloat16 [768, 768], P('batch', 'mp'), may hold values from -0.875 to 0.875
- gain_cross: bfloat16 [768], P('batch'), may hold values from 0.25 to 1.75
- q_cross: bfloat16 [768, 768], P('batch', 'mp'), may hold values from -0.0546875 to 0.0546875
- k_cross: bfloat16 [768, 768], P('batch', 'mp'), may hold values from -0.21875 to 0.21875
- v_cross: bfloat16 [768, 768], P('batch', 'mp'), may hold values from -0.21875 to 0.21875
- o_cross: bfloat16 [768, 768], P('batch', 'mp'), may hold values from -0.875 to 0.875
- gain_mlp: bfloat16 [768], P('batch'), may hold values from 0.25 to 1.75
- mlp_gate: bfloat16 [768, 2048], P('batch', 'mp'), may hold values from -0.21875 to 0.21875
- mlp_up: bfloat16 [768, 2048], P('batch', 'mp'), may hold values from -0.21875 to 0.21875
- mlp_down: bfloat16 [768, 2048], P('batch', 'mp'), may hold values from -0.1875 to 0.1875
- gain_exit: bfloat16 [768], P('batch'), may hold values from 0.25 to 1.75
- embed_table: bfloat16 [768, 32128], P('batch', 'mp'), may hold values from -12 to 12
Outputs:
- block_out: bfloat16 [16, 512, 768], P('batch', 'mp')
- pair_loss: float32 [16], P('batch')
- hidden_grad: float32 [16, 512, 768], P('batch', 'mp')
- memory_grad: float32 [16, 1024, 768], P('batch', 'mp')
- gain_self_grad: float32 [768], P('batch')
- q_self_grad: float32 [768, 768], P('batch', 'mp')
- k_self_grad: float32 [768, 768], P('batch', 'mp')
- v_self_grad: float32 [768, 768], P('batch', 'mp')
- o_self_grad: float32 [768, 768], P('batch', 'mp')
- gain_cross_grad: float32 [768], P('batch')
- q_cross_grad: float32 [768, 768], P('batch', 'mp')
- k_cross_grad: float32 [768, 768], P('batch', 'mp')
- v_cross_grad: float32 [768, 768], P('batch', 'mp')
- o_cross_grad: float32 [768, 768], P('batch', 'mp')
- gain_mlp_grad: float32 [768], P('batch')
- mlp_gate_grad: float32 [768, 2048], P('batch', 'mp')
- mlp_up_grad: float32 [768, 2048], P('batch', 'mp')
- mlp_down_grad: float32 [768, 2048], P('batch', 'mp')
- gain_exit_grad: float32 [768], P('batch')
- embed_table_grad: float32 [768, 32128], P('batch', 'mp')
Inputs may be any that keep to these rules, and one draw needn't show every extreme that they name: `tgt_len`: some pair has a target of exactly 512 positions. `src_len`: some pair has a source of exactly 1024 positions.
All inputs are finite; a program needn't handle non-finite values.
Results may differ from a plain program's by a relative error of at most 0.025.
The roundings to bfloat16 on the way count: a program that leaves them out, or rounds other values in their place, can miss the bound.
Values may be sent and summed in bfloat16 or wider, within the bound.
No kernel may reach another device: no remote copies, remote signals or barrier semaphores. Data moves between devices by JAX's collectives and lax.ppermute only.
A program may use at most 320 MiB of HBM per device.

v0:
```python
import jax
import jax.numpy as jnp
from jax import lax
from jax.sharding import PartitionSpec as P

D = 768
DH = 64
TASKS = 3
TGT = 512
SRC = 1024


EPSILON = 1e-06
MASKED_OUT = -1000000000.0
GELU_SCALE = 0.7978845608028654


def joined(value, axis, join):
    pieces = jax.tree.map(lambda part: lax.all_gather(part, axis), value)
    head = jax.tree.map(lambda part: part[0], pieces)
    tail = jax.tree.map(lambda part: part[1:], pieces)
    so_far, _ = lax.scan(lambda so_far, share: (join(so_far, share), None), head, tail)
    return so_far


def gelu_tanh(values):
    return (
        0.5 * values * (1.0 + jnp.tanh(GELU_SCALE * (values + 0.044715 * values * values * values)))
    )


def gated_unit(gate_in, up_in):
    return gelu_tanh(gate_in) * up_in


def norm_rows(values, gain_vec):
    inverse = lax.rsqrt(jnp.mean(values * values, -1, keepdims=True) + EPSILON)
    return (values * inverse * gain_vec, inverse)


def norm_back(values, inverse, gain_vec, upstream):
    scaled = upstream * gain_vec
    inner_sum = jnp.mean(scaled * values, -1, keepdims=True)
    d_values = inverse * scaled - values * (inverse * inverse * inverse) * inner_sum
    d_gain = jnp.sum(upstream * values * inverse, axis=(0, 1))
    return (d_values, d_gain)


def project(row_block, weight):
    return jnp.einsum("ptd,de->pte", row_block, weight, preferred_element_type=jnp.float32)


def project_back(d_block, weight):
    return jnp.einsum("pte,de->ptd", d_block, weight, preferred_element_type=jnp.float32)


def weight_grad(row_block, d_block):
    return jnp.einsum("ptd,pte->de", row_block, d_block, preferred_element_type=jnp.float32)


def split_heads(values):
    return values.reshape(values.shape[0], values.shape[1], -1, DH)


def join_heads(values):
    return values.reshape(values.shape[0], values.shape[1], -1).astype(jnp.bfloat16)


def attend_pair(queries, key_rows, value_rows, allowed):
    scores = jnp.einsum("qhd,khd->hqk", queries, key_rows, preferred_element_type=jnp.float32)
    scores = jnp.where(allowed[None], scores, MASKED_OUT)
    highest = jnp.max(scores, -1, keepdims=True)
    raised = jnp.exp(scores - highest)
    totals = jnp.sum(raised, -1, keepdims=True)
    attn_weights = (raised / totals).astype(jnp.bfloat16)
    mixed = jnp.einsum("hqk,khd->qhd", attn_weights, value_rows, preferred_element_type=jnp.float32)
    return (mixed, (highest + jnp.log(totals))[..., 0])


def attend_back(queries, key_rows, value_rows, allowed, log_totals, d_mixed):
    scores = jnp.einsum("qhd,khd->hqk", queries, key_rows, preferred_element_type=jnp.float32)
    scores = jnp.where(allowed[None], scores, MASKED_OUT)
    attn_weights = jnp.exp(scores - log_totals[..., None])
    d_weights = jnp.einsum("qhd,khd->hqk", d_mixed, value_rows, preferred_element_type=jnp.float32)
    inner_sum = jnp.sum(attn_weights * d_weights, -1, keepdims=True)
    d_scores = (attn_weights * (d_weights - inner_sum)).astype(jnp.bfloat16)
    d_queries = jnp.einsum("hqk,khd->qhd", d_scores, key_rows, preferred_element_type=jnp.float32)
    d_keys = jnp.einsum("hqk,qhd->khd", d_scores, queries, preferred_element_type=jnp.float32)
    d_values = jnp.einsum(
        "hqk,qhd->khd",
        attn_weights.astype(jnp.bfloat16),
        d_mixed,
        preferred_element_type=jnp.float32,
    )
    return (d_queries, d_keys, d_values)


def combine_totals(former, latter):
    high_a, sum_a, pick_a = former
    high_b, sum_b, pick_b = latter
    highest = jnp.maximum(high_a, high_b)
    return (
        highest,
        sum_a * jnp.exp(high_a - highest) + sum_b * jnp.exp(high_b - highest),
        pick_a + pick_b,
    )


def spread_rows(normed):
    return lax.all_gather(normed.astype(jnp.bfloat16), "mp", axis=1, tiled=True)


def collect_rows(terms):
    return lax.psum_scatter(terms, "mp", scatter_dimension=1, tiled=True)


def spread_grads(d_residual):
    return lax.all_gather(d_residual.astype(jnp.bfloat16), "mp", axis=1, tiled=True)


def collect_grads(terms):
    return lax.psum_scatter(terms, "mp", scatter_dimension=1, tiled=True)


def local(
    hidden_in,
    memory,
    tgt_len,
    src_len,
    target_ids,
    task_ids,
    task_weight,
    gain_self,
    q_self,
    k_self,
    v_self,
    o_self,
    gain_cross,
    q_cross,
    k_cross,
    v_cross,
    o_cross,
    gain_mlp,
    mlp_gate,
    mlp_up,
    mlp_down,
    gain_exit,
    embed_table,
):
    (
        gain_self,
        q_self,
        k_self,
        v_self,
        o_self,
        gain_cross,
        q_cross,
        k_cross,
        v_cross,
        o_cross,
        gain_mlp,
        mlp_gate,
        mlp_up,
        mlp_down,
        gain_exit,
        embed_table,
    ) = (
        lax.all_gather(gain_self, "batch", axis=0, tiled=True),
        lax.all_gather(q_self, "batch", axis=0, tiled=True),
        lax.all_gather(k_self, "batch", axis=0, tiled=True),
        lax.all_gather(v_self, "batch", axis=0, tiled=True),
        lax.all_gather(o_self, "batch", axis=0, tiled=True),
        lax.all_gather(gain_cross, "batch", axis=0, tiled=True),
        lax.all_gather(q_cross, "batch", axis=0, tiled=True),
        lax.all_gather(k_cross, "batch", axis=0, tiled=True),
        lax.all_gather(v_cross, "batch", axis=0, tiled=True),
        lax.all_gather(o_cross, "batch", axis=0, tiled=True),
        lax.all_gather(gain_mlp, "batch", axis=0, tiled=True),
        lax.all_gather(mlp_gate, "batch", axis=0, tiled=True),
        lax.all_gather(mlp_up, "batch", axis=0, tiled=True),
        lax.all_gather(mlp_down, "batch", axis=0, tiled=True),
        lax.all_gather(gain_exit, "batch", axis=0, tiled=True),
        lax.all_gather(embed_table, "batch", axis=0, tiled=True),
    )
    positions = jnp.arange(TGT)
    sources = jnp.arange(SRC)
    causal = positions[None, :] <= positions[:, None]

    def self_allowed(length):
        return causal & (positions[None, :] < length)

    def cross_allowed(length):
        return jnp.broadcast_to(sources[None, :] < length, (TGT, SRC))

    def self_forward(inputs):
        queries, key_rows, value_rows, length = inputs
        return attend_pair(queries, key_rows, value_rows, self_allowed(length))

    def cross_forward(inputs):
        queries, key_rows, value_rows, length = inputs
        return attend_pair(queries, key_rows, value_rows, cross_allowed(length))

    def self_backward(inputs):
        queries, key_rows, value_rows, length, log_totals, d_mixed = inputs
        return attend_back(queries, key_rows, value_rows, self_allowed(length), log_totals, d_mixed)

    def cross_backward(inputs):
        queries, key_rows, value_rows, length, log_totals, d_mixed = inputs
        return attend_back(
            queries, key_rows, value_rows, cross_allowed(length), log_totals, d_mixed
        )

    residual = hidden_in.astype(jnp.float32)
    normed_one, inverse_one = norm_rows(residual, gain_self)
    rows_one = spread_rows(normed_one)
    memory_all = lax.all_gather(memory, "mp", axis=1, tiled=True)
    queries_one = project(rows_one, q_self).astype(jnp.bfloat16)
    keys_one = project(rows_one, k_self).astype(jnp.bfloat16)
    values_one = project(rows_one, v_self).astype(jnp.bfloat16)
    mixed_one, lse_one = lax.map(
        self_forward,
        (split_heads(queries_one), split_heads(keys_one), split_heads(values_one), tgt_len),
    )
    attended_one = join_heads(mixed_one)
    residual_one = residual + collect_rows(project_back(attended_one, o_self))
    normed_two, inverse_two = norm_rows(residual_one, gain_cross)
    rows_two = spread_rows(normed_two)
    queries_two = project(rows_two, q_cross).astype(jnp.bfloat16)
    keys_two = project(memory_all, k_cross).astype(jnp.bfloat16)
    values_two = project(memory_all, v_cross).astype(jnp.bfloat16)
    mixed_two, lse_two = lax.map(
        cross_forward,
        (split_heads(queries_two), split_heads(keys_two), split_heads(values_two), src_len),
    )
    attended_two = join_heads(mixed_two)
    residual_two = residual_one + collect_rows(project_back(attended_two, o_cross))
    normed_three, inverse_three = norm_rows(residual_two, gain_mlp)
    rows_three = spread_rows(normed_three)
    gate = project(rows_three, mlp_gate)
    up_proj = project(rows_three, mlp_up)
    hidden = gated_unit(gate, up_proj).astype(jnp.bfloat16)
    residual_three = residual_two + collect_rows(project_back(hidden, mlp_down))
    block_out = residual_three.astype(jnp.bfloat16)
    normed_four, inverse_four = norm_rows(residual_three, gain_exit)
    rows_four = spread_rows(normed_four)
    vocab_local = embed_table.shape[1]
    local_ids = target_ids - lax.axis_index("mp") * vocab_local
    columns = jnp.arange(vocab_local)
    logit_scale = D ** (-0.5)

    def head_forward(inputs):
        row_block, id_rows = inputs
        logits = jnp.dot(row_block, embed_table, preferred_element_type=jnp.float32) * logit_scale
        highest = jnp.max(logits, -1)
        totals = jnp.sum(jnp.exp(logits - highest[:, None]), -1)
        picked = jnp.sum(jnp.where(columns[None, :] == id_rows[:, None], logits, 0.0), -1)
        return (logits, highest, totals, picked)

    logits, highest, totals, picked = lax.map(head_forward, (rows_four, local_ids))
    highest, totals, picked = joined((highest, totals, picked), "mp", combine_totals)
    log_totals = highest + jnp.log(totals)
    valid_rows = (positions[None, :] < tgt_len[:, None]).astype(jnp.float32)
    losses = (log_totals - picked) * valid_rows
    pair_loss = jnp.sum(losses, -1) / tgt_len.astype(jnp.float32)
    task_scale = jnp.sum(
        jnp.where(task_ids[:, None] == jnp.arange(TASKS)[None, :], task_weight[None, :], 0.0), -1
    )
    row_scale = task_scale[:, None] * valid_rows * logit_scale

    def head_back(running, inputs):
        logit_block, row_block, id_rows, lse_rows, scale_rows = inputs
        attn_weights = jnp.exp(logit_block - lse_rows[:, None])
        onehot = (columns[None, :] == id_rows[:, None]).astype(jnp.float32)
        d_logits = ((attn_weights - onehot) * scale_rows[:, None]).astype(jnp.bfloat16)
        d_rows = jnp.einsum("tv,dv->td", d_logits, embed_table, preferred_element_type=jnp.float32)
        running = running + jnp.einsum(
            "td,tv->dv", row_block, d_logits, preferred_element_type=jnp.float32
        )
        return (running, d_rows)

    embed_grad, d_rows_four = lax.scan(
        head_back,
        jnp.zeros(embed_table.shape, jnp.float32),
        (logits, rows_four, local_ids, log_totals, row_scale),
    )
    d_residual, gain_exit_grad = norm_back(
        residual_three, inverse_four, gain_exit, collect_grads(d_rows_four)
    )
    d_branch = spread_grads(d_residual)
    d_hidden = project(d_branch, mlp_down)
    down_grad = weight_grad(d_branch, hidden)
    unused_value, pullback = jax.vjp(gated_unit, gate, up_proj)
    d_gate, d_up = pullback(d_hidden)
    d_gate = d_gate.astype(jnp.bfloat16)
    d_up = d_up.astype(jnp.bfloat16)
    gate_grad = weight_grad(rows_three, d_gate)
    up_grad = weight_grad(rows_three, d_up)
    d_rows = project_back(d_gate, mlp_gate) + project_back(d_up, mlp_up)
    d_input, gain_mlp_grad = norm_back(residual_two, inverse_three, gain_mlp, collect_grads(d_rows))
    d_residual = d_residual + d_input
    gate_sum, up_sum, down_sum, embed_sum = (gate_grad, up_grad, down_grad, embed_grad)
    d_branch = spread_grads(d_residual)
    d_attended = project(d_branch, o_cross).astype(jnp.bfloat16)
    out_cross_grad = weight_grad(d_branch, attended_two)
    d_queries, d_keys, d_values = lax.map(
        cross_backward,
        (
            split_heads(queries_two),
            split_heads(keys_two),
            split_heads(values_two),
            src_len,
            lse_two,
            split_heads(d_attended),
        ),
    )
    d_queries = join_heads(d_queries)
    d_keys = join_heads(d_keys)
    d_values = join_heads(d_values)
    query_cross_grad = weight_grad(rows_two, d_queries)
    key_cross_grad = weight_grad(memory_all, d_keys)
    value_cross_grad = weight_grad(memory_all, d_values)
    memory_terms = project_back(d_keys, k_cross) + project_back(d_values, v_cross)
    memory_grad = lax.psum_scatter(memory_terms, "mp", scatter_dimension=1, tiled=True)
    d_input, gain_cross_grad = norm_back(
        residual_one, inverse_two, gain_cross, collect_grads(project_back(d_queries, q_cross))
    )
    d_residual = d_residual + d_input
    d_branch = spread_grads(d_residual)
    d_attended = project(d_branch, o_self).astype(jnp.bfloat16)
    out_self_grad = weight_grad(d_branch, attended_one)
    d_queries, d_keys, d_values = lax.map(
        self_backward,
        (
            split_heads(queries_one),
            split_heads(keys_one),
            split_heads(values_one),
            tgt_len,
            lse_one,
            split_heads(d_attended),
        ),
    )
    d_queries = join_heads(d_queries)
    d_keys = join_heads(d_keys)
    d_values = join_heads(d_values)
    query_self_grad = weight_grad(rows_one, d_queries)
    key_self_grad = weight_grad(rows_one, d_keys)
    value_self_grad = weight_grad(rows_one, d_values)
    d_rows = (
        project_back(d_queries, q_self)
        + project_back(d_keys, k_self)
        + project_back(d_values, v_self)
    )
    d_input, gain_self_grad = norm_back(residual, inverse_one, gain_self, collect_grads(d_rows))
    hidden_grad = d_residual + d_input
    gain_self_grad, gain_cross_grad, gain_mlp_grad, gain_exit_grad = lax.psum(
        (gain_self_grad, gain_cross_grad, gain_mlp_grad, gain_exit_grad), "mp"
    )
    (
        gain_self_grad,
        gain_cross_grad,
        gain_mlp_grad,
        gain_exit_grad,
        query_self_grad,
        key_self_grad,
        value_self_grad,
        out_self_grad,
        query_cross_grad,
        key_cross_grad,
        value_cross_grad,
        out_cross_grad,
        gate_sum,
        up_sum,
        down_sum,
        embed_sum,
    ) = (
        lax.psum_scatter(gain_self_grad, "batch", scatter_dimension=0, tiled=True),
        lax.psum_scatter(gain_cross_grad, "batch", scatter_dimension=0, tiled=True),
        lax.psum_scatter(gain_mlp_grad, "batch", scatter_dimension=0, tiled=True),
        lax.psum_scatter(gain_exit_grad, "batch", scatter_dimension=0, tiled=True),
        lax.psum_scatter(query_self_grad, "batch", scatter_dimension=0, tiled=True),
        lax.psum_scatter(key_self_grad, "batch", scatter_dimension=0, tiled=True),
        lax.psum_scatter(value_self_grad, "batch", scatter_dimension=0, tiled=True),
        lax.psum_scatter(out_self_grad, "batch", scatter_dimension=0, tiled=True),
        lax.psum_scatter(query_cross_grad, "batch", scatter_dimension=0, tiled=True),
        lax.psum_scatter(key_cross_grad, "batch", scatter_dimension=0, tiled=True),
        lax.psum_scatter(value_cross_grad, "batch", scatter_dimension=0, tiled=True),
        lax.psum_scatter(out_cross_grad, "batch", scatter_dimension=0, tiled=True),
        lax.psum_scatter(gate_sum, "batch", scatter_dimension=0, tiled=True),
        lax.psum_scatter(up_sum, "batch", scatter_dimension=0, tiled=True),
        lax.psum_scatter(down_sum, "batch", scatter_dimension=0, tiled=True),
        lax.psum_scatter(embed_sum, "batch", scatter_dimension=0, tiled=True),
    )
    return (
        block_out,
        pair_loss,
        hidden_grad,
        memory_grad,
        gain_self_grad,
        query_self_grad,
        key_self_grad,
        value_self_grad,
        out_self_grad,
        gain_cross_grad,
        query_cross_grad,
        key_cross_grad,
        value_cross_grad,
        out_cross_grad,
        gain_mlp_grad,
        gate_sum,
        up_sum,
        down_sum,
        gain_exit_grad,
        embed_sum,
    )


def solution(mesh):
    in_specs = (
        P("batch", "mp", None),
        P("batch", "mp", None),
        P("batch"),
        P("batch"),
        P("batch", None),
        P("batch"),
        P(),
        P("batch"),
        P("batch", "mp"),
        P("batch", "mp"),
        P("batch", "mp"),
        P("batch", "mp"),
        P("batch"),
        P("batch", "mp"),
        P("batch", "mp"),
        P("batch", "mp"),
        P("batch", "mp"),
        P("batch"),
        P("batch", "mp"),
        P("batch", "mp"),
        P("batch", "mp"),
        P("batch"),
        P("batch", "mp"),
    )
    out_specs = (
        P("batch", "mp", None),
        P("batch"),
        P("batch", "mp", None),
        P("batch", "mp", None),
        P("batch"),
        P("batch", "mp"),
        P("batch", "mp"),
        P("batch", "mp"),
        P("batch", "mp"),
        P("batch"),
        P("batch", "mp"),
        P("batch", "mp"),
        P("batch", "mp"),
        P("batch", "mp"),
        P("batch"),
        P("batch", "mp"),
        P("batch", "mp"),
        P("batch", "mp"),
        P("batch"),
        P("batch", "mp"),
    )
    return jax.shard_map(local, mesh=mesh, in_specs=in_specs, out_specs=out_specs, check_vma=False)
```

profile of v0, /device:TPU:0, one launch (start us, length us, event | category | flops | bytes accessed | tf_op | source)
XLA Modules:
  0.0 1872.8 jit_solution(12079838616149719970)
XLA Ops:
  86.7 59.6 %reduce-scatter.25.cloned.1.call-done = f32[2,128,768]{2,1,0:T(8,128)} async-done(((f32[2,512,768]{2,1,0:T(8,128)}), f32[2,128,768]{2,1,0:T(8,128)}) %reduce-scatter.25.cloned.1.call-update) | async-done | bytes 786448 | tf_op jit(solution)/shard_map/reduce_scatter | solution.py:114
  266.9 58.6 %reduce-scatter.27.cloned.1.call-done = f32[2,128,768]{2,1,0:T(8,128)} async-done(((f32[2,512,768]{2,1,0:T(8,128)}), f32[2,128,768]{2,1,0:T(8,128)}) %reduce-scatter.27.cloned.1.call-update) | async-done | bytes 786448 | tf_op jit(solution)/shard_map/reduce_scatter | solution.py:114
  375.1 58.6 %reduce-scatter.29.cloned.1.call-done = f32[2,128,768]{2,1,0:T(8,128)} async-done(((f32[2,512,768]{2,1,0:T(8,128)}), f32[2,128,768]{2,1,0:T(8,128)}) %reduce-scatter.29.cloned.1.call-update) | async-done | bytes 786448 | tf_op jit(solution)/shard_map/reduce_scatter | solution.py:114
  446.8 39.0 %all-gather.24.cloned.1.call-done = bf16[2,512,768]{2,1,0:T(8,128)(2,1)} async-done(((bf16[2,128,768]{2,1,0:T(8,128)(2,1)}), bf16[2,512,768]{2,1,0:T(8,128)(2,1)}) %all-gather.24.cloned.1.call-update) | async-done | bytes 1572880 | tf_op jit(solution)/shard_map/all_gather | solution.py:110
  485.8 69.7 %while.111 = (s32[]{:T(128)}, f32[2,512,8032]{1,2,0:T(8,128)}, f32[2,512]{1,0:T(2,128)S(1)}, f32[2,512]{1,0:T(2,128)S(1)}, f32[2,512]{1,0:T(2,128)S(1)}, /*index...) while((s32[]{:T(128)}, f32[2,512,8032]{1,2,0:T(8,128)}, ...), condition=%wide.region_19.20_spmd.clone.clone, body=%wide.region_15.19_spmd.clone.sunk.clone | while | flops 6353631744 | bytes 78998616 | solution.py:259
  596.2 141.9 %while.114 = (s32[]{:T(128)}, f32[768,8032]{0,1:T(8,128)}, f32[2,512,768]{2,1,0:T(8,128)}, bf16[2,512,768]{2,1,0:T(8,128)(2,1)}, f32[2,512,8032]{1,2,0:T(8,128)}...) while((s32[]{:T(128)}, f32[768,8032]{0,1:T(8,128)}, ...), condition=%wide.region_25.26_spmd.clone.clone.clone, body=%wide.region_24.25_spmd.clone.clone.sunk.clone | while | flops 12694929408 | bytes 169173648 | solution.py:281
  738.2 59.2 %reduce-scatter.31.cloned.1.call-done = f32[2,128,768]{2,1,0:T(8,128)} async-done(((f32[2,512,768]{2,1,0:T(8,128)}), f32[2,128,768]{2,1,0:T(8,128)}) %reduce-scatter.31.cloned.1.call-update) | async-done | bytes 786448 | tf_op jit(solution)/shard_map/reduce_scatter | solution.py:122
  801.4 36.9 %all-gather.28.cloned.1.call-done = bf16[2,512,768]{2,1,0:T(8,128)(2,1)} async-done(((bf16[2,128,768]{2,1,0:T(8,128)(2,1)}), bf16[2,512,768]{2,1,0:T(8,128)(2,1)}) %all-gather.28.cloned.1.call-update) | async-done | bytes 1572880 | tf_op jit(solution)/shard_map/all_gather | solution.py:118
  847.9 59.0 %reduce-scatter.33.cloned.1.call-done = f32[2,128,768]{2,1,0:T(8,128)} async-done(((f32[2,512,768]{2,1,0:T(8,128)}), f32[2,128,768]{2,1,0:T(8,128)}) %reduce-scatter.33.cloned.1.call-update) | async-done | bytes 786448 | tf_op jit(solution)/shard_map/reduce_scatter | solution.py:122
  912.1 37.0 %all-gather.30.cloned.1.call-done = bf16[2,512,768]{2,1,0:T(8,128)(2,1)} async-done(((bf16[2,128,768]{2,1,0:T(8,128)(2,1)}), bf16[2,512,768]{2,1,0:T(8,128)(2,1)}) %all-gather.30.cloned.1.call-update) | async-done | bytes 1572880 | tf_op jit(solution)/shard_map/all_gather | solution.py:118
  977.0 59.2 %reduce-scatter.35.cloned.1.call-done = f32[2,128,768]{2,1,0:T(8,128)} async-done(((f32[2,512,768]{2,1,0:T(8,128)}), f32[2,128,768]{2,1,0:T(8,128)}) %reduce-scatter.35.cloned.1.call-update) | async-done | bytes 786448 | tf_op jit(solution)/shard_map/reduce_scatter | solution.py:122
  1041.0 36.9 %all-gather.32.cloned.1.call-done = bf16[2,512,768]{2,1,0:T(8,128)(2,1)} async-done(((bf16[2,128,768]{2,1,0:T(8,128)(2,1)}), bf16[2,512,768]{2,1,0:T(8,128)(2,1)}) %all-gather.32.cloned.1.call-update) | async-done | bytes 1572880 | tf_op jit(solution)/shard_map/all_gather | solution.py:118
  1204.0 36.5 %reduce-scatter.53.cloned.1.call-done = f32[96,512]{1,0:T(8,128)} async-done(((f32[768,512]{1,0:T(8,128)}), f32[96,512]{1,0:T(8,128)}) %reduce-scatter.53.cloned.1.call-update) | async-done | bytes 196624 | tf_op jit(solution)/shard_map/reduce_scatter | solution.py:388
  1240.5 42.4 %reduce-scatter.55.cloned.1.call-done = f32[96,512]{1,0:T(8,128)} async-done(((f32[768,512]{1,0:T(8,128)}), f32[96,512]{1,0:T(8,128)}) %reduce-scatter.55.cloned.1.call-update) | async-done | bytes 196624 | tf_op jit(solution)/shard_map/reduce_scatter | solution.py:389
  1282.8 38.6 %reduce-scatter.49.cloned.1.call-done = f32[96,192]{1,0:T(8,128)} async-done(((f32[768,192]{1,0:T(8,128)}), f32[96,192]{1,0:T(8,128)}) %reduce-scatter.49.cloned.1.call-update) | async-done | bytes 73744 | tf_op jit(solution)/shard_map/reduce_scatter | solution.py:384
  1321.4 38.6 %reduce-scatter.51.cloned.1.call-done = f32[96,192]{1,0:T(8,128)} async-done(((f32[768,192]{1,0:T(8,128)}), f32[96,192]{1,0:T(8,128)}) %reduce-scatter.51.cloned.1.call-update) | async-done | bytes 73744 | tf_op jit(solution)/shard_map/reduce_scatter | solution.py:387
  1360.0 38.6 %reduce-scatter.61.cloned.1.call-done = f32[96,192]{1,0:T(8,128)} async-done(((f32[768,192]{1,0:T(8,128)}), f32[96,192]{1,0:T(8,128)}) %reduce-scatter.61.cloned.1.call-update) | async-done | bytes 73744
  1398.6 38.6 %reduce-scatter.63.cloned.1.call-done = f32[96,192]{1,0:T(8,128)} async-done(((f32[768,192]{1,0:T(8,128)}), f32[96,192]{1,0:T(8,128)}) %reduce-scatter.63.cloned.1.call-update) | async-done | bytes 73744
  1437.2 38.6 %reduce-scatter.47.cloned.1.call-done = f32[96,192]{1,0:T(8,128)} async-done(((f32[768,192]{1,0:T(8,128)}), f32[96,192]{1,0:T(8,128)}) %reduce-scatter.47.cloned.1.call-update) | async-done | bytes 73744 | tf_op jit(solution)/shard_map/reduce_scatter | solution.py:383
  1475.8 38.7 %reduce-scatter.41.cloned.1.call-done = f32[96,192]{1,0:T(8,128)} async-done(((f32[768,192]{1,0:T(8,128)}), f32[96,192]{1,0:T(8,128)}) %reduce-scatter.41.cloned.1.call-update) | async-done | bytes 73744 | tf_op jit(solution)/shard_map/reduce_scatter | solution.py:380
  1514.6 38.6 %reduce-scatter.43.cloned.1.call-done = f32[96,192]{1,0:T(8,128)} async-done(((f32[768,192]{1,0:T(8,128)}), f32[96,192]{1,0:T(8,128)}) %reduce-scatter.43.cloned.1.call-update) | async-done | bytes 73744 | tf_op jit(solution)/shard_map/reduce_scatter | solution.py:381
  1553.2 38.8 %reduce-scatter.45.cloned.1.call-done = f32[96,192]{1,0:T(8,128)} async-done(((f32[768,192]{1,0:T(8,128)}), f32[96,192]{1,0:T(8,128)}) %reduce-scatter.45.cloned.1.call-update) | async-done | bytes 73744 | tf_op jit(solution)/shard_map/reduce_scatter | solution.py:382
  1591.9 113.7 %reduce-scatter.39.cloned.1.call-done = f32[2,256,768]{2,1,0:T(8,128)} async-done(((f32[2,1024,768]{2,1,0:T(8,128)}), f32[2,256,768]{2,1,0:T(8,128)}) %reduce-scatter.39.cloned.1.call-update) | async-done | bytes 1572880 | tf_op jit(solution)/shard_map/reduce_scatter | solution.py:323
  1705.6 159.7 %reduce-scatter.59.cloned.1.call-done = f32[96,8032]{1,0:T(8,128)} async-done(((f32[768,8032]{1,0:T(8,128)}), f32[96,8032]{1,0:T(8,128)}) %reduce-scatter.59.cloned.1.call-update) | async-done | bytes 3084304 | tf_op jit(solution)/shard_map/reduce_scatter | solution.py:391
  (513 shorter events, 741.8 us)
Async XLA Ops:
  33.6 112.7 %reduce-scatter.25.cloned.1.call-start = ((), (), s32[]{:S(2)}) async-start(), calls=%async_computation.21 | async-start | bytes 3932160 | tf_op jit(solution)/shard_map/reduce_scatter | solution.py:114
  85.9 125.5 %all-gather.18.cloned.1.call-start = ((), (), s32[]{:S(2)}) async-start(), calls=%async_computation.22 | async-start | bytes 3932160 | tf_op jit(solution)/shard_map/all_gather | solution.py:216
  86.6 162.6 %all-gather.20.cloned.1.call-start = ((), (), s32[]{:S(2)}) async-start(), calls=%async_computation.23 | async-start | bytes 1966080 | tf_op jit(solution)/shard_map/all_gather | solution.py:110
  149.2 176.3 %reduce-scatter.27.cloned.1.call-start = ((), (), s32[]{:S(2)}) async-start(), calls=%async_computation.24 | async-start | bytes 3932160 | tf_op jit(solution)/shard_map/reduce_scatter | solution.py:114
  328.4 105.3 %reduce-scatter.29.cloned.1.call-start = ((), (), s32[]{:S(2)}) async-start(), calls=%async_computation.26 | async-start | bytes 3932160 | tf_op jit(solution)/shard_map/reduce_scatter | solution.py:114
  375.0 110.8 %all-gather.24.cloned.1.call-start = ((), (), s32[]{:S(2)}) async-start(), calls=%async_computation.27 | async-start | bytes 1966080 | tf_op jit(solution)/shard_map/all_gather | solution.py:110
  437.1 360.3 %reduce-scatter.31.cloned.1.call-start = ((), (), s32[]{:S(2)}) async-start(), calls=%async_computation.29 | async-start | bytes 3932160 | tf_op jit(solution)/shard_map/reduce_scatter | solution.py:122
  801.4 105.5 %reduce-scatter.33.cloned.1.call-start = ((), (), s32[]{:S(2)}) async-start(), calls=%async_computation.31 | async-start | bytes 3932160 | tf_op jit(solution)/shard_map/reduce_scatter | solution.py:122
  847.7 101.4 %all-gather.30.cloned.1.call-start = ((), (), s32[]{:S(2)}) async-start(), calls=%async_computation.32 | async-start | bytes 1966080 | tf_op jit(solution)/shard_map/all_gather | solution.py:118
  912.0 124.2 %reduce-scatter.35.cloned.1.call-start = ((), (), s32[]{:S(2)}) async-start(), calls=%async_computation.33 | async-start | bytes 3932160 | tf_op jit(solution)/shard_map/reduce_scatter | solution.py:122
  1040.7 125.1 %reduce-scatter.37.cloned.1.call-start = ((), (), s32[]{:S(2)}) async-start(), calls=%async_computation.35 | async-start | bytes 3932160 | tf_op jit(solution)/shard_map/reduce_scatter | solution.py:122
  1096.4 107.6 %reduce-scatter.57.cloned.1.call-start = ((), (), s32[]{:S(2)}) async-start(), calls=%async_computation.45 | async-start | bytes 1769472 | tf_op jit(solution)/shard_map/reduce_scatter | solution.py:390
  1101.3 139.2 %reduce-scatter.53.cloned.1.call-start = ((), (), s32[]{:S(2)}) async-start(), calls=%async_computation.43 | async-start | bytes 1769472 | tf_op jit(solution)/shard_map/reduce_scatter | solution.py:388
  1105.2 177.6 %reduce-scatter.55.cloned.1.call-start = ((), (), s32[]{:S(2)}) async-start(), calls=%async_computation.44 | async-start | bytes 1769472 | tf_op jit(solution)/shard_map/reduce_scatter | solution.py:389
  1108.9 212.6 %reduce-scatter.49.cloned.1.call-start = ((), (), s32[]{:S(2)}) async-start(), calls=%async_computation.41 | async-start | bytes 884736 | tf_op jit(solution)/shard_map/reduce_scatter | solution.py:384
  1112.1 248.0 %reduce-scatter.51.cloned.1.call-start = ((), (), s32[]{:S(2)}) async-start(), calls=%async_computation.42 | async-start | bytes 884736 | tf_op jit(solution)/shard_map/reduce_scatter | solution.py:387
  1115.1 283.5 %reduce-scatter.61.cloned.1.call-start = ((), (), s32[]{:S(2)}) async-start(), calls=%async_computation.47 | async-start | bytes 884736
  1120.2 317.1 %reduce-scatter.63.cloned.1.call-start = ((), (), s32[]{:S(2)}) async-start(), calls=%async_computation.48 | async-start | bytes 884736
  1125.4 350.4 %reduce-scatter.47.cloned.1.call-start = ((), (), s32[]{:S(2)}) async-start(), calls=%async_computation.40 | async-start | bytes 884736 | tf_op jit(solution)/shard_map/reduce_scatter | solution.py:383
  1128.5 386.1 %reduce-scatter.41.cloned.1.call-start = ((), (), s32[]{:S(2)}) async-start(), calls=%async_computation.37 | async-start | bytes 884736 | tf_op jit(solution)/shard_map/reduce_scatter | solution.py:380
  1130.3 422.8 %reduce-scatter.43.cloned.1.call-start = ((), (), s32[]{:S(2)}) async-start(), calls=%async_computation.38 | async-start | bytes 884736 | tf_op jit(solution)/shard_map/reduce_scatter | solution.py:381
  1131.9 460.0 %reduce-scatter.45.cloned.1.call-start = ((), (), s32[]{:S(2)}) async-start(), calls=%async_computation.39 | async-start | bytes 884736 | tf_op jit(solution)/shard_map/reduce_scatter | solution.py:382
  1133.5 572.0 %reduce-scatter.39.cloned.1.call-start = ((), (), s32[]{:S(2)}) async-start(), calls=%async_computation.36 | async-start | bytes 7864320 | tf_op jit(solution)/shard_map/reduce_scatter | solution.py:323
  1139.6 725.6 %reduce-scatter.59.cloned.1.call-start = ((), (), s32[]{:S(2)}) async-start(), calls=%async_computation.46 | async-start | bytes 27869184 | tf_op jit(solution)/shard_map/reduce_scatter | solution.py:391
  (120 other events, 3834.5 us)
Sparse Core Ops, SparseCore 0:
  33.7 36.4 all-gather.15
  86.0 60.3 reduce-scatter.24
  147.9 63.4 all-gather.17
  213.4 35.7 all-gather.19
  266.4 59.1 reduce-scatter.26
  328.5 37.0 all-gather.21
  374.5 59.0 reduce-scatter.28
  847.8 59.0 reduce-scatter.32
  1040.8 36.9 all-gather.31
  1096.6 59.1 reduce-scatter.36
  1159.6 38.6 reduce-scatter.56
  1202.0 38.4 reduce-scatter.52
  1244.3 38.4 reduce-scatter.54
  1286.4 34.9 reduce-scatter.48
  1325.0 34.9 reduce-scatter.50
  1363.6 34.9 reduce-scatter.60
  1402.2 34.9 reduce-scatter.62
  1440.8 34.9 reduce-scatter.46
  1479.5 34.9 reduce-scatter.40
  1518.1 34.9 reduce-scatter.42
  1556.9 34.9 reduce-scatter.44
  1594.8 110.7 reduce-scatter.38
  1709.9 155.3 reduce-scatter.58
Sparse Core Ops, SparseCore 1:
  376.8 69.9 all-gather.25
  448.8 36.9 all-gather.23
  738.2 59.1 reduce-scatter.30
  801.5 36.8 all-gather.27
  912.1 36.9 all-gather.29
  977.1 59.1 reduce-scatter.34
where the time goes:
time: 1880 us; the launch traced here: 1870 us
  waiting for transfers between devices  1240 us (66%)
  matrix products  229 us (12%)
  blocking collectives  194 us (10%)
  local copies, waits for them, and re-layouts  107 us (6%)
  other arithmetic  80.4 us (4%)
    reduce_scatter x4, waiting for transfers between devices, collect_grads(): return lax.psum_scatter(terms, 'mp', scatter_dimension=1, tiled=True)  177 us
    reduce_scatter x3, waiting for transfers between devices, collect_rows(): return lax.psum_scatter(terms, 'mp', scatter_dimension=1, tiled=True)  177 us
    reduce_scatter x1, waiting for transfers between devices, local(): lax.psum_scatter(embed_sum, 'batch', scatter_dimension=0, tiled=True)  160 us
    reduce_scatter x1, waiting for transfers between devices, local(): lax.psum_scatter(memory_terms, 'mp', scatter_dimension=1, tiled=True)  114 us
    all_gather x3, waiting for transfers between devices, spread_grads(): lax.all_gather(d_residual.astype(jnp.bfloat16), 'mp', axis=1, tiled=True)  111 us
    all_gather x4, waiting for transfers between devices, spread_rows(): return lax.all_gather(normed.astype(jnp.bfloat16), 'mp', axis=1, tiled=True)  79.6 us
    unnamed x31, waiting for transfers between devices  78.8 us
    dynamic_slice x6, local copies, waits for them, and re-layouts, local(): lax.scan(head_back, jnp.zeros(embed_table.shape, jnp.float32), (logits, r...  57.3 us
  transfers between devices with their start and end apart: 29, of which 27 were waited for; matrix products, arithmetic and copies ran while one was open for 4% of the time, Pallas kernels for 0%

commit v1 on v0

v1 whole, which is shorter than its diff:
```python
import functools

import jax
import jax.numpy as jnp
from jax import lax
from jax.experimental import pallas as pl
from jax.experimental.pallas import tpu as pltpu
from jax.sharding import PartitionSpec as P

DH = 64
LANES = 128
EPSILON = 1e-06
MASKED_OUT = -1000000000.0
GELU_SCALE = 0.7978845608028654
VMEM_LIMIT = 56 * 1024 * 1024
VOCAB_BLOCK = 1024
BF16 = jnp.bfloat16
F32 = jnp.float32


def params():
    return pltpu.CompilerParams(
        dimension_semantics=("arbitrary",), vmem_limit_bytes=VMEM_LIMIT
    )


def mm(a, b):
    return lax.dot_general(a, b, (((1,), (0,)), ((), ())), preferred_element_type=F32)


def mm_nt(a, b):
    return lax.dot_general(a, b, (((1,), (1,)), ((), ())), preferred_element_type=F32)


def mm_tn(a, b):
    return lax.dot_general(a, b, (((0,), (0,)), ((), ())), preferred_element_type=F32)


def block_positions(scal_ref, count, size, dim):
    shape = (size, 1) if dim == 0 else (1, size)
    pieces = [
        lax.broadcasted_iota(jnp.int32, shape, dim) + scal_ref[i] * size for i in range(count)
    ]
    return jnp.concatenate(pieces, axis=dim)


def allowed_mask(scal_ref, rows, keys, causal):
    key_pos = block_positions(scal_ref, 4, keys // 4, 1)
    allowed = jnp.broadcast_to(key_pos < scal_ref[4], (rows, keys))
    if causal:
        row_pos = block_positions(scal_ref, 4, rows // 4, 0)
        allowed = allowed & (key_pos <= row_pos)
    return allowed


def head_lanes(rows, head):
    lane = lax.broadcasted_iota(jnp.int32, (rows, LANES), 1)
    return (lane < DH) if head == 0 else (lane >= DH)


def attend_kernel(causal, scal_ref, q_ref, k_ref, v_ref, out_ref, lse_ref):
    rows, keys = q_ref.shape[0], k_ref.shape[0]
    allowed = allowed_mask(scal_ref, rows, keys, causal)
    q, k, v = q_ref[...], k_ref[...], v_ref[...]
    outs, lses = [], []
    for head in range(2):
        q_head = jnp.where(head_lanes(rows, head), q, jnp.zeros_like(q))
        scores = jnp.where(allowed, mm_nt(q_head, k), MASKED_OUT)
        highest = jnp.max(scores, -1, keepdims=True)
        raised = jnp.exp(scores - highest)
        totals = jnp.sum(raised, -1, keepdims=True)
        weights = (raised * (1.0 / totals)).astype(BF16)
        outs.append(mm(weights, v))
        lses.append(highest + jnp.log(totals))
    first = head_lanes(rows, 0)
    out_ref[...] = jnp.where(first, outs[0], outs[1]).astype(out_ref.dtype)
    lse_ref[...] = jnp.where(first, lses[0], lses[1])


def attend(scal, q, k, v, causal):
    rows, width = q.shape
    keys = k.shape[0]
    cost = pl.CostEstimate(
        flops=8 * rows * keys * width,
        transcendentals=rows * keys * width // DH,
        bytes_accessed=2 * (2 * rows + 2 * keys) * width + 4 * rows * width,
    )
    row_spec = pl.BlockSpec((rows, LANES), lambda j, s: (0, j))
    key_spec = pl.BlockSpec((keys, LANES), lambda j, s: (0, j))
    return pl.pallas_call(
        functools.partial(attend_kernel, causal),
        out_shape=(
            jax.ShapeDtypeStruct((rows, width), BF16),
            jax.ShapeDtypeStruct((rows, width), F32),
        ),
        grid_spec=pltpu.PrefetchScalarGridSpec(
            num_scalar_prefetch=1,
            grid=(width // LANES,),
            in_specs=[row_spec, key_spec, key_spec],
            out_specs=(row_spec, row_spec),
        ),
        compiler_params=params(),
        cost_estimate=cost,
        name="attend",
    )(scal, q, k, v)


def attend_back_kernel(
    causal, scal_ref, q_ref, k_ref, v_ref, lse_ref, d_ref, dq_ref, dk_ref, dv_ref
):
    rows, keys = q_ref.shape[0], k_ref.shape[0]
    allowed = allowed_mask(scal_ref, rows, keys, causal)
    q, k, v, d_out = q_ref[...], k_ref[...], v_ref[...], d_ref[...]
    dqs, dks, dvs = [], [], []
    for head in range(2):
        mine = head_lanes(rows, head)
        q_head = jnp.where(mine, q, jnp.zeros_like(q))
        d_head = jnp.where(mine, d_out, jnp.zeros_like(d_out))
        scores = jnp.where(allowed, mm_nt(q_head, k), MASKED_OUT)
        weights = jnp.exp(scores - lse_ref[:, head * DH : head * DH + 1])
        d_weights = mm_nt(d_head, v)
        inner = jnp.sum(weights * d_weights, -1, keepdims=True)
        d_scores = (weights * (d_weights - inner)).astype(BF16)
        dqs.append(mm(d_scores, k))
        dks.append(mm_tn(d_scores, q))
        dvs.append(mm_tn(weights.astype(BF16), d_out))
    dq_ref[...] = jnp.where(head_lanes(rows, 0), dqs[0], dqs[1]).astype(BF16)
    first = head_lanes(keys, 0)
    dk_ref[...] = jnp.where(first, dks[0], dks[1]).astype(BF16)
    dv_ref[...] = jnp.where(first, dvs[0], dvs[1]).astype(BF16)


def attend_back(scal, q, k, v, lse, d_out, causal):
    rows, width = q.shape
    keys = k.shape[0]
    cost = pl.CostEstimate(
        flops=20 * rows * keys * width,
        transcendentals=rows * keys * width // DH,
        bytes_accessed=2 * (3 * rows + 4 * keys) * width + 4 * rows * width,
    )
    row_spec = pl.BlockSpec((rows, LANES), lambda j, s: (0, j))
    key_spec = pl.BlockSpec((keys, LANES), lambda j, s: (0, j))
    return pl.pallas_call(
        functools.partial(attend_back_kernel, causal),
        out_shape=(
            jax.ShapeDtypeStruct((rows, width), BF16),
            jax.ShapeDtypeStruct((keys, width), BF16),
            jax.ShapeDtypeStruct((keys, width), BF16),
        ),
        grid_spec=pltpu.PrefetchScalarGridSpec(
            num_scalar_prefetch=1,
            grid=(width // LANES,),
            in_specs=[row_spec, key_spec, key_spec, row_spec, row_spec],
            out_specs=(row_spec, key_spec, key_spec),
        ),
        compiler_params=params(),
        cost_estimate=cost,
        name="attend_back",
    )(scal, q, k, v, lse, d_out)


STAT = 64
WEIGHT_LANE = 64
ID_LANE = 65
TURNED = 8


def head_kernel(vocab, scale, rows_ref, table_ref, ids_ref, prob_ref, stat_ref, turned_ref):
    step = pl.program_id(0)
    block = table_ref.shape[1]
    table = table_ref[...]
    chunk = 256
    first = step == 0
    for start in range(0, rows_ref.shape[0], chunk):
        part = pl.ds(start, chunk)
        column = lax.broadcasted_iota(jnp.int32, (chunk, block), 1) + step * block
        logits = mm(rows_ref[part, :], table) * scale
        logits = jnp.where(column < vocab, logits, MASKED_OUT)
        highest = jnp.max(logits, -1, keepdims=True)
        raised = jnp.exp(logits - highest)
        totals = jnp.sum(raised, -1, keepdims=True)
        prob_ref[part, :] = raised.astype(BF16)
        picked = jnp.sum(jnp.where(column == ids_ref[part, :], logits, 0.0), -1, keepdims=True)
        stats = jnp.where(first, 0.0, stat_ref[part, :])
        old_high = jnp.where(first, MASKED_OUT, stats[:, STAT : STAT + 1])
        old_total = stats[:, STAT + 1 : STAT + 2]
        old_picked = stats[:, STAT + 2 : STAT + 3]
        new_high = jnp.maximum(old_high, highest)
        new_total = old_total * jnp.exp(old_high - new_high) + totals * jnp.exp(highest - new_high)
        lane = lax.broadcasted_iota(jnp.int32, (chunk, LANES), 1)
        stats = jnp.where(lane == step, highest, stats)
        stats = jnp.where(lane == STAT, new_high, stats)
        stats = jnp.where(lane == STAT + 1, new_total, stats)
        stat_ref[part, :] = jnp.where(lane == STAT + 2, old_picked + picked, stats)

    @pl.when(step == pl.num_programs(0) - 1)
    def _():
        turned_ref[...] = stat_ref[...].T[STAT : STAT + TURNED]


def head_forward(rows, table, ids, scale):
    count, width = rows.shape
    vocab = table.shape[1]
    steps = pl.cdiv(vocab, VOCAB_BLOCK)
    return pl.pallas_call(
        functools.partial(head_kernel, vocab, scale),
        out_shape=(
            jax.ShapeDtypeStruct((count, vocab), BF16),
            jax.ShapeDtypeStruct((count, LANES), F32),
            jax.ShapeDtypeStruct((TURNED, count), F32),
        ),
        grid=(steps,),
        in_specs=[
            pl.BlockSpec((count, width), lambda j: (0, 0)),
            pl.BlockSpec((width, VOCAB_BLOCK), lambda j: (0, j)),
            pl.BlockSpec((count, 1), lambda j: (0, 0)),
        ],
        out_specs=(
            pl.BlockSpec((count, VOCAB_BLOCK), lambda j: (0, j)),
            pl.BlockSpec((count, LANES), lambda j: (0, 0)),
            pl.BlockSpec((TURNED, count), lambda j: (0, 0)),
        ),
        compiler_params=params(),
        cost_estimate=pl.CostEstimate(
            flops=2 * count * width * vocab,
            transcendentals=count * vocab,
            bytes_accessed=2 * (count + width) * vocab + 2 * count * width,
        ),
        name="head_forward",
    )(rows, table, ids)


def combine_kernel(stat_ref, share_refs, info_ref, coef_ref, loss_ref):
    count = stat_ref.shape[0]
    shares = [ref[...] for ref in share_refs]
    highest = functools.reduce(jnp.maximum, [share[0:1] for share in shares])
    totals = sum(share[1:2] * jnp.exp(share[0:1] - highest) for share in shares)
    picked = sum(share[2:3] for share in shares)
    log_totals = highest + jnp.log(totals)
    info = info_ref[...]
    loss_ref[...] = jnp.broadcast_to((log_totals - picked) * info[1:2], (TURNED, count))
    row = lax.broadcasted_iota(jnp.int32, (LANES, count), 0)
    wide = jnp.where(row == 0, log_totals, jnp.where(row == 1, info[0:1], info[2:3]))
    turned = wide.T
    weight = turned[:, 1:2]
    lane = lax.broadcasted_iota(jnp.int32, (count, LANES), 1)
    coef = weight * jnp.exp(jnp.minimum(stat_ref[...] - turned[:, 0:1], 0.0))
    coef = jnp.where(lane == WEIGHT_LANE, weight, coef)
    coef_ref[...] = jnp.where(lane == ID_LANE, turned[:, 2:3], coef)


def combine(stats, shares, info):
    count = stats.shape[0]

    def kernel(stat_ref, *refs):
        combine_kernel(stat_ref, refs[: len(shares)], *refs[len(shares) :])

    return pl.pallas_call(
        kernel,
        out_shape=(
            jax.ShapeDtypeStruct((count, LANES), F32),
            jax.ShapeDtypeStruct((TURNED, count), F32),
        ),
        compiler_params=pltpu.CompilerParams(vmem_limit_bytes=VMEM_LIMIT),
        cost_estimate=pl.CostEstimate(
            flops=10 * count * LANES, transcendentals=count * LANES, bytes_accessed=8 * count * LANES
        ),
        name="combine",
    )(stats, *shares, info)


def logit_grads(vocab, step, prob_ref, coef_ref):
    prob = prob_ref[...].astype(F32)
    coef = coef_ref[...]
    lane = lax.broadcasted_iota(jnp.int32, coef.shape, 1)
    factor = jnp.sum(jnp.where(lane == step, coef, 0.0), -1, keepdims=True)
    weight = coef[:, WEIGHT_LANE : WEIGHT_LANE + 1]
    ids = coef[:, ID_LANE : ID_LANE + 1].astype(jnp.int32)
    column = lax.broadcasted_iota(jnp.int32, prob.shape, 1) + step * prob.shape[1]
    grads = prob * factor - jnp.where(column == ids, weight, 0.0)
    return jnp.where(column < vocab, grads, 0.0).astype(BF16)


def table_grad_kernel(vocab, parts, *refs):
    step = pl.program_id(0)
    total = 0.0
    for i in range(parts):
        turned_ref, prob_ref, coef_ref = refs[3 * i : 3 * i + 3]
        total = total + mm(turned_ref[...], logit_grads(vocab, step, prob_ref, coef_ref))
    refs[-1][...] = total.astype(refs[-1].dtype)


def table_grad(parts):
    width = parts[0][0].shape[0]
    vocab = parts[0][1].shape[1]
    steps = pl.cdiv(vocab, VOCAB_BLOCK)
    count = sum(part[0].shape[1] for part in parts)
    specs, operands = [], []
    for turned, prob, coef in parts:
        rows = turned.shape[1]
        specs += [
            pl.BlockSpec((width, rows), lambda j: (0, 0)),
            pl.BlockSpec((rows, VOCAB_BLOCK), lambda j: (0, j)),
            pl.BlockSpec((rows, LANES), lambda j: (0, 0)),
        ]
        operands += [turned, prob, coef]
    return pl.pallas_call(
        functools.partial(table_grad_kernel, vocab, len(parts)),
        out_shape=jax.ShapeDtypeStruct((width, vocab), BF16),
        grid=(steps,),
        in_specs=specs,
        out_specs=pl.BlockSpec((width, VOCAB_BLOCK), lambda j: (0, j)),
        compiler_params=params(),
        cost_estimate=pl.CostEstimate(
            flops=2 * count * width * vocab,
            transcendentals=0,
            bytes_accessed=2 * (count + width) * vocab + 2 * count * width,
        ),
        name="table_grad",
    )(*operands)


def row_grad_kernel(vocab, table_ref, prob_ref, coef_ref, out_ref):
    step = pl.program_id(0)
    grads = logit_grads(vocab, step, prob_ref, coef_ref)
    table = table_ref[...]
    column = lax.broadcasted_iota(jnp.int32, table.shape, 1) + step * table.shape[1]
    table = jnp.where(column < vocab, table, jnp.zeros_like(table))
    terms = mm_nt(grads, table)

    @pl.when(step == 0)
    def _():
        out_ref[...] = terms

    @pl.when(step > 0)
    def _():
        out_ref[...] += terms


def row_grad(table, prob, coef):
    width = table.shape[0]
    count, vocab = prob.shape
    steps = pl.cdiv(vocab, VOCAB_BLOCK)
    return pl.pallas_call(
        functools.partial(row_grad_kernel, vocab),
        out_shape=jax.ShapeDtypeStruct((count, width), F32),
        grid=(steps,),
        in_specs=[
            pl.BlockSpec((width, VOCAB_BLOCK), lambda j: (0, j)),
            pl.BlockSpec((count, VOCAB_BLOCK), lambda j: (0, j)),
            pl.BlockSpec((count, LANES), lambda j: (0, 0)),
        ],
        out_specs=pl.BlockSpec((count, width), lambda j: (0, 0)),
        compiler_params=params(),
        cost_estimate=pl.CostEstimate(
            flops=2 * count * width * vocab,
            transcendentals=0,
            bytes_accessed=2 * (count + width) * vocab + 4 * count * width,
        ),
        name="row_grad",
    )(table, prob, coef)


def gelu_tanh(values):
    return (
        0.5 * values * (1.0 + jnp.tanh(GELU_SCALE * (values + 0.044715 * values * values * values)))
    )


def gated_unit(gate_in, up_in):
    return gelu_tanh(gate_in) * up_in


def norm_rows(values, gain_vec):
    inverse = lax.rsqrt(jnp.mean(values * values, -1, keepdims=True) + EPSILON)
    return (values * inverse * gain_vec, inverse)


def norm_back(values, inverse, gain_vec, upstream):
    scaled = upstream * gain_vec
    inner_sum = jnp.mean(scaled * values, -1, keepdims=True)
    d_values = inverse * scaled - values * (inverse * inverse * inverse) * inner_sum
    d_gain = jnp.sum(upstream * values * inverse, axis=0)
    return (d_values, d_gain)


def swap(values, step):
    return lax.ppermute(values, "mp", [(i, i ^ step) for i in range(4)])


def gather_batch(values, axis):
    return lax.all_gather(values, "batch", axis=axis, tiled=True)


def scatter_batch(values, axis):
    return lax.psum_scatter(values, "batch", scatter_dimension=axis, tiled=True)


def after(values, earlier):
    return lax.optimization_barrier((values, earlier))[0]


def both_slices(weights):
    return jnp.concatenate([weights, swap(weights, 2)], axis=-1)


def own_slice(grads):
    cut = grads.shape[-1] // 2
    return grads[..., :cut].astype(F32) + swap(grads[..., cut:], 2).astype(F32)


def local(
    hidden_in,
    memory,
    tgt_len,
    src_len,
    target_ids,
    task_ids,
    task_weight,
    gain_self,
    q_self,
    k_self,
    v_self,
    o_self,
    gain_cross,
    q_cross,
    k_cross,
    v_cross,
    o_cross,
    gain_mlp,
    mlp_gate,
    mlp_up,
    mlp_down,
    gain_exit,
    embed_table,
):
    place = lax.axis_index("mp")
    pair = place // 2
    lower = pair == 0
    others = [place, place ^ 2, place ^ 1, place ^ 3]
    block = hidden_in.shape[1]
    own_rows = 2 * block
    width = hidden_in.shape[2]
    vocab = embed_table.shape[1]

    def of_pair(values):
        return jnp.where(lower, values[0], values[1])

    def of_other(values):
        return jnp.where(lower, values[1], values[0])

    def pair_rows(values):
        mine, other = of_pair(values), of_other(values)
        return [mine, swap(other, 2), swap(mine, 1), swap(other, 3)]

    def placed(own, far):
        far = swap(far.astype(BF16), 2).astype(own.dtype)
        return jnp.stack([jnp.where(lower, own, far), jnp.where(lower, far, own)])

    self_part = both_slices(jnp.stack([q_self, k_self, v_self, o_self]))
    w_self = gather_batch(self_part, 1)
    cross_part = both_slices(jnp.stack([q_cross, k_cross, v_cross, o_cross]))
    w_cross = gather_batch(after(cross_part, w_self), 1)
    mlp_part = both_slices(jnp.stack([mlp_gate, mlp_up, mlp_down]))
    gains = lax.all_gather(jnp.stack([gain_self, gain_cross, gain_mlp, gain_exit]), "batch", axis=1, tiled=True)
    gain_self, gain_cross, gain_mlp, gain_exit = (gains[i].astype(F32) for i in range(4))

    pair_tgt = jnp.where(lower, tgt_len[0], tgt_len[1])
    pair_src = jnp.where(lower, src_len[0], src_len[1])
    self_scal = jnp.stack(others + [pair_tgt]).astype(jnp.int32)
    cross_scal = jnp.stack(others + [pair_src]).astype(jnp.int32)

    pieces = pair_rows(hidden_in)
    all_in = jnp.concatenate(pieces, axis=0).astype(F32)
    residual = all_in[:own_rows]
    normed_one, inverse_one = norm_rows(all_in, gain_self)
    rows_one = normed_one.astype(BF16)
    q_one = mm(rows_one, w_self[0]).astype(BF16)
    k_one = mm(rows_one, w_self[1]).astype(BF16)
    v_one = mm(rows_one, w_self[2]).astype(BF16)
    mixed_one, lse_one = attend(self_scal, q_one, k_one, v_one, True)

    def gather_pair(own):
        return jnp.concatenate([own, swap(own, 1)], axis=0)

    def reduce_pair(terms):
        return terms[:own_rows] + swap(terms[own_rows:].astype(BF16), 1).astype(F32)

    w_mlp = gather_batch(after(mlp_part, (w_cross, mixed_one)), 1)
    residual_one = residual + reduce_pair(mm_nt(mixed_one, w_self[3]))

    memory_rows = jnp.concatenate(pair_rows(memory), axis=0)
    k_two = mm(memory_rows, w_cross[1]).astype(BF16)
    v_two = mm(memory_rows, w_cross[2]).astype(BF16)
    normed_two, inverse_two = norm_rows(residual_one, gain_cross)
    rows_two = gather_pair(normed_two.astype(BF16))
    q_two = mm(rows_two, w_cross[0]).astype(BF16)
    mixed_two, lse_two = attend(cross_scal, q_two, k_two, v_two, False)
    table = gather_batch(after(embed_table, (w_mlp, mixed_two)), 0)
    residual_two = residual_one + reduce_pair(mm_nt(mixed_two, w_cross[3]))

    normed_three, inverse_three = norm_rows(residual_two, gain_mlp)
    rows_three = gather_pair(normed_three.astype(BF16))
    gate = mm(rows_three, w_mlp[0])
    up_proj = mm(rows_three, w_mlp[1])
    hidden = gated_unit(gate, up_proj).astype(BF16)
    residual_three = residual_two + reduce_pair(mm_nt(hidden, w_mlp[2]))
    finished = residual_three.astype(BF16)
    block_out = placed(finished[:block], finished[block:])

    normed_four, inverse_four = norm_rows(residual_three, gain_exit)
    own_four = normed_four.astype(BF16)
    near_four = jnp.concatenate([own_four, swap(own_four, 1)], axis=0)
    far_four = jnp.concatenate([swap(own_four, 2), swap(own_four, 3)], axis=0)
    slot_blocks = [
        (of, other)
        for of, order in ((pair, others), (1 - pair, [others[i] for i in (1, 0, 3, 2)]))
        for other in order
    ]
    row_order = jnp.stack([of * 4 + other for of, other in slot_blocks])
    ids = target_ids.reshape(8, block)[row_order].reshape(8 * block)
    local_ids = ids - place * vocab
    local_ids = jnp.where((local_ids >= 0) & (local_ids < vocab), local_ids, -1)
    positions = (
        jnp.stack([other * block for _, other in slot_blocks])[:, None] + jnp.arange(block)[None, :]
    ).reshape(8 * block)
    slot_pair = jnp.repeat(jnp.stack([pair, 1 - pair]), 4 * block)
    lengths = jnp.where(slot_pair == 0, tgt_len[0], tgt_len[1])
    valid = (positions < lengths).astype(F32)
    tasks = task_weight.shape[0]
    task_scale = jnp.sum(
        jnp.where(task_ids[:, None] == jnp.arange(tasks)[None, :], task_weight[None, :], 0.0), -1
    )
    logit_scale = width ** (-0.5)
    row_scale = jnp.where(slot_pair == 0, task_scale[0], task_scale[1]) * valid * logit_scale

    info = jnp.stack([row_scale, valid, local_ids.astype(F32)])
    info = jnp.concatenate([info, jnp.zeros((TURNED - 3, info.shape[1]), F32)])
    half_rows = 2 * own_rows
    near_prob, near_stats, near_turned = head_forward(
        near_four, table, local_ids[:half_rows, None], logit_scale
    )
    far_prob, far_stats, far_turned = head_forward(
        far_four, table, local_ids[half_rows:, None], logit_scale
    )
    mine = jnp.concatenate([near_turned, far_turned], axis=1)
    shares = [mine]
    for step in (1, 2, 3):
        moved = swap(mine, step)
        shares.append(
            jnp.concatenate(
                [
                    moved[:, (slot ^ step) * own_rows : ((slot ^ step) + 1) * own_rows]
                    for slot in range(4)
                ],
                axis=1,
            )
        )
    coef, losses = combine(jnp.concatenate([near_stats, far_stats]), shares, info)
    half_sums = jnp.sum(losses[0].reshape(2, half_rows), -1)
    pair_sums = jnp.where(lower, half_sums, half_sums[::-1])
    pair_loss = pair_sums / tgt_len.astype(F32)

    near_coef, far_coef = coef[:half_rows], coef[half_rows:]
    far_rows_grad = row_grad(table, far_prob, far_coef)
    table_terms = table_grad(
        [(near_four.T, near_prob, after(near_coef, far_rows_grad)), (far_four.T, far_prob, far_coef)]
    )
    embed_sum = scatter_batch(table_terms, 0)
    near_rows_grad = row_grad(table, near_prob, after(near_coef, table_terms))
    d_four = near_rows_grad[:own_rows]
    for step, part in (
        (2, far_rows_grad[:own_rows]),
        (3, far_rows_grad[own_rows:]),
        (1, near_rows_grad[own_rows:]),
    ):
        d_four = d_four + swap(part.astype(BF16), step).astype(F32)
    d_residual, exit_grad = norm_back(residual_three, inverse_four, gain_exit, d_four)

    d_branch = gather_pair(d_residual.astype(BF16))
    d_hidden = mm(d_branch, w_mlp[2])
    _, pullback = jax.vjp(gated_unit, gate, up_proj)
    d_gate, d_up = pullback(d_hidden)
    d_gate = d_gate.astype(BF16)
    d_up = d_up.astype(BF16)
    d_rows = reduce_pair(mm_nt(d_gate, w_mlp[0]) + mm_nt(d_up, w_mlp[1]))
    late_three, late_branch = after((rows_three, d_branch), embed_sum)
    mlp_grads = [mm_tn(late_three, d_gate), mm_tn(late_three, d_up), mm_tn(late_branch, hidden)]
    mlp_scattered = scatter_batch(jnp.stack(mlp_grads).astype(BF16), 1)
    mlp_sum = own_slice(mlp_scattered)
    d_input, mlp_grad = norm_back(residual_two, inverse_three, gain_mlp, d_rows)
    d_residual = d_residual + d_input

    d_branch = gather_pair(d_residual.astype(BF16))
    d_mixed = mm(d_branch, w_cross[3]).astype(BF16)
    out_grad = mm_tn(d_branch, mixed_two)
    d_q, d_k, d_v = attend_back(cross_scal, q_two, k_two, v_two, lse_two, d_mixed, False)
    d_rows = reduce_pair(mm_nt(d_q, w_cross[0]))
    memory_terms = mm_nt(d_k, w_cross[1]) + mm_nt(d_v, w_cross[2])
    half = memory_terms.shape[0] // 2
    memory_own = memory_terms[:half] + swap(memory_terms[half:].astype(BF16), 1).astype(F32)
    memory_grad = placed(memory_own[: half // 2], memory_own[half // 2 :])
    cross_grads = [
        mm_tn(rows_two, d_q),
        mm_tn(memory_rows, d_k),
        mm_tn(memory_rows, d_v),
        out_grad,
    ]
    d_input, cross_grad = norm_back(residual_one, inverse_two, gain_cross, d_rows)
    d_residual = d_residual + d_input

    d_branch = gather_pair(d_residual.astype(BF16))
    d_mixed = mm(d_branch, w_self[3]).astype(BF16)
    out_grad = mm_tn(d_branch, mixed_one)
    d_q, d_k, d_v = attend_back(self_scal, q_one, k_one, v_one, lse_one, d_mixed, True)
    d_terms = mm_nt(d_q, w_self[0]) + mm_nt(d_k, w_self[1]) + mm_nt(d_v, w_self[2])
    d_rows = reduce_pair(d_terms)
    self_grad = jnp.sum(d_terms * (all_in * inverse_one), axis=0)
    d_input, _ = norm_back(residual, inverse_one[:own_rows], gain_self, d_rows)
    late_one = after(rows_one, mlp_scattered)
    self_grads = [mm_tn(late_one, d_q), mm_tn(late_one, d_k), mm_tn(late_one, d_v), out_grad]
    gain_grads = jnp.stack([self_grad, cross_grad, mlp_grad, exit_grad], axis=1)
    gain_slab = jnp.pad(gain_grads, ((0, 0), (0, d_q.shape[1] - 4)))
    last_sum = scatter_batch(jnp.stack(self_grads + cross_grads + [gain_slab]).astype(BF16), 1)
    last_split = own_slice(last_sum[:8])
    self_sum, cross_sum = last_split[:4], last_split[4:]
    gain_own = last_sum[8, :, :LANES]
    gain_sums = gain_own.astype(F32) + sum(swap(gain_own, step).astype(F32) for step in (1, 2, 3))
    d_residual = d_residual + d_input
    hidden_grad = placed(d_residual[:block], d_residual[block:])

    return (
        block_out,
        pair_loss,
        hidden_grad,
        memory_grad,
        gain_sums[:, 0],
        self_sum[0],
        self_sum[1],
        self_sum[2],
        self_sum[3],
        gain_sums[:, 1],
        cross_sum[0],
        cross_sum[1],
        cross_sum[2],
        cross_sum[3],
        gain_sums[:, 2],
        mlp_sum[0],
        mlp_sum[1],
        mlp_sum[2],
        gain_sums[:, 3],
        embed_sum.astype(F32),
    )


def solution(mesh):
    assert mesh.shape["mp"] == 4
    rows = P("batch", "mp", None)
    vector = P("batch")
    matrix = P("batch", "mp")
    sub = (vector, matrix, matrix, matrix, matrix)
    mlp = (vector, matrix, matrix, matrix)
    weights = sub + sub + mlp + (vector, matrix)
    in_specs = (rows, rows, vector, vector, P("batch", None), vector, P()) + weights
    out_specs = (rows, vector, rows, rows) + weights
    return jax.shard_map(local, mesh=mesh, in_specs=in_specs, out_specs=out_specs, check_vma=False)
```

time: 1880 us -> 646 us (0.34)
  waiting for transfers between devices: 1240 us -> 276 us
  blocking collectives: 194 us -> 8.86 us
  matrix products: 229 us -> 68 us
  Pallas kernels: 0 us -> 141 us
  local copies, waits for them, and re-layouts: 107 us -> 28.2 us
  starting transfers between devices: 2.06 us -> 51.3 us
  other arithmetic: 80.4 us -> 44.9 us
    reduce_scatter x18 -> x3, waiting for transfers between devices: 938 us -> 35.7 us  [scatter_batch(): return lax.psum_scatter(values, 'batch', scatter_dimension=axis, tiled=True)]
    ppermute x0 -> x38, waiting for transfers between devices: none -> 223 us  [swap(): return lax.ppermute(values, 'mp', [(i, i ^ step) for i in range(4)])]
    all_gather x9 -> x4, waiting for transfers between devices: 224 us -> 17.3 us  [gather_batch(): return lax.all_gather(values, 'batch', axis=axis, tiled=True)]
    dot_general x67 -> x33, matrix products: 229 us -> 68 us  [the longest x11 27.6 us: mm(): lax.dot_general(a, b, (((1,), (0,)), ((), ())), preferred_element_type=F32)]
    pallas_call x0 -> x10, Pallas kernels: none -> 141 us  [the longest x2 43.7 us: head_forward(): pl.pallas_call(functools.partial(head_kernel, vocab, scale), out_shape=(j...]
    all_gather x14 -> x1, blocking collectives: 144 us -> 8.86 us  [local(): lax.all_gather(jnp.stack([gain_self, gain_cross, gain_mlp, gain_exit]), '...]
    unnamed x31 -> x7, waiting for transfers between devices: 78.8 us -> 0.12 us
    dynamic_slice x18 -> x0, local copies, waits for them, and re-layouts: 63.3 us -> none  [the longest x6 57.3 us: local(): lax.scan(head_back, jnp.zeros(embed_table.shape, jnp.float32), (logits, r...]
  transfers between devices with their start and end apart: 29 -> 45, of which waited for: 27 -> 28; matrix products, arithmetic and copies ran while one was open for 4% -> 17% of each run, Pallas kernels for 0% -> 9%
where the time goes in v1:
time: 646 us; the launch traced here: 637 us
  waiting for transfers between devices  276 us (43%)
  Pallas kernels  141 us (22%)
  matrix products  68 us (11%)
  starting transfers between devices  51.3 us (8%)
  other arithmetic  44.9 us (7%)
  local copies, waits for them, and re-layouts  28.2 us (4%)
  between operations  18.1 us (3%)
  blocking collectives  8.86 us (1%)
    ppermute x38, waiting for transfers between devices, swap(): return lax.ppermute(values, 'mp', [(i, i ^ step) for i in range(4)])  223 us
    ppermute x38, starting transfers between devices, swap(): return lax.ppermute(values, 'mp', [(i, i ^ step) for i in range(4)])  50.7 us
    pallas_call x2, Pallas kernels, head_forward(): pl.pallas_call(functools.partial(head_kernel, vocab, scale), out_shape=(j...  43.7 us
    reduce_scatter x3, waiting for transfers between devices, scatter_batch(): return lax.psum_scatter(values, 'batch', scatter_dimension=axis, tiled=True)  35.7 us
    pallas_call x2, Pallas kernels, row_grad(): pl.pallas_call(functools.partial(row_grad_kernel, vocab), out_shape=jax.S...  33.5 us
    dot_general x11, matrix products, mm(): lax.dot_general(a, b, (((1,), (0,)), ((), ())), preferred_element_type=F32)  27.6 us
    pallas_call x2, Pallas kernels, attend_back(): pl.pallas_call(functools.partial(attend_back_kernel, causal), out_shape=(...  24.2 us
    dot_general x11, matrix products, mm_tn(): lax.dot_general(a, b, (((0,), (0,)), ((), ())), preferred_element_type=F32)  20.9 us
  transfers between devices with their start and end apart: 45, of which 28 were waited for; matrix products, arithmetic and copies ran while one was open for 17% of the time, Pallas kernels for 9%

profile of v1, /device:TPU:0, one launch (start us, length us, event | category | flops | bytes accessed | tf_op | source)
XLA Modules:
  0.0 636.8 jit_solution(7303014204451941112)
XLA Ops:
  12.4 9.1 %collective-permute-done.3 = bf16[4,96,192]{2,1,0:T(8,128)(2,1)S(1)} collective-permute-done((bf16[4,96,192]{2,1,0:T(8,128)(2,1)S(1)}, bf16[4,96,192]{2,1,0:T(8,128)(2,1)S(1)}, u32[]{:S(2)}, u32[]{:S(2)}) %collective-permute-start.3) | collective-permute-done | bytes 147488 | tf_op jit(solution)/shard_map/ppermute | solution.py:388
  24.4 11.2 %collective-permute-done.6 = bf16[4,96,192]{2,1,0:T(8,128)(2,1)S(1)} collective-permute-done((bf16[4,96,192]{2,1,0:T(8,128)(2,1)S(1)}, bf16[4,96,192]{2,1,0:T(8,128)(2,1)S(1)}, u32[]{:S(2)}, u32[]{:S(2)}) %collective-permute-start.6) | collective-permute-done | bytes 147488 | tf_op jit(solution)/shard_map/ppermute | solution.py:388
  36.4 17.3 %all-gather.6.cloned.1.call-done = bf16[4,768,384]{2,1,0:T(8,128)(2,1)} async-done(((bf16[4,96,384]{2,1,0:T(8,128)(2,1)}), bf16[4,768,384]{2,1,0:T(8,128)(2,1)}) %all-gather.6.cloned.1.call-update) | async-done | bytes 2359312 | tf_op jit(solution)/shard_map/all_gather | solution.py:392
  60.9 8.9 %all-gather = bf16[8,96,4]{1,2,0:T(4,128)(2,1)S(1)} all-gather(bf16[1,96,4]{1,2,0:T(4,128)(2,1)S(1)} %maximum_bitcast_fusion), channel_id=1, replica_groups=mesh['batch'=8,'mp'=4] {'batch'}, dimensions={0}, use_global_device_ids=true | all-gather | bytes 6912 | tf_op jit(solution)/shard_map/all_gather | solution.py:465
  72.4 9.1 %collective-permute-done = bf16[128,768]{1,0:T(8,128)(2,1)S(1)} collective-permute-done((bf16[128,768]{1,0:T(8,128)(2,1)S(1)}, bf16[128,768]{1,0:T(8,128)(2,1)S(1)}, u32[]{:S(2)}, u32[]{:S(2)}) %collective-permute-start) | collective-permute-done | bytes 196640 | tf_op jit(solution)/shard_map/ppermute | solution.py:388
  103.0 10.3 %collective-permute-done.4 = bf16[256,768]{1,0:T(8,128)(2,1)S(1)} collective-permute-done((bf16[256,768]{1,0:T(8,128)(2,1)S(1)}, bf16[256,768]{1,0:T(8,128)(2,1)S(1)}, u32[]{:S(2)}, u32[]{:S(2)}) %collective-permute-start.4) | collective-permute-done | bytes 393248 | tf_op jit(solution)/shard_map/ppermute | solution.py:388
  123.2 13.4 %collective-permute-done.5 = bf16[256,768]{1,0:T(8,128)(2,1)} collective-permute-done((bf16[256,768]{1,0:T(8,128)(2,1)}, bf16[256,768]{1,0:T(8,128)(2,1)}, u32[]{:S(2)}, u32[]{:S(2)}) %collective-permute-start.5) | collective-permute-done | bytes 393248 | tf_op jit(solution)/shard_map/ppermute | solution.py:388
  139.0 13.4 %collective-permute-done.7 = bf16[256,768]{1,0:T(8,128)(2,1)} collective-permute-done((bf16[256,768]{1,0:T(8,128)(2,1)}, bf16[256,768]{1,0:T(8,128)(2,1)}, u32[]{:S(2)}, u32[]{:S(2)}) %collective-permute-start.7) | collective-permute-done | bytes 393248 | tf_op jit(solution)/shard_map/ppermute | solution.py:388
  158.8 10.0 %attend.3 = (bf16[512,384]{1,0:T(8,128)(2,1)}, f32[512,384]{1,0:T(8,128)}) custom-call(s32[5]{0:T(128)} %stack.263.scal_ref, bf16[512,384]{1,0:T(8,128)(2,1)} %convolution_convert_fusion.15.q_ref, bf16[1024,384]{1,0:T(8,128)(2,1)} %convolution_convert_fusion.4.k_ref, bf16[1024,384]{1,0:T(8,128)(2,1)} %convolution_convert_fusion.3.v_ref), custom_call_target="tpu_custom_call" | custom-call | flops 1610612736 | bytes 3145728 | tf_op jit(solution)/shard_map/attend/pallas_call | solution.py:90
  216.6 24.0 %collective-permute-done.16 = bf16[256,768]{1,0:T(8,128)(2,1)} collective-permute-done((bf16[256,768]{1,0:T(8,128)(2,1)}, bf16[256,768]{1,0:T(8,128)(2,1)}, u32[]{:S(2)}, u32[]{:S(2)}) %collective-permute-start.16) | collective-permute-done | bytes 393248 | tf_op jit(solution)/shard_map/ppermute | solution.py:388
  247.2 22.0 %head_forward.2 = (bf16[512,8032]{1,0:T(8,128)(2,1)}, f32[512,128]{1,0:T(8,128)}, f32[8,512]{1,0:T(8,128)}) custom-call(bf16[512,768]{1,0:T(8,128)(2,1)} %get-tuple-element.117.rows_ref, bf16[768,8032]{1,0:T(8,128)(2,1)} %all-gather.12.cloned.1.call-done.table_ref, s32[512,1]{1,0:T(8,128)} %copy.61.ids_ref), custom_call_target="tpu_custom_call" | custom-call | flops 6316621824 | bytes 21348352 | tf_op jit(solution)/shard_map/head_forward/pallas_call | solution.py:205
  269.9 21.7 %head_forward.3 = (bf16[512,8032]{1,0:T(8,128)(2,1)}, f32[512,128]{1,0:T(8,128)}, f32[8,512]{1,0:T(8,128)}) custom-call(bf16[512,768]{1,0:T(8,128)(2,1)} %copy-done.12, bf16[768,8032]{1,0:T(8,128)(2,1)} %all-gather.12.cloned.1.call-done.table_ref, s32[512,1]{1,0:T(8,128)} %copy.62.ids_ref), custom_call_target="tpu_custom_call" | custom-call | flops 6316621824 | bytes 21348352 | tf_op jit(solution)/shard_map/head_forward/pallas_call | solution.py:205
  304.9 15.4 %row_grad.2 = f32[512,768]{1,0:T(8,128)} custom-call(bf16[768,8032]{1,0:T(8,128)(2,1)} %all-gather.12.cloned.1.call-done.table_ref, bf16[512,8032]{1,0:T(8,128)(2,1)} %get-tuple-element.58.prob_ref.refs_4_, f32[512,128]{1,0:T(8,128)} %get-tuple-element.125.coef_ref.refs_5_), custom_call_target="tpu_custom_call" | custom-call | flops 6316621824 | bytes 22134784 | tf_op jit(solution)/shard_map/row_grad/pallas_call | solution.py:344
  320.4 20.8 %table_grad.1 = bf16[768,8032]{1,0:T(8,128)(2,1)} custom-call(bf16[768,512]{1,0:T(8,128)(2,1)} %copy.63.refs_0_, bf16[512,8032]{1,0:T(8,128)(2,1)} %get-tuple-element.56.refs_1_.prob_ref, f32[512,128]{1,0:T(8,128)} %get-tuple-element.60.refs_2_.coef_ref, bf16[768,512]{1,0:T(8,128)(2,1)} %copy.64.refs_3_, ...), custom_call_target="tpu_custom_call" | custom-call | flops 12633243648 | bytes 30359552 | tf_op jit(solution)/shard_map/table_grad/pallas_call | solution.py:307
  346.7 18.0 %row_grad.3 = f32[512,768]{1,0:T(8,128)} custom-call(bf16[768,8032]{1,0:T(8,128)(2,1)} %all-gather.12.cloned.1.call-done.table_ref, bf16[512,8032]{1,0:T(8,128)(2,1)} %get-tuple-element.56.refs_1_.prob_ref, f32[512,128]{1,0:T(8,128)} %get-tuple-element.60.refs_2_.coef_ref), custom_call_target="tpu_custom_call" | custom-call | flops 6316621824 | bytes 22134784 | tf_op jit(solution)/shard_map/row_grad/pallas_call | solution.py:344
  381.0 8.4 %collective-permute-done.24 = bf16[256,768]{1,0:T(8,128)(2,1)S(1)} collective-permute-done((bf16[256,768]{1,0:T(8,128)(2,1)S(1)}, bf16[256,768]{1,0:T(8,128)(2,1)S(1)}, u32[]{:S(2)}, u32[]{:S(2)}) %collective-permute-start.24) | collective-permute-done | bytes 393248 | tf_op jit(solution)/shard_map/ppermute | solution.py:388
  396.1 35.7 %reduce-scatter.4.cloned.1.call-done = bf16[96,8032]{1,0:T(8,128)(2,1)} async-done(((bf16[768,8032]{1,0:T(8,128)(2,1)}), bf16[96,8032]{1,0:T(8,128)(2,1)}) %reduce-scatter.4.cloned.1.call-update) | async-done | bytes 1542160 | tf_op jit(solution)/shard_map/reduce_scatter | solution.py:396
  446.1 9.4 %collective-permute-done.25 = bf16[256,768]{1,0:T(8,128)(2,1)S(1)} collective-permute-done((bf16[256,768]{1,0:T(8,128)(2,1)S(1)}, bf16[256,768]{1,0:T(8,128)(2,1)S(1)}, u32[]{:S(2)}, u32[]{:S(2)}) %collective-permute-start.25) | collective-permute-done | bytes 393248 | tf_op jit(solution)/shard_map/ppermute | solution.py:388
  458.5 8.5 %collective-permute-done.26 = bf16[256,768]{1,0:T(8,128)(2,1)S(1)} collective-permute-done((bf16[256,768]{1,0:T(8,128)(2,1)S(1)}, bf16[256,768]{1,0:T(8,128)(2,1)S(1)}, u32[]{:S(2)}, u32[]{:S(2)}) %collective-permute-start.26) | collective-permute-done | bytes 393248 | tf_op jit(solution)/shard_map/ppermute | solution.py:388
  468.3 14.7 %attend_back.2 = (bf16[512,384]{1,0:T(8,128)(2,1)}, bf16[1024,384]{1,0:T(8,128)(2,1)}, bf16[1024,384]{1,0:T(8,128)(2,1)}) custom-call(s32[5]{0:T(128)} %stack.263.scal_ref, bf16[512,384]{1,0:T(8,128)(2,1)} %convolution_convert_fusion.15.q_ref, bf16[1024,384]{1,0:T(8,128)(2,1)} %convolution_convert_fusion.4.k_ref, ...), custom_call_target="tpu_custom_call" | custom-call | flops 4026531840 | bytes 5111808 | tf_op jit(solution)/shard_map/attend_back/pallas_call | solution.py:143
  505.1 9.4 %attend_back.3 = (bf16[512,384]{1,0:T(8,128)(2,1)}, bf16[512,384]{1,0:T(8,128)(2,1)}, bf16[512,384]{1,0:T(8,128)(2,1)}) custom-call(s32[5]{0:T(128)} %stack.251.scal_ref, bf16[512,384]{1,0:T(8,128)(2,1)} %convolution_convert_fusion.18.q_ref, bf16[512,384]{1,0:T(8,128)(2,1)} %convolution_convert_fusion.17.k_ref, ...), custom_call_target="tpu_custom_call" | custom-call | flops 2013265920 | bytes 3538944 | tf_op jit(solution)/shard_map/attend_back/pallas_call | solution.py:143
  548.7 12.9 %collective-permute-done.14 = bf16[128,768]{1,0:T(8,128)(2,1)S(1)} collective-permute-done((bf16[128,768]{1,0:T(8,128)(2,1)S(1)}, bf16[128,768]{1,0:T(8,128)(2,1)S(1)}, u32[]{:S(2)}, u32[]{:S(2)}) %collective-permute-start.14) | collective-permute-done | bytes 196640 | tf_op jit(solution)/shard_map/ppermute | solution.py:388
  578.9 12.7 %collective-permute-done.32 = bf16[256,768]{1,0:T(8,128)(2,1)S(1)} collective-permute-done((bf16[256,768]{1,0:T(8,128)(2,1)S(1)}, bf16[256,768]{1,0:T(8,128)(2,1)S(1)}, u32[]{:S(2)}, u32[]{:S(2)}) %collective-permute-start.32) | collective-permute-done | bytes 393248 | tf_op jit(solution)/shard_map/ppermute | solution.py:388
  615.0 13.8 %collective-permute-done.36 = bf16[8,96,192]{2,1,0:T(8,128)(2,1)S(1)} collective-permute-done((bf16[8,96,192]{2,1,0:T(8,128)(2,1)S(1)}, bf16[8,96,192]{2,1,0:T(8,128)(2,1)S(1)}, u32[]{:S(2)}, u32[]{:S(2)}) %collective-permute-start.36) | collective-permute-done | bytes 294944 | tf_op jit(solution)/shard_map/ppermute | solution.py:388
  (421 shorter events, 268.7 us)
Async XLA Ops:
  7.2 46.4 %all-gather.6.cloned.1.call-start = ((), (), s32[]{:S(2)}) async-start(), calls=%async_computation.3 | async-start | bytes 2654208 | tf_op jit(solution)/shard_map/all_gather | solution.py:392
  23.3 77.8 %all-gather.8.cloned.1.call-start = ((), (), s32[]{:S(2)}) async-start(), calls=%async_computation.4 | async-start | bytes 2654208 | tf_op jit(solution)/shard_map/all_gather | solution.py:392
  53.7 115.1 %all-gather.10.cloned.1.call-start = ((), (), s32[]{:S(2)}) async-start(), calls=%async_computation.5 | async-start | bytes 5308416 | tf_op jit(solution)/shard_map/all_gather | solution.py:392
  53.8 18.6 %collective-permute-start.2 = (bf16[128,768]{1,0:T(8,128)(2,1)S(1)}, bf16[128,768]{1,0:T(8,128)(2,1)S(1)}, u32[]{:S(2)}, u32[]{:S(2)}) collective-permute-start(bf16[128,768]{1,0:T(8,128)(2,1)S(1)} %get-tuple-element.128), channel_id=1, source_target_pairs={{0,3},{1,2},{2,1},{3,0},{4,7},{5,6},{6,5},{7,4},{8,11},{9,10},{10,... | collective-permute-start | bytes 589832 | tf_op jit(solution)/shard_map/ppermute | solution.py:388
  57.2 24.3 %collective-permute-start = (bf16[128,768]{1,0:T(8,128)(2,1)S(1)}, bf16[128,768]{1,0:T(8,128)(2,1)S(1)}, u32[]{:S(2)}, u32[]{:S(2)}) collective-permute-start(bf16[128,768]{1,0:T(8,128)(2,1)S(1)} %get-tuple-element.128), channel_id=1, source_target_pairs={{0,2},{1,3},{2,0},{3,1},{4,6},{5,7},{6,4},{7,5},{8,10},{9,11},{10,... | collective-permute-start | bytes 589832 | tf_op jit(solution)/shard_map/ppermute | solution.py:388
  58.0 29.3 %collective-permute-start.12 = (bf16[3,96,512]{2,1,0:T(8,128)(2,1)}, bf16[3,96,512]{2,1,0:T(8,128)(2,1)}, u32[]{:S(2)}, u32[]{:S(2)}) collective-permute-start(bf16[3,96,512]{2,1,0:T(8,128)(2,1)} %pad_maximum_fusion.22), channel_id=1, source_target_pairs={{0,2},{1,3},{2,0},{3,1},{4,6},{5,7},{6,4},{7,5},{8,10},{9,11},{10,... | collective-permute-start | bytes 884744 | tf_op jit(solution)/shard_map/ppermute | solution.py:388
  60.9 20.6 %collective-permute-start.1 = (bf16[128,768]{1,0:T(8,128)(2,1)S(1)}, bf16[128,768]{1,0:T(8,128)(2,1)S(1)}, u32[]{:S(2)}, u32[]{:S(2)}) collective-permute-start(bf16[128,768]{1,0:T(8,128)(2,1)S(1)} %get-tuple-element.127), channel_id=1, source_target_pairs={{0,1},{1,0},{2,3},{3,2},{4,5},{5,4},{6,7},{7,6},{8,9},{9,8},{10,11... | collective-permute-start | bytes 589832 | tf_op jit(solution)/shard_map/ppermute | solution.py:388
  101.1 146.1 %all-gather.12.cloned.1.call-start = ((), (), s32[]{:S(2)}) async-start(), calls=%async_computation.6 | async-start | bytes 13934592 | tf_op jit(solution)/shard_map/all_gather | solution.py:392
  115.0 21.6 %collective-permute-start.5 = (bf16[256,768]{1,0:T(8,128)(2,1)}, bf16[256,768]{1,0:T(8,128)(2,1)}, u32[]{:S(2)}, u32[]{:S(2)}) collective-permute-start(bf16[256,768]{1,0:T(8,128)(2,1)} %multiply_convert_fusion.5), channel_id=1, source_target_pairs={{0,1},{1,0},{2,3},{3,2},{4,5},{5,4},{6,7},{7,6},{8,9},{9,8},{10,11... | collective-permute-start | bytes 1179656 | tf_op jit(solution)/shard_map/ppermute | solution.py:388
  116.2 22.8 %collective-permute-start.9 = (bf16[256,768]{1,0:T(8,128)(2,1)}, bf16[256,768]{1,0:T(8,128)(2,1)}, u32[]{:S(2)}, u32[]{:S(2)}) collective-permute-start(bf16[256,768]{1,0:T(8,128)(2,1)} %get-tuple-element.119), channel_id=1, source_target_pairs={{0,3},{1,2},{2,1},{3,0},{4,7},{5,6},{6,5},{7,4},{8,11},{9,10},{10,... | collective-permute-start | bytes 1179656 | tf_op jit(solution)/shard_map/ppermute | solution.py:388
  118.6 33.8 %collective-permute-start.7 = (bf16[256,768]{1,0:T(8,128)(2,1)}, bf16[256,768]{1,0:T(8,128)(2,1)}, u32[]{:S(2)}, u32[]{:S(2)}) collective-permute-start(bf16[256,768]{1,0:T(8,128)(2,1)} %get-tuple-element.119), channel_id=1, source_target_pairs={{0,2},{1,3},{2,0},{3,1},{4,6},{5,7},{6,4},{7,5},{8,10},{9,11},{10,... | collective-permute-start | bytes 1179656 | tf_op jit(solution)/shard_map/ppermute | solution.py:388
  119.4 32.9 %collective-permute-start.8 = (bf16[256,768]{1,0:T(8,128)(2,1)}, bf16[256,768]{1,0:T(8,128)(2,1)}, u32[]{:S(2)}, u32[]{:S(2)}) collective-permute-start(bf16[256,768]{1,0:T(8,128)(2,1)} %get-tuple-element.118), channel_id=1, source_target_pairs={{0,1},{1,0},{2,3},{3,2},{4,5},{5,4},{6,7},{7,6},{8,9},{9,8},{10,11... | collective-permute-start | bytes 1179656 | tf_op jit(solution)/shard_map/ppermute | solution.py:388
  168.9 262.9 %reduce-scatter.4.cloned.1.call-start = ((), (), s32[]{:S(2)}) async-start(), calls=%async_computation.7 | async-start | bytes 13934592 | tf_op jit(solution)/shard_map/reduce_scatter | solution.py:396
  209.3 32.4 %collective-permute-start.17 = (bf16[256,768]{1,0:T(8,128)(2,1)}, bf16[256,768]{1,0:T(8,128)(2,1)}, u32[]{:S(2)}, u32[]{:S(2)}) collective-permute-start(bf16[256,768]{1,0:T(8,128)(2,1)} %multiply_convert_fusion.3), channel_id=1, source_target_pairs={{0,3},{1,2},{2,1},{3,0},{4,7},{5,6},{6,5},{7,4},{8,11},{9,10},{10,... | collective-permute-start | bytes 1179656 | tf_op jit(solution)/shard_map/ppermute | solution.py:388
  211.5 29.2 %collective-permute-start.16 = (bf16[256,768]{1,0:T(8,128)(2,1)}, bf16[256,768]{1,0:T(8,128)(2,1)}, u32[]{:S(2)}, u32[]{:S(2)}) collective-permute-start(bf16[256,768]{1,0:T(8,128)(2,1)} %multiply_convert_fusion.3), channel_id=1, source_target_pairs={{0,2},{1,3},{2,0},{3,1},{4,6},{5,7},{6,4},{7,5},{8,10},{9,11},{10,... | collective-permute-start | bytes 1179656 | tf_op jit(solution)/shard_map/ppermute | solution.py:388
  213.8 30.1 %collective-permute-start.15 = (bf16[256,768]{1,0:T(8,128)(2,1)}, bf16[256,768]{1,0:T(8,128)(2,1)}, u32[]{:S(2)}, u32[]{:S(2)}) collective-permute-start(bf16[256,768]{1,0:T(8,128)(2,1)} %multiply_convert_fusion.3), channel_id=1, source_target_pairs={{0,1},{1,0},{2,3},{3,2},{4,5},{5,4},{6,7},{7,6},{8,9},{9,8},{10,11... | collective-permute-start | bytes 1179656 | tf_op jit(solution)/shard_map/ppermute | solution.py:388
  341.2 178.3 %reduce-scatter.6.cloned.1.call-start = ((), (), s32[]{:S(2)}) async-start(), calls=%async_computation.8 | async-start | bytes 5308416 | tf_op jit(solution)/shard_map/reduce_scatter | solution.py:396
  342.8 26.4 %collective-permute-start.21 = (bf16[256,768]{1,0:T(8,128)(2,1)S(1)}, bf16[256,768]{1,0:T(8,128)(2,1)S(1)}, u32[]{:S(2)}, u32[]{:S(2)}) collective-permute-start(bf16[256,768]{1,0:T(8,128)(2,1)S(1)} %get-tuple-element.114), channel_id=1, source_target_pairs={{0,2},{1,3},{2,0},{3,1},{4,6},{5,7},{6,4},{7,5},{8,10},{9,11},{10,... | collective-permute-start | bytes 1179656 | tf_op jit(solution)/shard_map/ppermute | solution.py:388
  344.9 24.4 %collective-permute-start.22 = (bf16[256,768]{1,0:T(8,128)(2,1)S(1)}, bf16[256,768]{1,0:T(8,128)(2,1)S(1)}, u32[]{:S(2)}, u32[]{:S(2)}) collective-permute-start(bf16[256,768]{1,0:T(8,128)(2,1)S(1)} %get-tuple-element.115), channel_id=1, source_target_pairs={{0,3},{1,2},{2,1},{3,0},{4,7},{5,6},{6,5},{7,4},{8,11},{9,10},{10,... | collective-permute-start | bytes 1179656 | tf_op jit(solution)/shard_map/ppermute | solution.py:388
  439.1 165.8 %reduce-scatter.8.cloned.1.call-start = ((), (), s32[]{:S(2)}) async-start(), calls=%async_computation.9 | async-start | bytes 5971968 | tf_op jit(solution)/shard_map/reduce_scatter | solution.py:396
  541.9 25.5 %collective-permute-start.31 = (bf16[512,768]{1,0:T(8,128)(2,1)}, bf16[512,768]{1,0:T(8,128)(2,1)}, u32[]{:S(2)}, u32[]{:S(2)}) collective-permute-start(bf16[512,768]{1,0:T(8,128)(2,1)} %slice.595), channel_id=1, source_target_pairs={{0,1},{1,0},{2,3},{3,2},{4,5},{5,4},{6,7},{7,6},{8,9},{9,8},{10,11... | collective-permute-start | bytes 2359304 | tf_op jit(solution)/shard_map/ppermute | solution.py:388
  569.0 22.6 %collective-permute-start.32 = (bf16[256,768]{1,0:T(8,128)(2,1)S(1)}, bf16[256,768]{1,0:T(8,128)(2,1)S(1)}, u32[]{:S(2)}, u32[]{:S(2)}) collective-permute-start(bf16[256,768]{1,0:T(8,128)(2,1)S(1)} %slice.596), channel_id=1, source_target_pairs={{0,2},{1,3},{2,0},{3,1},{4,6},{5,7},{6,4},{7,5},{8,10},{9,11},{10,... | collective-permute-start | bytes 1179656 | tf_op jit(solution)/shard_map/ppermute | solution.py:388
  576.7 24.7 %collective-permute-start.30 = (bf16[128,768]{1,0:T(8,128)(2,1)S(1)}, bf16[128,768]{1,0:T(8,128)(2,1)S(1)}, u32[]{:S(2)}, u32[]{:S(2)}) collective-permute-start(bf16[128,768]{1,0:T(8,128)(2,1)S(1)} %slice.604), channel_id=1, source_target_pairs={{0,2},{1,3},{2,0},{3,1},{4,6},{5,7},{6,4},{7,5},{8,10},{9,11},{10,... | collective-permute-start | bytes 589832 | tf_op jit(solution)/shard_map/ppermute | solution.py:388
  612.1 16.6 %collective-permute-start.36 = (bf16[8,96,192]{2,1,0:T(8,128)(2,1)S(1)}, bf16[8,96,192]{2,1,0:T(8,128)(2,1)S(1)}, u32[]{:S(2)}, u32[]{:S(2)}) collective-permute-start(bf16[8,96,192]{2,1,0:T(8,128)(2,1)S(1)} %slice.449), channel_id=1, source_target_pairs={{0,2},{1,3},{2,0},{3,1},{4,6},{5,7},{6,4},{7,5},{8,10},{9,11},{10,... | collective-permute-start | bytes 884744 | tf_op jit(solution)/shard_map/ppermute | solution.py:388
  (110 other events, 1338.3 us)
Sparse Core Ops, SparseCore 0:
  23.4 30.1 all-gather.5
  56.1 29.0 all-gather.7
  101.2 37.9 all-gather.9
  169.0 70.3 all-gather.11
  341.3 90.3 reduce-scatter.3
  439.2 53.8 reduce-scatter.5
  536.8 57.0 reduce-scatter.7

commit v2 on v1

v2 whole, which is shorter than its diff:
```python
import functools

import jax
import jax.numpy as jnp
from jax import lax
from jax.experimental import pallas as pl
from jax.experimental.pallas import tpu as pltpu
from jax.sharding import PartitionSpec as P

DH = 64
LANES = 128
EPSILON = 1e-06
MASKED_OUT = -1000000000.0
GELU_SCALE = 0.7978845608028654
VMEM_LIMIT = 56 * 1024 * 1024
VOCAB_BLOCK = 2048
HIDDEN_BLOCK = 256
LOG2_E = 1.4426950408889634
BF16 = jnp.bfloat16
F32 = jnp.float32


def params():
    return pltpu.CompilerParams(
        dimension_semantics=("arbitrary",), vmem_limit_bytes=VMEM_LIMIT
    )


def mm(a, b):
    return lax.dot_general(a, b, (((1,), (0,)), ((), ())), preferred_element_type=F32)


def mm_nt(a, b):
    return lax.dot_general(a, b, (((1,), (1,)), ((), ())), preferred_element_type=F32)


def mm_tn(a, b):
    return lax.dot_general(a, b, (((0,), (0,)), ((), ())), preferred_element_type=F32)


def block_positions(scal_ref, size, dim):
    shape = (size, 1) if dim == 0 else (1, size)
    pieces = [lax.broadcasted_iota(jnp.int32, shape, dim) + scal_ref[i] * size for i in range(4)]
    return jnp.concatenate(pieces, axis=dim)


def score_bias(scal_ref, rows, keys, causal):
    key_pos = block_positions(scal_ref, keys // 4, 1)
    allowed = key_pos < scal_ref[4]
    if causal:
        row_pos = block_positions(scal_ref, rows // 4, 0)
        allowed = allowed & (key_pos <= row_pos)
    return jnp.where(allowed, 0.0, MASKED_OUT)


def head_lanes(rows, head):
    lane = lax.broadcasted_iota(jnp.int32, (rows, LANES), 1)
    return (lane < DH) if head == 0 else (lane >= DH)


def attend_heads(q, k, v, bias):
    rows = q.shape[0]
    outs, lses = [], []
    for head in range(2):
        q_head = jnp.where(head_lanes(rows, head), q, jnp.zeros_like(q))
        scores = mm_nt(q_head, k) + bias
        highest = jnp.max(scores, -1, keepdims=True)
        raised = jnp.exp(scores - highest)
        totals = jnp.sum(raised, -1, keepdims=True)
        outs.append(mm(raised.astype(BF16), v) * (1.0 / totals))
        lses.append(highest + jnp.log(totals))
    first = head_lanes(rows, 0)
    return jnp.where(first, outs[0], outs[1]).astype(BF16), jnp.where(first, lses[0], lses[1])


def attend_heads_back(q, k, v, lse, d_out, bias):
    rows, keys = q.shape[0], k.shape[0]
    dqs, dks, dvs = [], [], []
    for head in range(2):
        mine = head_lanes(rows, head)
        q_head = jnp.where(mine, q, jnp.zeros_like(q))
        d_head = jnp.where(mine, d_out, jnp.zeros_like(d_out))
        weights = jnp.exp(mm_nt(q_head, k) + bias - lse[:, head * DH : head * DH + 1])
        d_weights = mm_nt(d_head, v)
        inner = jnp.sum(weights * d_weights, -1, keepdims=True)
        d_scores = (weights * (d_weights - inner)).astype(BF16)
        dqs.append(mm(d_scores, k))
        dks.append(mm_tn(d_scores, q))
        dvs.append(mm_tn(weights.astype(BF16), d_out))
    first = head_lanes(keys, 0)
    return (
        jnp.where(head_lanes(rows, 0), dqs[0], dqs[1]).astype(BF16),
        jnp.where(first, dks[0], dks[1]).astype(BF16),
        jnp.where(first, dvs[0], dvs[1]).astype(BF16),
    )


def leave(total, own_ref, other_ref):
    @pl.when(pl.program_id(0) == pl.num_programs(0) - 1)
    def _():
        half = own_ref.shape[0]
        own_ref[...] = total[:half, :]
        other_ref[...] = total[half:, :].astype(BF16)


def stack_rows(own_ref, other_ref, rows):
    half = own_ref.shape[0]
    rows[:half, :] = own_ref[...]
    rows[half:, :] = other_ref[...]


def whole(shape):
    return pl.BlockSpec(shape, lambda j, *_: (0,) * len(shape))


def columns(rows, block):
    return pl.BlockSpec((rows, block), lambda j, *_: (0, j))


def weight_block(count, place, width, block):
    return pl.BlockSpec((count, width, block), lambda j, *_: (place, 0, j))


def sized(shape, dtype):
    return jax.ShapeDtypeStruct(shape, dtype)


def sublayer(kernel, name, scal, operands, specs, outs, out_specs, scratch, steps, flops, moved):
    return pl.pallas_call(
        kernel,
        out_shape=outs,
        grid_spec=pltpu.PrefetchScalarGridSpec(
            num_scalar_prefetch=1,
            grid=(steps,),
            in_specs=specs,
            out_specs=out_specs,
            scratch_shapes=scratch,
        ),
        compiler_params=params(),
        cost_estimate=pl.CostEstimate(flops=flops, transcendentals=0, bytes_accessed=moved),
        name=name,
    )(scal, *operands)


def self_forward_kernel(
    scal_ref, *refs
):
    pieces, (gain_ref, w_ref) = refs[:4], refs[4:6]
    q_ref, k_ref, v_ref, mixed_ref, lse_ref, rows_ref, own_ref, other_ref, total, bias = refs[6:]
    count = rows_ref.shape[0]

    @pl.when(pl.program_id(0) == 0)
    def _():
        size = pieces[0].shape[0]
        for i, piece in enumerate(pieces):
            normed, _ = norm_rows(piece[...].astype(F32), gain_ref[...])
            rows_ref[i * size : (i + 1) * size, :] = normed.astype(BF16)
        bias[...] = score_bias(scal_ref, count, count, True)
        total[...] = jnp.zeros_like(total)

    rows = rows_ref[...]
    q_ref[...] = mm(rows, w_ref[0]).astype(BF16)
    k_ref[...] = mm(rows, w_ref[1]).astype(BF16)
    v_ref[...] = mm(rows, w_ref[2]).astype(BF16)
    mixed, lse_ref[...] = attend_heads(q_ref[...], k_ref[...], v_ref[...], bias[...])
    mixed_ref[...] = mixed
    total[...] += mm_nt(mixed, w_ref[3])
    leave(total, own_ref, other_ref)


def self_forward(scal, pieces, gain, weights):
    block, width = pieces[0].shape
    count, cols = 4 * block, weights.shape[2]
    half = count // 2
    narrow = sized((count, cols), BF16)
    return sublayer(
        self_forward_kernel,
        "self_forward",
        scal,
        (*pieces, gain, weights),
        [whole((block, width))] * 4 + [whole((1, width)), weight_block(4, 0, width, LANES)],
        (narrow, narrow, narrow, narrow, sized((count, cols), F32))
        + (sized((count, width), BF16), sized((half, width), F32), sized((half, width), BF16)),
        [columns(count, LANES)] * 5
        + [whole((count, width)), whole((half, width)), whole((half, width))],
        [pltpu.VMEM((count, width), F32), pltpu.VMEM((count, count), F32)],
        cols // LANES,
        8 * count * width * cols + 8 * count * count * cols,
        8 * width * cols + 12 * count * cols + 8 * count * width,
    )


def cross_forward_kernel(
    scal_ref, h_own_ref, h_other_ref, w_ref, k_ref, v_ref,
    q_ref, mixed_ref, lse_ref, own_ref, other_ref, rows, total,
):
    @pl.when(pl.program_id(0) == 0)
    def _():
        stack_rows(h_own_ref, h_other_ref, rows)
        total[...] = jnp.zeros_like(total)

    bias = score_bias(scal_ref, rows.shape[0], k_ref.shape[0], False)
    q_ref[...] = mm(rows[...], w_ref[0]).astype(BF16)
    mixed, lse_ref[...] = attend_heads(q_ref[...], k_ref[...], v_ref[...], bias)
    mixed_ref[...] = mixed
    total[...] += mm_nt(mixed, w_ref[3])
    leave(total, own_ref, other_ref)


def cross_forward(scal, own, other, weights, k, v):
    half, width = own.shape
    count, cols, keys = 2 * half, weights.shape[2], k.shape[0]
    return sublayer(
        cross_forward_kernel,
        "cross_forward",
        scal,
        (own, other, weights, k, v),
        [whole((half, width))] * 2
        + [weight_block(4, 1, width, LANES), columns(keys, LANES), columns(keys, LANES)],
        (sized((count, cols), BF16), sized((count, cols), BF16), sized((count, cols), F32))
        + (sized((half, width), F32), sized((half, width), BF16)),
        [columns(count, LANES)] * 3 + [whole((half, width))] * 2,
        [pltpu.VMEM((count, width), BF16), pltpu.VMEM((count, width), F32)],
        cols // LANES,
        4 * count * width * cols + 8 * count * keys * cols,
        8 * width * cols + 8 * count * cols + 4 * keys * cols + 8 * count * width,
    )


def mlp_forward_kernel(
    scal_ref, h_own_ref, h_other_ref, w_ref,
    gate_ref, up_ref, hidden_ref, own_ref, other_ref, rows, total,
):
    @pl.when(pl.program_id(0) == 0)
    def _():
        stack_rows(h_own_ref, h_other_ref, rows)
        total[...] = jnp.zeros_like(total)

    gate = mm(rows[...], w_ref[0])
    up = mm(rows[...], w_ref[1])
    hidden = gated_unit(gate, up).astype(BF16)
    gate_ref[...] = gate
    up_ref[...] = up
    hidden_ref[...] = hidden
    total[...] += mm_nt(hidden, w_ref[2])
    leave(total, own_ref, other_ref)


def mlp_forward(scal, own, other, weights):
    half, width = own.shape
    count, cols = 2 * half, weights.shape[2]
    return sublayer(
        mlp_forward_kernel,
        "mlp_forward",
        scal,
        (own, other, weights),
        [whole((half, width))] * 2 + [weight_block(3, 0, width, HIDDEN_BLOCK)],
        (sized((count, cols), F32), sized((count, cols), F32), sized((count, cols), BF16))
        + (sized((half, width), F32), sized((half, width), BF16)),
        [columns(count, HIDDEN_BLOCK)] * 3 + [whole((half, width))] * 2,
        [pltpu.VMEM((count, width), BF16), pltpu.VMEM((count, width), F32)],
        cols // HIDDEN_BLOCK,
        6 * count * width * cols,
        6 * width * cols + 10 * count * cols + 5 * count * width,
    )


def mlp_back_kernel(
    scal_ref, e_own_ref, e_other_ref, w_ref, gate_ref, up_ref,
    d_gate_ref, d_up_ref, own_ref, other_ref, rows, total,
):
    @pl.when(pl.program_id(0) == 0)
    def _():
        stack_rows(e_own_ref, e_other_ref, rows)
        total[...] = jnp.zeros_like(total)

    d_hidden = mm(rows[...], w_ref[2])
    gate, up = gate_ref[...], up_ref[...]
    inner = GELU_SCALE * (gate + 0.044715 * gate * gate * gate)
    bent = jnp.tanh(inner)
    slope = GELU_SCALE * (1.0 + 3.0 * 0.044715 * gate * gate)
    d_gelu = 0.5 * (1.0 + bent) + 0.5 * gate * (1.0 - bent * bent) * slope
    d_gate = (d_hidden * up * d_gelu).astype(BF16)
    d_up = (d_hidden * (0.5 * gate * (1.0 + bent))).astype(BF16)
    d_gate_ref[...] = d_gate
    d_up_ref[...] = d_up
    total[...] += mm_nt(d_gate, w_ref[0]) + mm_nt(d_up, w_ref[1])
    leave(total, own_ref, other_ref)


def mlp_back(scal, own, other, weights, gate, up):
    half, width = own.shape
    count, cols = 2 * half, weights.shape[2]
    return sublayer(
        mlp_back_kernel,
        "mlp_back",
        scal,
        (own, other, weights, gate, up),
        [whole((half, width))] * 2
        + [weight_block(3, 0, width, HIDDEN_BLOCK)]
        + [columns(count, HIDDEN_BLOCK)] * 2,
        (sized((count, cols), BF16), sized((count, cols), BF16))
        + (sized((half, width), F32), sized((half, width), BF16)),
        [columns(count, HIDDEN_BLOCK)] * 2 + [whole((half, width))] * 2,
        [pltpu.VMEM((count, width), BF16), pltpu.VMEM((count, width), F32)],
        cols // HIDDEN_BLOCK,
        6 * count * width * cols,
        6 * width * cols + 12 * count * cols + 5 * count * width,
    )


def mlp_grads_kernel(
    scal_ref, h_own_ref, h_other_ref, e_own_ref, e_other_ref, d_gate_ref, d_up_ref, hidden_ref,
    out_ref,
):
    half = h_own_ref.shape[0]
    for i, (own, other, d_ref) in enumerate(
        (
            (h_own_ref, h_other_ref, d_gate_ref),
            (h_own_ref, h_other_ref, d_up_ref),
            (e_own_ref, e_other_ref, hidden_ref),
        )
    ):
        terms = mm_tn(own[...], d_ref[:half, :]) + mm_tn(other[...], d_ref[half:, :])
        out_ref[i] = terms.astype(BF16)


def mlp_grads(scal, rows, branch, d_gate, d_up, hidden):
    half, width = rows[0].shape
    count, cols = hidden.shape
    return sublayer(
        mlp_grads_kernel,
        "mlp_grads",
        scal,
        (*rows, *branch, d_gate, d_up, hidden),
        [whole((half, width))] * 4 + [columns(count, HIDDEN_BLOCK)] * 3,
        sized((3, width, cols), BF16),
        weight_block(3, 0, width, HIDDEN_BLOCK),
        [],
        cols // HIDDEN_BLOCK,
        6 * count * width * cols,
        6 * width * cols + 6 * count * cols + 4 * count * width,
    )


def attention_back_kernel(
    causal, scal_ref, e_own_ref, e_other_ref, w_ref, q_ref, k_ref, v_ref, lse_ref,
    dq_ref, dk_ref, dv_ref, own_ref, other_ref, gain_ref, rows, total, bias, *pieces,
):
    @pl.when(pl.program_id(0) == 0)
    def _():
        stack_rows(e_own_ref, e_other_ref, rows)
        total[...] = jnp.zeros_like(total)
        bias[...] = score_bias(scal_ref, rows.shape[0], k_ref.shape[0], causal)

    d_mixed = mm(rows[...], w_ref[3]).astype(BF16)
    dq, dk, dv = attend_heads_back(
        q_ref[...], k_ref[...], v_ref[...], lse_ref[...], d_mixed, bias[...]
    )
    dq_ref[...] = dq
    dk_ref[...] = dk
    dv_ref[...] = dv
    terms = mm_nt(dq, w_ref[0])
    if causal:
        terms += mm_nt(dk, w_ref[1]) + mm_nt(dv, w_ref[2])
    total[...] += terms
    leave(total, own_ref, other_ref)

    if causal:
        @pl.when(pl.program_id(0) == pl.num_programs(0) - 1)
        def _():
            size = pieces[0].shape[0]
            summed = 0.0
            for i, piece in enumerate(pieces):
                values = piece[...].astype(F32)
                unit, _ = norm_rows(values, 1.0)
                part = total[i * size : (i + 1) * size, :] * unit
                summed = summed + jnp.sum(part, 0, keepdims=True)
            gain_ref[...] = jnp.broadcast_to(summed, gain_ref.shape)


def cross_back(scal, own, other, weights, q, k, v, lse):
    half, width = own.shape
    count, cols, keys = 2 * half, weights.shape[2], k.shape[0]

    def kernel(scal_ref, *refs):
        attention_back_kernel(False, scal_ref, *refs[:12], None, *refs[12:])

    return sublayer(
        kernel,
        "cross_back",
        scal,
        (own, other, weights, q, k, v, lse),
        [whole((half, width))] * 2
        + [weight_block(4, 1, width, LANES), columns(count, LANES)]
        + [columns(keys, LANES)] * 2
        + [columns(count, LANES)],
        (sized((count, cols), BF16), sized((keys, cols), BF16), sized((keys, cols), BF16))
        + (sized((half, width), F32), sized((half, width), BF16)),
        [columns(count, LANES), columns(keys, LANES), columns(keys, LANES)]
        + [whole((half, width))] * 2,
        [
            pltpu.VMEM((count, width), BF16),
            pltpu.VMEM((count, width), F32),
            pltpu.VMEM((1, keys), F32),
        ],
        cols // LANES,
        4 * count * width * cols + 20 * count * keys * cols,
        8 * width * cols + 8 * count * cols + 8 * keys * cols + 8 * count * width,
    )


def self_back(scal, own, other, weights, q, k, v, lse, pieces):
    half, width = own.shape
    count, cols = 2 * half, weights.shape[2]
    block = pieces[0].shape[0]

    def kernel(scal_ref, *refs):
        attention_back_kernel(True, scal_ref, *refs[:7], *refs[11:], *refs[7:11])

    narrow = sized((count, cols), BF16)
    return sublayer(
        kernel,
        "self_back",
        scal,
        (own, other, weights, q, k, v, lse, *pieces),
        [whole((half, width))] * 2
        + [weight_block(4, 0, width, LANES)]
        + [columns(count, LANES)] * 4
        + [whole((block, width))] * 4,
        (narrow, narrow, narrow, sized((half, width), F32), sized((half, width), BF16))
        + (sized((8, width), F32),),
        [columns(count, LANES)] * 3 + [whole((half, width))] * 2 + [whole((8, width))],
        [
            pltpu.VMEM((count, width), BF16),
            pltpu.VMEM((count, width), F32),
            pltpu.VMEM((count, count), F32),
        ],
        cols // LANES,
        8 * count * width * cols + 20 * count * count * cols,
        8 * width * cols + 20 * count * cols + 10 * count * width,
    )


def cross_grads_kernel(
    scal_ref, h_own, h_other, e_own, e_other, memory, dq, dk, dv, mixed, out_ref
):
    half = e_own.shape[0]

    def whole_grad(rows, d_ref):
        return mm_tn(rows[...], d_ref[...]).astype(BF16)

    def split_grad(own, other, d_ref):
        return (mm_tn(own[...], d_ref[:half, :]) + mm_tn(other[...], d_ref[half:, :])).astype(BF16)

    out_ref[0] = split_grad(h_own, h_other, dq)
    out_ref[1] = whole_grad(memory, dk)
    out_ref[2] = whole_grad(memory, dv)
    out_ref[3] = split_grad(e_own, e_other, mixed)


def cross_grads(scal, rows, branch, memory, narrow):
    half, width = rows[0].shape
    cols, keys = narrow[0].shape[1], memory.shape[0]
    return sublayer(
        cross_grads_kernel,
        "cross_grads",
        scal,
        (*rows, *branch, memory, *narrow),
        [whole((half, width))] * 4
        + [whole((keys, width))]
        + [columns(array.shape[0], LANES) for array in narrow],
        sized((8, width, cols), BF16),
        weight_block(4, 1, width, LANES),
        [],
        cols // LANES,
        (8 * half + 4 * keys) * width * cols,
        8 * width * cols + (8 * half + 4 * keys) * cols + 8 * half * width,
    )


def self_grads_kernel(scal_ref, h, e_own, e_other, dq, dk, dv, mixed, rest_ref, out_ref):
    half = e_own.shape[0]
    for i, d_ref in enumerate((dq, dk, dv)):
        out_ref[i] = mm_tn(h[...], d_ref[...]).astype(BF16)
    terms = mm_tn(e_own[...], mixed[:half, :]) + mm_tn(e_other[...], mixed[half:, :])
    out_ref[3] = terms.astype(BF16)


def self_grads(scal, rows, branch, narrow, rest):
    count, width = rows.shape
    cols = narrow[0].shape[1]
    return pl.pallas_call(
        self_grads_kernel,
        out_shape=sized(rest.shape, BF16),
        grid_spec=pltpu.PrefetchScalarGridSpec(
            num_scalar_prefetch=1,
            grid=(cols // LANES,),
            in_specs=[whole((count, width))]
            + [whole((count // 2, width))] * 2
            + [columns(count, LANES)] * 4
            + [pl.BlockSpec(memory_space=pl.ANY)],
            out_specs=weight_block(4, 0, width, LANES),
        ),
        input_output_aliases={8: 0},
        compiler_params=params(),
        cost_estimate=pl.CostEstimate(
            flops=8 * count * width * cols,
            transcendentals=0,
            bytes_accessed=8 * width * cols + 8 * count * cols + 4 * count * width,
        ),
        name="self_grads",
    )(scal, rows, *branch, *narrow, rest)


SUMS = 32
PICKS = 64
WEIGHT_LANE = 126
ID_LANE = 127
TURNED = 8


def column_bias(vocab, step, block):
    column = lax.broadcasted_iota(jnp.int32, (1, block), 1) + step * block
    return jnp.where(column < vocab, 0.0, MASKED_OUT)


def head_kernel(vocab, scale, rows_ref, table_ref, ids_ref, prob_ref, stat_ref, turned_ref):
    step = pl.program_id(0)
    block = table_ref.shape[1]
    table = table_ref[...]
    chunk = 128
    bias = column_bias(vocab, step, block)
    column = lax.broadcasted_iota(jnp.int32, (1, block), 1)
    lane = lax.broadcasted_iota(jnp.int32, (chunk, LANES), 1)
    for start in range(0, rows_ref.shape[0], chunk):
        part = pl.ds(start, chunk)
        products = mm(rows_ref[part, :], table) + bias
        highest = jnp.max(products, -1, keepdims=True)
        raised = jnp.exp2((products - highest) * (scale * LOG2_E))
        prob_ref[part, :] = raised.astype(BF16)
        totals = jnp.sum(raised, -1, keepdims=True)
        target = ids_ref[part, :] - step * block
        picked = jnp.sum(jnp.where(column == target, products, 0.0), -1, keepdims=True)
        stats = jnp.where(step == 0, 0.0, stat_ref[part, :])
        stats = jnp.where(lane == step, highest * scale, stats)
        stats = jnp.where(lane == SUMS + step, totals, stats)
        stat_ref[part, :] = jnp.where(lane == PICKS + step, picked * scale, stats)

    @pl.when(step == pl.num_programs(0) - 1)
    def _():
        stats = stat_ref[...].T
        steps = pl.num_programs(0)
        row = lax.broadcasted_iota(jnp.int32, (SUMS, stats.shape[1]), 0)
        tops = jnp.where(row < steps, stats[:SUMS], MASKED_OUT)
        highest = jnp.max(tops, 0, keepdims=True)
        totals = jnp.sum(stats[SUMS:PICKS] * jnp.exp(tops - highest), 0, keepdims=True)
        picked = jnp.sum(stats[PICKS : PICKS + SUMS], 0, keepdims=True)
        row = lax.broadcasted_iota(jnp.int32, (TURNED, stats.shape[1]), 0)
        turned_ref[...] = jnp.where(row == 0, highest, jnp.where(row == 1, totals, picked))


def head_forward(rows, table, ids, scale):
    count, width = rows.shape
    vocab = table.shape[1]
    steps = pl.cdiv(vocab, VOCAB_BLOCK)
    return pl.pallas_call(
        functools.partial(head_kernel, vocab, scale),
        out_shape=(
            jax.ShapeDtypeStruct((count, vocab), BF16),
            jax.ShapeDtypeStruct((count, LANES), F32),
            jax.ShapeDtypeStruct((TURNED, count), F32),
        ),
        grid=(steps,),
        in_specs=[
            pl.BlockSpec((count, width), lambda j: (0, 0)),
            pl.BlockSpec((width, VOCAB_BLOCK), lambda j: (0, j)),
            pl.BlockSpec((count, 1), lambda j: (0, 0)),
        ],
        out_specs=(
            pl.BlockSpec((count, VOCAB_BLOCK), lambda j: (0, j)),
            pl.BlockSpec((count, LANES), lambda j: (0, 0)),
            pl.BlockSpec((TURNED, count), lambda j: (0, 0)),
        ),
        compiler_params=params(),
        cost_estimate=pl.CostEstimate(
            flops=2 * count * width * vocab,
            transcendentals=count * vocab,
            bytes_accessed=2 * (count + width) * vocab + 2 * count * width,
        ),
        name="head_forward",
    )(rows, table, ids)


def combine_kernel(near_stat_ref, far_stat_ref, *refs):
    share_refs, (info_ref, near_ref, far_ref, loss_ref) = refs[:4], refs[4:]
    half = near_stat_ref.shape[0]
    count = 2 * half
    own = count // 4
    shares = [
        jnp.concatenate(
            [ref[:, (slot ^ step) * own : ((slot ^ step) + 1) * own] for slot in range(4)], axis=1
        )
        for step, ref in enumerate(share_refs)
    ]
    highest = functools.reduce(jnp.maximum, [share[0:1] for share in shares])
    totals = sum(share[1:2] * jnp.exp(share[0:1] - highest) for share in shares)
    picked = sum(share[2:3] for share in shares)
    log_totals = highest + jnp.log(totals)
    info = info_ref[...]
    loss_ref[...] = jnp.broadcast_to((log_totals - picked) * info[1:2], (TURNED, count))
    row = lax.broadcasted_iota(jnp.int32, (LANES, count), 0)
    turned = jnp.where(row == 0, log_totals, jnp.where(row == 1, info[0:1], info[2:3])).T
    lane = lax.broadcasted_iota(jnp.int32, (half, LANES), 1)
    for stat_ref, coef_ref, start in ((near_stat_ref, near_ref, 0), (far_stat_ref, far_ref, half)):
        part = turned[start : start + half]
        weight = part[:, 1:2]
        coef = weight * jnp.exp(jnp.minimum(stat_ref[...] - part[:, 0:1], 0.0))
        coef = jnp.where(lane == WEIGHT_LANE, weight, coef)
        coef_ref[...] = jnp.where(lane == ID_LANE, part[:, 2:3], coef)


def combine(near_stats, far_stats, shares, info):
    half = near_stats.shape[0]
    return pl.pallas_call(
        combine_kernel,
        out_shape=(
            sized((half, LANES), F32),
            sized((half, LANES), F32),
            sized((TURNED, 2 * half), F32),
        ),
        compiler_params=pltpu.CompilerParams(vmem_limit_bytes=VMEM_LIMIT),
        cost_estimate=pl.CostEstimate(
            flops=20 * half * LANES,
            transcendentals=2 * half * LANES,
            bytes_accessed=16 * half * LANES,
        ),
        name="combine",
    )(near_stats, far_stats, *shares, info)


def logit_grads(vocab, step, part, prob_ref, coef_ref):
    block = prob_ref.shape[1]
    coef = coef_ref[part, :]
    lane = lax.broadcasted_iota(jnp.int32, coef.shape, 1)
    factor = jnp.sum(jnp.where(lane == step, coef, 0.0), -1, keepdims=True)
    weight = coef[:, WEIGHT_LANE : WEIGHT_LANE + 1]
    target = coef[:, ID_LANE : ID_LANE + 1].astype(jnp.int32) - step * block
    column = lax.broadcasted_iota(jnp.int32, (1, block), 1)
    inside = column < vocab - step * block
    prob = prob_ref[part, :].astype(F32)
    grads = prob * factor - jnp.where(column == target, weight, 0.0)
    return jnp.where(inside, grads, 0.0).astype(BF16)


def table_block(vocab, step, table_ref):
    table = table_ref[...]
    column = lax.broadcasted_iota(jnp.int32, (1, table.shape[1]), 1) + step * table.shape[1]
    return jnp.where(column < vocab, table, jnp.zeros_like(table))


def add_up(step, out_ref, terms):
    @pl.when(step == 0)
    def _():
        out_ref[...] = terms

    @pl.when(step > 0)
    def _():
        out_ref[...] += terms


def rows_grad_kernel(vocab, table_ref, prob_ref, coef_ref, first_ref, second_ref, total):
    step = pl.program_id(0)
    grads = logit_grads(vocab, step, slice(None), prob_ref, coef_ref)
    add_up(step, total, mm_nt(grads, table_block(vocab, step, table_ref)))

    @pl.when(step == pl.num_programs(0) - 1)
    def _():
        half = first_ref.shape[0]
        first_ref[...] = total[:half, :].astype(first_ref.dtype)
        second_ref[...] = total[half:, :].astype(second_ref.dtype)


def rows_grad(table, prob, coef, dtype):
    width = table.shape[0]
    count, vocab = prob.shape
    half = whole((count // 2, width))
    return pl.pallas_call(
        functools.partial(rows_grad_kernel, vocab),
        out_shape=(sized((count // 2, width), dtype), sized((count // 2, width), BF16)),
        grid=(pl.cdiv(vocab, VOCAB_BLOCK),),
        in_specs=[
            columns(width, VOCAB_BLOCK),
            columns(count, VOCAB_BLOCK),
            whole((count, LANES)),
        ],
        out_specs=(half, half),
        scratch_shapes=[pltpu.VMEM((count, width), F32)],
        compiler_params=params(),
        cost_estimate=pl.CostEstimate(
            flops=2 * count * width * vocab,
            transcendentals=0,
            bytes_accessed=2 * (count + width) * vocab + 4 * count * width,
        ),
        name="rows_grad",
    )(table, prob, coef)


def table_grad_kernel(
    vocab, near_rows_ref, near_prob_ref, near_coef_ref, far_rows_ref, far_prob_ref, far_coef_ref, out_ref
):
    step = pl.program_id(0)
    near = logit_grads(vocab, step, slice(None), near_prob_ref, near_coef_ref)
    far = logit_grads(vocab, step, slice(None), far_prob_ref, far_coef_ref)
    out_ref[...] = (mm_tn(near_rows_ref[...], near) + mm_tn(far_rows_ref[...], far)).astype(BF16)


def table_grad(near, far):
    count, width = near[0].shape
    vocab = near[1].shape[1]
    specs = [whole((count, width)), columns(count, VOCAB_BLOCK), whole((count, LANES))]
    return pl.pallas_call(
        functools.partial(table_grad_kernel, vocab),
        out_shape=sized((width, vocab), BF16),
        grid=(pl.cdiv(vocab, VOCAB_BLOCK),),
        in_specs=specs * 2,
        out_specs=columns(width, VOCAB_BLOCK),
        compiler_params=params(),
        cost_estimate=pl.CostEstimate(
            flops=4 * count * width * vocab,
            transcendentals=0,
            bytes_accessed=(4 * count + 2 * width) * vocab + 4 * count * width,
        ),
        name="table_grad",
    )(*near, *far)


def gelu_tanh(values):
    return (
        0.5 * values * (1.0 + jnp.tanh(GELU_SCALE * (values + 0.044715 * values * values * values)))
    )


def gated_unit(gate_in, up_in):
    return gelu_tanh(gate_in) * up_in


def norm_rows(values, gain_vec):
    inverse = lax.rsqrt(jnp.mean(values * values, -1, keepdims=True) + EPSILON)
    return (values * inverse * gain_vec, inverse)


def norm_back(values, inverse, gain_vec, upstream):
    scaled = upstream * gain_vec
    inner_sum = jnp.mean(scaled * values, -1, keepdims=True)
    d_values = inverse * scaled - values * (inverse * inverse * inverse) * inner_sum
    d_gain = jnp.sum(upstream * values * inverse, axis=0)
    return (d_values, d_gain)


def swap(values, step):
    return lax.ppermute(values, "mp", [(i, i ^ step) for i in range(4)])


def total_of_all(values):
    for axis in ("mp", "batch"):
        size, step = lax.axis_size(axis), 1
        while step < size:
            moved = lax.ppermute(values, axis, [(i, i ^ step) for i in range(size)])
            values, step = values + moved, 2 * step
    return values


def gather_batch(values, axis):
    return lax.all_gather(values, "batch", axis=axis, tiled=True)


def scatter_batch(values, axis):
    return lax.psum_scatter(values, "batch", scatter_dimension=axis, tiled=True)


def after(values, earlier):
    return lax.optimization_barrier((values, earlier))[0]


def both_slices(weights):
    return jnp.concatenate([weights, swap(weights, 2)], axis=-1)


def own_slice(grads):
    cut = grads.shape[-1] // 2
    return grads[..., :cut], swap(grads[..., cut:], 2)


def local(
    hidden_in,
    memory,
    tgt_len,
    src_len,
    target_ids,
    task_ids,
    task_weight,
    gain_self,
    q_self,
    k_self,
    v_self,
    o_self,
    gain_cross,
    q_cross,
    k_cross,
    v_cross,
    o_cross,
    gain_mlp,
    mlp_gate,
    mlp_up,
    mlp_down,
    gain_exit,
    embed_table,
):
    place = lax.axis_index("mp")
    pair = place // 2
    lower = pair == 0
    others = [place, place ^ 2, place ^ 1, place ^ 3]
    block = hidden_in.shape[1]
    own_rows = 2 * block
    width = hidden_in.shape[2]
    vocab = embed_table.shape[1]

    def of_pair(values):
        return jnp.where(lower, values[0], values[1])

    def of_other(values):
        return jnp.where(lower, values[1], values[0])

    def pair_rows(values):
        mine, other = of_pair(values), of_other(values)
        second = swap(other, 2)
        return [mine, second, swap(mine, 1), swap(second, 1)]

    def placed(own, received):
        far = received.astype(own.dtype)
        return jnp.stack([jnp.where(lower, own, far), jnp.where(lower, far, own)])

    gain_size = gain_self.shape[0]
    gains = lax.all_gather(
        jnp.stack([gain_self, gain_cross, gain_mlp, gain_exit]), "batch", axis=1, tiled=True
    )
    gain_self, gain_cross, gain_mlp, gain_exit = (gains[i].astype(F32) for i in range(4))
    attention = [q_self, k_self, v_self, o_self, q_cross, k_cross, v_cross, o_cross]
    depth, slim = q_self.shape
    packed = [jnp.concatenate(attention[i : i + 2], axis=1) for i in range(0, 8, 2)]
    moved = swap(jnp.stack(packed), 2)
    w_both = jnp.stack(
        [
            jnp.concatenate([own, moved[i // 2, :, i % 2 * slim : (i % 2 + 1) * slim]], axis=1)
            for i, own in enumerate(attention)
        ]
    )
    w_both = gather_batch(after(w_both, gains), 1)
    own_rows_in = of_pair(hidden_in)
    second = swap(after(of_other(hidden_in), moved), 2)
    pieces = [own_rows_in, second, swap(own_rows_in, 1), swap(second, 1)]
    mlp_part = both_slices(after(jnp.stack([mlp_gate, mlp_up, mlp_down]), second))
    memory_pieces = pair_rows(after(memory, (pieces[2], pieces[3], mlp_part)))

    pair_tgt = jnp.where(lower, tgt_len[0], tgt_len[1])
    pair_src = jnp.where(lower, src_len[0], src_len[1])
    self_scal = jnp.stack(others + [pair_tgt]).astype(jnp.int32)
    cross_scal = jnp.stack(others + [pair_src]).astype(jnp.int32)

    residual = jnp.concatenate(pieces[:2], axis=0).astype(F32)
    q_one, k_one, v_one, mixed_one, lse_one, rows_one, own_terms, other_terms = self_forward(
        self_scal, pieces, gain_self[None], w_both
    )
    memory_rows = jnp.concatenate(memory_pieces, axis=0)
    w_mlp = gather_batch(after(mlp_part, (w_both, pieces, memory_pieces[1])), 1)
    k_two = mm(memory_rows, w_both[5]).astype(BF16)
    v_two = mm(memory_rows, w_both[6]).astype(BF16)
    own_terms = after(own_terms, (k_two, v_two))
    residual_one = residual + own_terms + swap(other_terms, 1).astype(F32)

    normed_two, inverse_two = norm_rows(residual_one, gain_cross)
    own_two = normed_two.astype(BF16)
    rows_two = (own_two, swap(own_two, 1))
    q_two, mixed_two, lse_two, own_terms, other_terms = cross_forward(
        cross_scal, *rows_two, w_both, k_two, v_two
    )
    table = gather_batch(after(embed_table, (w_mlp, rows_two[1])), 0)
    residual_two = residual_one + own_terms + swap(other_terms, 1).astype(F32)

    normed_three, inverse_three = norm_rows(residual_two, gain_mlp)
    own_three = normed_three.astype(BF16)
    rows_three = (own_three, swap(own_three, 1))
    gate, up_proj, hidden, own_terms, other_terms = mlp_forward(self_scal, *rows_three, w_mlp)
    residual_three = residual_two + own_terms + swap(other_terms, 1).astype(F32)
    finished = residual_three.astype(BF16)

    normed_four, inverse_four = norm_rows(residual_three, gain_exit)
    own_four = normed_four.astype(BF16)
    near_four = jnp.concatenate([own_four, swap(own_four, 1)], axis=0)
    far_four = (swap(own_four, 2), swap(own_four, 3))
    slot_blocks = [
        (of, other)
        for of, order in ((pair, others), (1 - pair, [others[i] for i in (1, 0, 3, 2)]))
        for other in order
    ]
    row_order = jnp.stack([of * 4 + other for of, other in slot_blocks])
    ids = target_ids.reshape(8, block)[row_order].reshape(8 * block)
    local_ids = ids - place * vocab
    local_ids = jnp.where((local_ids >= 0) & (local_ids < vocab), local_ids, -1)
    positions = (
        jnp.stack([other * block for _, other in slot_blocks])[:, None] + jnp.arange(block)[None, :]
    ).reshape(8 * block)
    slot_pair = jnp.repeat(jnp.stack([pair, 1 - pair]), 4 * block)
    lengths = jnp.where(slot_pair == 0, tgt_len[0], tgt_len[1])
    valid = (positions < lengths).astype(F32)
    tasks = task_weight.shape[0]
    task_scale = jnp.sum(
        jnp.where(task_ids[:, None] == jnp.arange(tasks)[None, :], task_weight[None, :], 0.0), -1
    )
    logit_scale = width ** (-0.5)
    row_scale = jnp.where(slot_pair == 0, task_scale[0], task_scale[1]) * valid * logit_scale

    info = jnp.stack([row_scale, valid, local_ids.astype(F32)])
    info = jnp.concatenate([info, jnp.zeros((TURNED - 3, info.shape[1]), F32)])
    half_rows = 2 * own_rows
    near_prob, near_stats, near_turned = head_forward(
        near_four, table, local_ids[:half_rows, None], logit_scale
    )
    far_four = jnp.concatenate(after(far_four, near_turned), axis=0)
    far_prob, far_stats, far_turned = head_forward(
        far_four, table, local_ids[half_rows:, None], logit_scale
    )
    mine = jnp.concatenate([near_turned, far_turned], axis=1)
    finished = after(finished, near_turned)
    finished_far = swap(finished[block:], 2)
    block_out = placed(finished[:block], finished_far)
    shares = [mine] + [swap(mine, step) for step in (1, 2, 3)]
    near_coef, far_coef, losses = combine(near_stats, far_stats, shares, info)
    half_sums = jnp.sum(losses[0].reshape(2, half_rows), -1)
    pair_sums = jnp.where(lower, half_sums, half_sums[::-1])
    pair_loss = pair_sums / tgt_len.astype(F32)

    table_terms = table_grad(
        (near_four, near_prob, after(near_coef, finished_far)), (far_four, far_prob, far_coef)
    )
    embed_sum = scatter_batch(table_terms, 0)
    far_two, far_three = rows_grad(table, far_prob, after(far_coef, table_terms), BF16)
    d_own, near_one = rows_grad(table, near_prob, after(near_coef, far_two), F32)
    far_two = swap(far_two, 2)
    d_four = d_own + swap(after(near_one, far_two), 1).astype(F32)
    d_four += far_two.astype(F32) + swap(far_three, 3).astype(F32)
    d_residual, exit_grad = norm_back(residual_three, inverse_four, gain_exit, d_four)

    own_branch = d_residual.astype(BF16)
    branch_three = (own_branch, swap(own_branch, 1))
    d_gate, d_up, own_terms, other_terms = mlp_back(self_scal, *branch_three, w_mlp, gate, up_proj)
    mlp_terms = mlp_grads(self_scal, rows_three, branch_three, d_gate, d_up, hidden)
    d_rows = own_terms + after(swap(other_terms, 1), mlp_terms).astype(F32)
    d_input, mlp_grad = norm_back(residual_two, inverse_three, gain_mlp, d_rows)
    d_residual = d_residual + d_input

    own_branch = d_residual.astype(BF16)
    branch_two = (own_branch, after(swap(own_branch, 1), embed_sum))
    mlp_scattered = scatter_batch(after(mlp_terms, branch_two[1]), 1)
    mlp_here, mlp_moved = own_slice(mlp_scattered)
    mlp_sum = mlp_here.astype(F32) + mlp_moved.astype(F32)
    dq_two, dk_two, dv_two, own_terms, other_terms = cross_back(
        cross_scal, *branch_two, w_both, q_two, k_two, v_two, lse_two
    )
    cross_terms = cross_grads(
        self_scal, rows_two, branch_two, memory_rows, (dq_two, dk_two, dv_two, mixed_two)
    )
    d_rows = own_terms + after(swap(other_terms, 1), cross_terms).astype(F32)
    d_input, cross_grad = norm_back(residual_one, inverse_two, gain_cross, d_rows)
    d_residual = d_residual + d_input

    own_branch = d_residual.astype(BF16)
    memory_terms = mm_nt(dk_two, w_both[5]) + mm_nt(dv_two, w_both[6])
    branch_one = (own_branch, after(swap(own_branch, 1), memory_terms))
    half = memory_terms.shape[0] // 2
    memory_sent = after(memory_terms[half:].astype(BF16), branch_one[1])
    memory_received = swap(memory_sent, 1)
    memory_own = memory_terms[:half] + memory_received.astype(F32)
    dq_one, dk_one, dv_one, own_terms, other_terms, self_grad = self_back(
        self_scal, *branch_one, w_both, q_one, k_one, v_one, lse_one, pieces
    )
    last_grads = self_grads(
        self_scal,
        after(rows_one, (mlp_scattered, memory_received)),
        branch_one,
        (dq_one, dk_one, dv_one, mixed_one),
        cross_terms,
    )
    last_sum = scatter_batch(last_grads, 1)
    memory_far = swap(memory_own[half // 2 :].astype(BF16), 2)
    memory_grad = placed(memory_own[: half // 2], memory_far)
    received = after(swap(other_terms, 1), (last_grads, mlp_moved))
    d_rows = own_terms + received.astype(F32)
    d_input, _ = norm_back(residual, norm_rows(residual, 1.0)[1], gain_self, d_rows)
    d_residual = d_residual + d_input
    hidden_far = swap(after(d_residual[block:].astype(BF16), memory_far), 2)
    hidden_grad = placed(d_residual[:block], hidden_far)
    gain_grads = jnp.stack([self_grad[0], cross_grad, mlp_grad, exit_grad])
    gain_grads = total_of_all(after(gain_grads, received))
    gain_sums = lax.dynamic_slice_in_dim(
        gain_grads, lax.axis_index("batch") * gain_size, gain_size, axis=1
    )
    sent = last_sum[..., slim:]
    moved = swap(jnp.concatenate([sent[:4], sent[4:]], axis=-1), 2)
    self_sum = last_sum[:4, :, :slim].astype(F32) + moved[..., :slim].astype(F32)
    cross_sum = last_sum[4:, :, :slim].astype(F32) + moved[..., slim:].astype(F32)
    return (
        block_out,
        pair_loss,
        hidden_grad,
        memory_grad,
        gain_sums[0],
        self_sum[0],
        self_sum[1],
        self_sum[2],
        self_sum[3],
        gain_sums[1],
        cross_sum[0],
        cross_sum[1],
        cross_sum[2],
        cross_sum[3],
        gain_sums[2],
        mlp_sum[0],
        mlp_sum[1],
        mlp_sum[2],
        gain_sums[3],
        embed_sum.astype(F32),
    )


def solution(mesh):
    assert mesh.shape["mp"] == 4
    rows = P("batch", "mp", None)
    vector = P("batch")
    matrix = P("batch", "mp")
    sub = (vector, matrix, matrix, matrix, matrix)
    mlp = (vector, matrix, matrix, matrix)
    weights = sub + sub + mlp + (vector, matrix)
    in_specs = (rows, rows, vector, vector, P("batch", None), vector, P()) + weights
    out_specs = (rows, vector, rows, rows) + weights
    return jax.shard_map(local, mesh=mesh, in_specs=in_specs, out_specs=out_specs, check_vma=False)
```

time: 646 us -> 522 us (0.81)
  waiting for transfers between devices: 276 us -> 196 us
  matrix products: 68 us -> 10.3 us
  Pallas kernels: 141 us -> 176 us
  local copies, waits for them, and re-layouts: 28.2 us -> 21.1 us
    pallas_call x8 -> x13, Pallas kernels: 97.7 us -> 150 us  [the longest x8 88.6 us: sublayer(): pl.pallas_call(kernel, out_shape=outs, grid_spec=pltpu.PrefetchScalarGrid...]
    ppermute x38 -> x34, waiting for transfers between devices: 223 us -> 186 us  [swap(): return lax.ppermute(values, 'mp', [(i, i ^ step) for i in range(4)])]
    reduce_scatter x3, waiting for transfers between devices: 35.7 us -> 1.39 us  [scatter_batch(): return lax.psum_scatter(values, 'batch', scatter_dimension=axis, tiled=True)]
    dot_general x11 -> x2, matrix products: 27.6 us -> 6.09 us  [mm(): lax.dot_general(a, b, (((1,), (0,)), ((), ())), preferred_element_type=F32)]
    dot_general x11 -> x0, matrix products: 20.9 us -> none  [mm_tn(): lax.dot_general(a, b, (((0,), (0,)), ((), ())), preferred_element_type=F32)]
    all_gather x4 -> x3, waiting for transfers between devices: 17.3 us -> 0.01 us  [gather_batch(): return lax.all_gather(values, 'batch', axis=axis, tiled=True)]
    pallas_call x2, Pallas kernels: 43.7 us -> 26.9 us  [head_forward(): pl.pallas_call(functools.partial(head_kernel, vocab, scale), out_shape=(j...]
    dot_general x11 -> x2, matrix products: 19.5 us -> 4.24 us  [mm_nt(): lax.dot_general(a, b, (((1,), (1,)), ((), ())), preferred_element_type=F32)]
  transfers between devices with their start and end apart: 45 -> 45, of which waited for: 28 -> 30; matrix products, arithmetic and copies ran while one was open for 17% -> 10% of each run, Pallas kernels for 9% -> 26%
where the time goes in v2:
time: 522 us; the launch traced here: 515 us
  waiting for transfers between devices  196 us (38%)
  Pallas kernels  176 us (34%)
  starting transfers between devices  45.5 us (9%)
  other arithmetic  39.2 us (8%)
  local copies, waits for them, and re-layouts  21.1 us (4%)
  between operations  18 us (3%)
  matrix products  10.3 us (2%)
  blocking collectives  8.9 us (2%)
    ppermute x34, waiting for transfers between devices, swap(): return lax.ppermute(values, 'mp', [(i, i ^ step) for i in range(4)])  186 us
    pallas_call x8, Pallas kernels, sublayer(): pl.pallas_call(kernel, out_shape=outs, grid_spec=pltpu.PrefetchScalarGrid...  88.6 us
    ppermute x34, starting transfers between devices, swap(): return lax.ppermute(values, 'mp', [(i, i ^ step) for i in range(4)])  40 us
    pallas_call x2, Pallas kernels, rows_grad(): pl.pallas_call(functools.partial(rows_grad_kernel, vocab), out_shape=(siz...  29.6 us
    pallas_call x2, Pallas kernels, head_forward(): pl.pallas_call(functools.partial(head_kernel, vocab, scale), out_shape=(j...  26.9 us
    pallas_call x1, Pallas kernels, table_grad(): pl.pallas_call(functools.partial(table_grad_kernel, vocab), out_shape=siz...  21.9 us
  transfers between devices with their start and end apart: 45, of which 30 were waited for; matrix products, arithmetic and copies ran while one was open for 10% of the time, Pallas kernels for 26%

profile of v2, /device:TPU:0, one launch (start us, length us, event | category | flops | bytes accessed | tf_op | source)
XLA Modules:
  0.0 515.4 jit_solution(1788697594543594151)
XLA Ops:
  14.3 8.9 %all-gather = bf16[8,96,4]{1,2,0:T(4,128)(2,1)S(1)} all-gather(bf16[1,96,4]{1,2,0:T(4,128)(2,1)S(1)} %maximum_bitcast_fusion.4), channel_id=1, replica_groups=mesh['batch'=8,'mp'=4] {'batch'}, dimensions={0}, use_global_device_ids=true | all-gather | bytes 6912 | tf_op jit(solution)/shard_map/all_gather | solution.py:845
  33.7 11.1 %collective-permute-done.1.refs_1_.refs_8_ = bf16[128,768]{1,0:T(8,128)(2,1)S(1)} collective-permute-done((bf16[128,768]{1,0:T(8,128)(2,1)S(1)}, bf16[128,768]{1,0:T(8,128)(2,1)S(1)}, u32[]{:S(2)}, u32[]{:S(2)}) %collective-permute-start.1) | collective-permute-done | bytes 196640 | tf_op jit(solution)/shard_map/ppermute | solution.py:762
  46.9 12.5 %collective-permute-done.4 = bf16[3,96,512]{2,1,0:T(8,128)(2,1)S(1)} collective-permute-done((bf16[3,96,512]{2,1,0:T(8,128)(2,1)S(1)}, bf16[3,96,512]{2,1,0:T(8,128)(2,1)S(1)}, u32[]{:S(2)}, u32[]{:S(2)}) %collective-permute-start.4) | collective-permute-done | bytes 294944 | tf_op jit(solution)/shard_map/ppermute | solution.py:762
  62.4 17.6 %collective-permute-done.5 = bf16[256,768]{1,0:T(8,128)(2,1)S(1)} collective-permute-done((bf16[256,768]{1,0:T(8,128)(2,1)S(1)}, bf16[256,768]{1,0:T(8,128)(2,1)S(1)}, u32[]{:S(2)}, u32[]{:S(2)}) %collective-permute-start.5) | collective-permute-done | bytes 393248 | tf_op jit(solution)/shard_map/ppermute | solution.py:762
  85.3 10.5 %self_forward.1 = (bf16[512,384]{1,0:T(8,128)(2,1)}, bf16[512,384]{1,0:T(8,128)(2,1)}, bf16[512,384]{1,0:T(8,128)(2,1)}, bf16[512,384]{1,0:T(8,128)(2,1)}, f32[5...) custom-call(s32[5]{0:T(128)} %stack.204.scal_ref, ...), custom_call_target="tpu_custom_call" | custom-call | flops 2013265920 | bytes 7864320 | tf_op jit(solution)/shard_map/self_forward/pallas_call | solution.py:129
  112.5 10.0 %collective-permute-done.9.h_other_ref.h_other = bf16[256,768]{1,0:T(8,128)(2,1)S(1)} collective-permute-done((bf16[256,768]{1,0:T(8,128)(2,1)S(1)}, bf16[256,768]{1,0:T(8,128)(2,1)S(1)}, u32[]{:S(2)}, u32[]{:S(2)}) %collective-permute-start.9) | collective-permute-done | bytes 393248 | tf_op jit(solution)/shard_map/ppermute | solution.py:762
  128.9 13.0 %cross_forward.1 = (bf16[512,384]{1,0:T(8,128)(2,1)}, bf16[512,384]{1,0:T(8,128)(2,1)}, f32[512,384]{1,0:T(8,128)}, f32[256,768]{1,0:T(8,128)}, bf16[256,768]{1,0:T(8,128)(2,1)}) custom-call(s32[5]{0:T(128)} %stack.224.scal_ref, bf16[256,768]{1,0:T(8,128)(2,1)} %copy-done.16, bf16[256,768]{1,0:T(8,128)(2,1)} %copy-done.30, ...), custom_call_target="tpu_custom_call" | custom-call | flops 2214592512 | bytes 8650752 | tf_op jit(solution)/shard_map/cross_forward/pallas_call | solution.py:129
  143.1 8.3 %collective-permute-done.10 = bf16[256,768]{1,0:T(8,128)(2,1)S(1)} collective-permute-done((bf16[256,768]{1,0:T(8,128)(2,1)}, bf16[256,768]{1,0:T(8,128)(2,1)S(1)}, u32[]{:S(2)}, u32[]{:S(2)}) %collective-permute-start.10) | collective-permute-done | bytes 393248 | tf_op jit(solution)/shard_map/ppermute | solution.py:762
  163.1 8.4 %mlp_forward.1 = (f32[512,1024]{1,0:T(8,128)}, f32[512,1024]{1,0:T(8,128)}, bf16[512,1024]{1,0:T(8,128)(2,1)}, f32[256,768]{1,0:T(8,128)}, bf16[256,768]{1,0:T(8,128)(2,1)}) custom-call(s32[5]{0:T(128)} %stack.204.scal_ref, bf16[256,768]{1,0:T(8,128)(2,1)} %copy-done.17, bf16[256,768]{1,0:T(8,128)(2,1)} %copy-done.31, ...), custom_call_target="tpu_custom_call" | custom-call | flops 2415919104 | bytes 11927552 | tf_op jit(solution)/shard_map/mlp_forward/pallas_call | solution.py:129
  192.6 13.4 %head_forward.2 = (bf16[512,8032]{1,0:T(8,128)(2,1)}, f32[512,128]{1,0:T(8,128)}, f32[8,512]{1,0:T(8,128)}) custom-call(bf16[512,768]{1,0:T(8,128)(2,1)} %pad_maximum_fusion.2.rows_ref.near_rows_ref, bf16[768,8032]{1,0:T(8,128)(2,1)} %all-gather.9.cloned.1.call-done.table_ref, s32[512,1]{1,0:T(8,128)} %copy.52.ids_ref), custom_call_target="tpu_custom_call" | custom-call | flops 6316621824 | bytes 21348352 | tf_op jit(solution)/shard_map/head_forward/pallas_call | solution.py:567
  206.7 14.3 %collective-permute-done.15 = bf16[256,768]{1,0:T(8,128)(2,1)} collective-permute-done((bf16[256,768]{1,0:T(8,128)(2,1)S(1)}, bf16[256,768]{1,0:T(8,128)(2,1)}, u32[]{:S(2)}, u32[]{:S(2)}) %collective-permute-start.15) | collective-permute-done | bytes 393248 | tf_op jit(solution)/shard_map/ppermute | solution.py:762
  223.0 13.5 %head_forward.3 = (bf16[512,8032]{1,0:T(8,128)(2,1)}, f32[512,128]{1,0:T(8,128)}, f32[8,512]{1,0:T(8,128)}) custom-call(bf16[512,768]{1,0:T(8,128)(2,1)} %copy-done.41, bf16[768,8032]{1,0:T(8,128)(2,1)} %all-gather.9.cloned.1.call-done.table_ref, s32[512,1]{1,0:T(8,128)} %copy.53.ids_ref), custom_call_target="tpu_custom_call" | custom-call | flops 6316621824 | bytes 21348352 | tf_op jit(solution)/shard_map/head_forward/pallas_call | solution.py:567
  252.2 21.9 %table_grad.1 = bf16[768,8032]{1,0:T(8,128)(2,1)} custom-call(bf16[512,768]{1,0:T(8,128)(2,1)} %pad_maximum_fusion.2.rows_ref.near_rows_ref, bf16[512,8032]{1,0:T(8,128)(2,1)} %get-tuple-element.111.near_prob_ref.prob_ref, f32[512,128]{1,0:T(8,128)} %get-tuple-element.118.near_coef_ref.coef_ref, bf16[512,768]{1,0:T(8,128)(2,1)} %copy-done.41, ...), custom_call_target="tpu_custom_call" | custom-call | flops 12633243648 | bytes 30359552 | tf_op jit(solution)/shard_map/table_grad/pallas_call | solution.py:722
  274.1 15.1 %rows_grad.2 = (bf16[256,768]{1,0:T(8,128)(2,1)}, bf16[256,768]{1,0:T(8,128)(2,1)}) custom-call(bf16[768,8032]{1,0:T(8,128)(2,1)} %all-gather.9.cloned.1.call-done.table_ref, bf16[512,8032]{1,0:T(8,128)(2,1)} %get-tuple-element.113.far_prob_ref.prob_ref, f32[512,128]{1,0:T(8,128)} %get-tuple-element.116.far_coef_ref.coef_ref), custom_call_target="tpu_custom_call" | custom-call | flops 6316621824 | bytes 22134784 | tf_op jit(solution)/shard_map/rows_grad/pallas_call | solution.py:688
  291.9 14.5 %rows_grad.3 = (f32[256,768]{1,0:T(8,128)}, bf16[256,768]{1,0:T(8,128)(2,1)}) custom-call(bf16[768,8032]{1,0:T(8,128)(2,1)} %all-gather.9.cloned.1.call-done.table_ref, bf16[512,8032]{1,0:T(8,128)(2,1)} %get-tuple-element.111.near_prob_ref.prob_ref, f32[512,128]{1,0:T(8,128)} %get-tuple-element.118.near_coef_ref.coef_ref), custom_call_target="tpu_custom_call" | custom-call | flops 6316621824 | bytes 22134784 | tf_op jit(solution)/shard_map/rows_grad/pallas_call | solution.py:688
  306.5 11.4 %collective-permute-done.20 = bf16[256,768]{1,0:T(8,128)(2,1)S(1)} collective-permute-done((bf16[256,768]{1,0:T(8,128)(2,1)}, bf16[256,768]{1,0:T(8,128)(2,1)S(1)}, u32[]{:S(2)}, u32[]{:S(2)}) %collective-permute-start.20) | collective-permute-done | bytes 393248 | tf_op jit(solution)/shard_map/ppermute | solution.py:762
  317.9 8.0 %collective-permute-done.21 = bf16[256,768]{1,0:T(8,128)(2,1)S(1)} collective-permute-done((bf16[256,768]{1,0:T(8,128)(2,1)}, bf16[256,768]{1,0:T(8,128)(2,1)S(1)}, u32[]{:S(2)}, u32[]{:S(2)}) %collective-permute-start.21) | collective-permute-done | bytes 393248 | tf_op jit(solution)/shard_map/ppermute | solution.py:762
  328.3 7.8 %collective-permute-done.23.e_other_ref = bf16[256,768]{1,0:T(8,128)(2,1)S(1)} collective-permute-done((bf16[256,768]{1,0:T(8,128)(2,1)S(1)}, bf16[256,768]{1,0:T(8,128)(2,1)S(1)}, u32[]{:S(2)}, u32[]{:S(2)}) %collective-permute-start.23) | collective-permute-done | bytes 393248 | tf_op jit(solution)/shard_map/ppermute | solution.py:762
  336.8 10.2 %mlp_back.1 = (bf16[512,1024]{1,0:T(8,128)(2,1)}, bf16[512,1024]{1,0:T(8,128)(2,1)}, f32[256,768]{1,0:T(8,128)}, bf16[256,768]{1,0:T(8,128)(2,1)}) custom-call(s32[5]{0:T(128)} %stack.204.scal_ref, bf16[256,768]{1,0:T(8,128)(2,1)} %copy-done, bf16[256,768]{1,0:T(8,128)(2,1)} %copy-done.13, bf16[3,768,1024]{2,1,0:T(8,128)(2,1)} %all-gather.7.cloned.1.call-done.w_ref, ...), custom_call_target="tpu_custom_call" | custom-call | flops 2415919104 | bytes 12976128 | tf_op jit(solution)/shard_map/mlp_back/pallas_call | solution.py:129
  369.1 16.3 %cross_back.1 = (bf16[512,384]{1,0:T(8,128)(2,1)}, bf16[1024,384]{1,0:T(8,128)(2,1)}, bf16[1024,384]{1,0:T(8,128)(2,1)}, f32[256,768]{1,0:T(8,128)}, bf16[256,768]{1,0:T(8,128)(2,1)}) custom-call(s32[5]{0:T(128)} %stack.224.scal_ref, bf16[256,768]{1,0:T(8,128)(2,1)} %copy-done.14, bf16[256,768]{1,0:T(8,128)(2,1)} %copy-done.32, ...), custom_call_target="tpu_custom_call" | custom-call | flops 4630511616 | bytes 10223616 | tf_op jit(solution)/shard_map/cross_back/pallas_call | solution.py:129
  387.1 8.5 %cross_grads.1.rest_ref = bf16[8,768,384]{2,1,0:T(8,128)(2,1)} custom-call(s32[5]{0:T(128)} %stack.204.scal_ref, bf16[256,768]{1,0:T(8,128)(2,1)} %copy-done.16, bf16[256,768]{1,0:T(8,128)(2,1)} %copy-done.30, bf16[256,768]{1,0:T(8,128)(2,1)} %copy-done.14, bf16[256,768]{1,0:T(8,128)(2,1)} %copy-done.32, bf16[1024,768]{1,0:T(8,128)(2,1)} %pad_maximum_fusion.memory, ...), custom_call_target="tpu_custom_call" | custom-call | flops 1811939328 | bytes 6291456 | tf_op jit(solution)/shard_map/cross_grads/pallas_call | solution.py:129
  409.3 14.0 %self_back.1 = (bf16[512,384]{1,0:T(8,128)(2,1)}, bf16[512,384]{1,0:T(8,128)(2,1)}, bf16[512,384]{1,0:T(8,128)(2,1)}, f32[256,768]{1,0:T(8,128)}, bf16[256,768]{1,0:T(8,128)(2,1)}, /*index=5*/f32[8,768]{1,0:T(8,128)}) custom-call(s32[5]{0:T(128)} %stack.204.scal_ref, bf16[256,768]{1,0:T(8,128)(2,1)} %copy-done.15, bf16[256,768]{1,0:T(8,128)(2,1)} %copy-done.33, ...), custom_call_target="tpu_custom_call" | custom-call | flops 3221225472 | bytes 10223616 | tf_op jit(solution)/shard_map/self_back/pallas_call | solution.py:129
  443.7 18.6 %collective-permute-done.31 = bf16[256,768]{1,0:T(8,128)(2,1)S(1)} collective-permute-done((bf16[256,768]{1,0:T(8,128)(2,1)S(1)}, bf16[256,768]{1,0:T(8,128)(2,1)S(1)}, u32[]{:S(2)}, u32[]{:S(2)}) %collective-permute-start.31) | collective-permute-done | bytes 393248 | tf_op jit(solution)/shard_map/ppermute | solution.py:762
  490.8 10.5 %collective-permute-done.32 = bf16[128,768]{1,0:T(8,128)(2,1)S(1)} collective-permute-done((bf16[128,768]{1,0:T(8,128)(2,1)S(1)}, bf16[128,768]{1,0:T(8,128)(2,1)S(1)}, u32[]{:S(2)}, u32[]{:S(2)}) %collective-permute-start.32) | collective-permute-done | bytes 196640 | tf_op jit(solution)/shard_map/ppermute | solution.py:762
  (357 shorter events, 199.1 us)
Async XLA Ops:
  7.3 72.7 %all-gather.5.cloned.1.call-start = ((), (), s32[]{:S(2)}) async-start(), calls=%async_computation.3 | async-start | bytes 5308416 | tf_op jit(solution)/shard_map/all_gather | solution.py:775
  9.5 17.4 %collective-permute-start = (bf16[4,96,384]{2,1,0:T(8,128)(2,1)S(1)}, bf16[4,96,384]{2,1,0:T(8,128)(2,1)S(1)}, u32[]{:S(2)}, u32[]{:S(2)}) collective-permute-start(bf16[4,96,384]{2,1,0:T(8,128)(2,1)S(1)} %pad_maximum_fusion.6), channel_id=1, source_target_pairs={{0,2},{1,3},{2,0},{3,1},{4,6},{5,7},{6,4},{7,5},{8,10},{9,11},{10,... | collective-permute-start | bytes 884744 | tf_op jit(solution)/shard_map/ppermute | solution.py:762
  33.5 89.0 %all-gather.7.cloned.1.call-start = ((), (), s32[]{:S(2)}) async-start(), calls=%async_computation.4 | async-start | bytes 5308416 | tf_op jit(solution)/shard_map/all_gather | solution.py:775
  44.9 14.6 %collective-permute-start.4 = (bf16[3,96,512]{2,1,0:T(8,128)(2,1)S(1)}, bf16[3,96,512]{2,1,0:T(8,128)(2,1)S(1)}, u32[]{:S(2)}, u32[]{:S(2)}) collective-permute-start(bf16[3,96,512]{2,1,0:T(8,128)(2,1)S(1)} %pad_maximum_fusion.7), channel_id=1, source_target_pairs={{0,2},{1,3},{2,0},{3,1},{4,6},{5,7},{6,4},{7,5},{8,10},{9,11},{10,... | collective-permute-start | bytes 884744 | tf_op jit(solution)/shard_map/ppermute | solution.py:762
  44.9 14.7 %collective-permute-start.2 = (bf16[128,768]{1,0:T(8,128)(2,1)S(1)}, bf16[128,768]{1,0:T(8,128)(2,1)S(1)}, u32[]{:S(2)}, u32[]{:S(2)}) collective-permute-start(bf16[128,768]{1,0:T(8,128)(2,1)S(1)} %get-tuple-element.211.refs_0_.refs_7_), channel_id=1, source_target_pairs={{0,1},{1,0},{2,3},{3,2},{4,5},{5,4},{6,7},{7,6},{8,9},{9,8},{10,11... | collective-permute-start | bytes 589832 | tf_op jit(solution)/shard_map/ppermute | solution.py:762
  46.6 15.0 %collective-permute-start.3 = (bf16[128,768]{1,0:T(8,128)(2,1)S(1)}, bf16[128,768]{1,0:T(8,128)(2,1)S(1)}, u32[]{:S(2)}, u32[]{:S(2)}) collective-permute-start(bf16[128,768]{1,0:T(8,128)(2,1)S(1)} %collective-permute-done.1.refs_1_.refs_8_), channel_id=1, source_target_pairs={{0,1},{1,0},{2,3},{3,2},{4,5},{5,4},{6,7},{7,6},{8,9},{9,8},{10,11... | collective-permute-start | bytes 589832 | tf_op jit(solution)/shard_map/ppermute | solution.py:762
  61.7 18.3 %collective-permute-start.5 = (bf16[256,768]{1,0:T(8,128)(2,1)S(1)}, bf16[256,768]{1,0:T(8,128)(2,1)S(1)}, u32[]{:S(2)}, u32[]{:S(2)}) collective-permute-start(bf16[256,768]{1,0:T(8,128)(2,1)S(1)} %get-tuple-element.194), channel_id=1, source_target_pairs={{0,2},{1,3},{2,0},{3,1},{4,6},{5,7},{6,4},{7,5},{8,10},{9,11},{10,... | collective-permute-start | bytes 1179656 | tf_op jit(solution)/shard_map/ppermute | solution.py:762
  80.0 112.5 %all-gather.9.cloned.1.call-start = ((), (), s32[]{:S(2)}) async-start(), calls=%async_computation.5 | async-start | bytes 13934592 | tf_op jit(solution)/shard_map/all_gather | solution.py:775
  82.6 13.3 %collective-permute-start.6 = (bf16[256,768]{1,0:T(8,128)(2,1)S(1)}, bf16[256,768]{1,0:T(8,128)(2,1)S(1)}, u32[]{:S(2)}, u32[]{:S(2)}) collective-permute-start(bf16[256,768]{1,0:T(8,128)(2,1)S(1)} %get-tuple-element.193), channel_id=1, source_target_pairs={{0,1},{1,0},{2,3},{3,2},{4,5},{5,4},{6,7},{7,6},{8,9},{9,8},{10,11... | collective-permute-start | bytes 1179656 | tf_op jit(solution)/shard_map/ppermute | solution.py:762
  82.7 20.4 %collective-permute-start.7 = (bf16[256,768]{1,0:T(8,128)(2,1)S(1)}, bf16[256,768]{1,0:T(8,128)(2,1)S(1)}, u32[]{:S(2)}, u32[]{:S(2)}) collective-permute-start(bf16[256,768]{1,0:T(8,128)(2,1)S(1)} %collective-permute-done.5), channel_id=1, source_target_pairs={{0,1},{1,0},{2,3},{3,2},{4,5},{5,4},{6,7},{7,6},{8,9},{9,8},{10,11... | collective-permute-start | bytes 1179656 | tf_op jit(solution)/shard_map/ppermute | solution.py:762
  95.8 14.8 %collective-permute-start.8 = (bf16[256,768]{1,0:T(8,128)(2,1)}, bf16[256,768]{1,0:T(8,128)(2,1)S(1)}, u32[]{:S(2)}, u32[]{:S(2)}) collective-permute-start(bf16[256,768]{1,0:T(8,128)(2,1)} %get-tuple-element.96), channel_id=1, source_target_pairs={{0,1},{1,0},{2,3},{3,2},{4,5},{5,4},{6,7},{7,6},{8,9},{9,8},{10,11... | collective-permute-start | bytes 1179656 | tf_op jit(solution)/shard_map/ppermute | solution.py:762
  122.5 245.2 %reduce-scatter.4.cloned.1.call-start = ((), (), s32[]{:S(2)}) async-start(), calls=%async_computation.6 | async-start | bytes 13934592 | tf_op jit(solution)/shard_map/reduce_scatter | solution.py:779
  184.9 21.8 %collective-permute-start.16 = (bf16[256,768]{1,0:T(8,128)(2,1)S(1)}, bf16[256,768]{1,0:T(8,128)(2,1)S(1)}, u32[]{:S(2)}, u32[]{:S(2)}) collective-permute-start(bf16[256,768]{1,0:T(8,128)(2,1)S(1)} %get-tuple-element.191), channel_id=1, source_target_pairs={{0,3},{1,2},{2,1},{3,0},{4,7},{5,6},{6,5},{7,4},{8,11},{9,10},{10,... | collective-permute-start | bytes 1179656 | tf_op jit(solution)/shard_map/ppermute | solution.py:762
  188.4 32.6 %collective-permute-start.15 = (bf16[256,768]{1,0:T(8,128)(2,1)S(1)}, bf16[256,768]{1,0:T(8,128)(2,1)}, u32[]{:S(2)}, u32[]{:S(2)}) collective-permute-start(bf16[256,768]{1,0:T(8,128)(2,1)S(1)} %get-tuple-element.191), channel_id=1, source_target_pairs={{0,2},{1,3},{2,0},{3,1},{4,6},{5,7},{6,4},{7,5},{8,10},{9,11},{10,... | collective-permute-start | bytes 1179656 | tf_op jit(solution)/shard_map/ppermute | solution.py:762
  274.1 150.1 %reduce-scatter.6.cloned.1.call-start = ((), (), s32[]{:S(2)}) async-start(), calls=%async_computation.7 | async-start | bytes 5308416 | tf_op jit(solution)/shard_map/reduce_scatter | solution.py:779
  289.2 28.7 %collective-permute-start.20 = (bf16[256,768]{1,0:T(8,128)(2,1)}, bf16[256,768]{1,0:T(8,128)(2,1)S(1)}, u32[]{:S(2)}, u32[]{:S(2)}) collective-permute-start(bf16[256,768]{1,0:T(8,128)(2,1)} %get-tuple-element.117), channel_id=1, source_target_pairs={{0,2},{1,3},{2,0},{3,1},{4,6},{5,7},{6,4},{7,5},{8,10},{9,11},{10,... | collective-permute-start | bytes 1179656 | tf_op jit(solution)/shard_map/ppermute | solution.py:762
  289.2 28.7 %collective-permute-start.22 = (bf16[256,768]{1,0:T(8,128)(2,1)}, bf16[256,768]{1,0:T(8,128)(2,1)S(1)}, u32[]{:S(2)}, u32[]{:S(2)}) collective-permute-start(bf16[256,768]{1,0:T(8,128)(2,1)} %get-tuple-element.122), channel_id=1, source_target_pairs={{0,3},{1,2},{2,1},{3,0},{4,7},{5,6},{6,5},{7,4},{8,11},{9,10},{10,... | collective-permute-start | bytes 1179656 | tf_op jit(solution)/shard_map/ppermute | solution.py:762
  367.7 119.1 %reduce-scatter.8.cloned.1.call-start = ((), (), s32[]{:S(2)}) async-start(), calls=%async_computation.8 | async-start | bytes 5308416 | tf_op jit(solution)/shard_map/reduce_scatter | solution.py:779
  408.6 15.6 %collective-permute-start.29 = (bf16[512,768]{1,0:T(8,128)(2,1)S(1)}, bf16[512,768]{1,0:T(8,128)(2,1)}, u32[]{:S(2)}, u32[]{:S(2)}) collective-permute-start(bf16[512,768]{1,0:T(8,128)(2,1)S(1)} %slice.356), channel_id=1, source_target_pairs={{0,1},{1,0},{2,3},{3,2},{4,5},{5,4},{6,7},{7,6},{8,9},{9,8},{10,11... | collective-permute-start | bytes 2359304 | tf_op jit(solution)/shard_map/ppermute | solution.py:762
  435.0 27.3 %collective-permute-start.31 = (bf16[256,768]{1,0:T(8,128)(2,1)S(1)}, bf16[256,768]{1,0:T(8,128)(2,1)S(1)}, u32[]{:S(2)}, u32[]{:S(2)}) collective-permute-start(bf16[256,768]{1,0:T(8,128)(2,1)S(1)} %slice.357), channel_id=1, source_target_pairs={{0,2},{1,3},{2,0},{3,1},{4,6},{5,7},{6,4},{7,5},{8,10},{9,11},{10,... | collective-permute-start | bytes 1179656 | tf_op jit(solution)/shard_map/ppermute | solution.py:762
  442.2 21.4 %collective-permute-start.28 = (bf16[256,768]{1,0:T(8,128)(2,1)S(1)}, bf16[256,768]{1,0:T(8,128)(2,1)S(1)}, u32[]{:S(2)}, u32[]{:S(2)}) collective-permute-start(bf16[256,768]{1,0:T(8,128)(2,1)S(1)} %copy-done.70), channel_id=1, source_target_pairs={{0,1},{1,0},{2,3},{3,2},{4,5},{5,4},{6,7},{7,6},{8,9},{9,8},{10,11... | collective-permute-start | bytes 1179656 | tf_op jit(solution)/shard_map/ppermute | solution.py:762
  443.6 24.0 %collective-permute-start.30 = (bf16[3,96,512]{2,1,0:T(8,128)(2,1)S(1)}, bf16[3,96,512]{2,1,0:T(8,128)(2,1)S(1)}, u32[]{:S(2)}, u32[]{:S(2)}) collective-permute-start(bf16[3,96,512]{2,1,0:T(8,128)(2,1)S(1)} %slice.267), channel_id=1, source_target_pairs={{0,2},{1,3},{2,0},{3,1},{4,6},{5,7},{6,4},{7,5},{8,10},{9,11},{10,... | collective-permute-start | bytes 884744 | tf_op jit(solution)/shard_map/ppermute | solution.py:762
  483.1 18.2 %collective-permute-start.32 = (bf16[128,768]{1,0:T(8,128)(2,1)S(1)}, bf16[128,768]{1,0:T(8,128)(2,1)S(1)}, u32[]{:S(2)}, u32[]{:S(2)}) collective-permute-start(bf16[128,768]{1,0:T(8,128)(2,1)S(1)} %slice.358), channel_id=1, source_target_pairs={{0,2},{1,3},{2,0},{3,1},{4,6},{5,7},{6,4},{7,5},{8,10},{9,11},{10,... | collective-permute-start | bytes 589832 | tf_op jit(solution)/shard_map/ppermute | solution.py:762
  488.3 18.5 %collective-permute-start.38 = (bf16[4,96,384]{2,1,0:T(8,128)(2,1)S(1)}, bf16[4,96,384]{2,1,0:T(8,128)(2,1)S(1)}, u32[]{:S(2)}, u32[]{:S(2)}) collective-permute-start(bf16[4,96,384]{2,1,0:T(8,128)(2,1)S(1)} %pad_maximum_fusion.8), channel_id=1, source_target_pairs={{0,2},{1,3},{2,0},{3,1},{4,6},{5,7},{6,4},{7,5},{8,10},{9,11},{10,... | collective-permute-start | bytes 884744 | tf_op jit(solution)/shard_map/ppermute | solution.py:762
  (96 other events, 1265.1 us)
Sparse Core Ops, SparseCore 0:
  33.6 40.0 all-gather.4
  80.1 38.2 all-gather.6
  122.6 68.9 all-gather.8
  274.2 90.6 reduce-scatter.3
  368.6 55.2 reduce-scatter.5
  431.3 55.5 reduce-scatter.7

commit v3 on v2

--- a/solution.py
+++ b/solution.py
@@ -442,33 +442,34 @@
     )
 
 
-def cross_grads_kernel(
-    scal_ref, h_own, h_other, e_own, e_other, memory, dq, dk, dv, mixed, out_ref
-):
+def cross_grads_kernel(scal_ref, h_own, h_other, e_own, e_other, *refs):
+    memory, (dq, dk, dv, mixed, out_ref) = refs[:4], refs[4:]
     half = e_own.shape[0]
 
-    def whole_grad(rows, d_ref):
-        return mm_tn(rows[...], d_ref[...]).astype(BF16)
+    def memory_grad(d_ref):
+        size = memory[0].shape[0]
+        terms = [mm_tn(m[...], d_ref[i * size : (i + 1) * size, :]) for i, m in enumerate(memory)]
+        return sum(terms).astype(BF16)
 
     def split_grad(own, other, d_ref):
         return (mm_tn(own[...], d_ref[:half, :]) + mm_tn(other[...], d_ref[half:, :])).astype(BF16)
 
     out_ref[0] = split_grad(h_own, h_other, dq)
-    out_ref[1] = whole_grad(memory, dk)
-    out_ref[2] = whole_grad(memory, dv)
+    out_ref[1] = memory_grad(dk)
+    out_ref[2] = memory_grad(dv)
     out_ref[3] = split_grad(e_own, e_other, mixed)
 
 
 def cross_grads(scal, rows, branch, memory, narrow):
     half, width = rows[0].shape
-    cols, keys = narrow[0].shape[1], memory.shape[0]
+    cols, keys = narrow[0].shape[1], narrow[1].shape[0]
     return sublayer(
         cross_grads_kernel,
         "cross_grads",
         scal,
-        (*rows, *branch, memory, *narrow),
+        (*rows, *branch, *memory, *narrow),
         [whole((half, width))] * 4
-        + [whole((keys, width))]
+        + [whole((keys // 4, width))] * 4
         + [columns(array.shape[0], LANES) for array in narrow],
         sized((8, width, cols), BF16),
         weight_block(4, 1, width, LANES),
@@ -756,6 +757,51 @@
     d_values = inverse * scaled - values * (inverse * inverse * inverse) * inner_sum
     d_gain = jnp.sum(upstream * values * inverse, axis=0)
     return (d_values, d_gain)
+
+
+def step_back(values, inverse, gain, own, received, d_residual):
+    upstream = own + sum(part.astype(F32) for part in received)
+    d_values, d_gain = norm_back(values, inverse, gain, upstream)
+    if d_residual is not None:
+        d_values = d_residual + d_values
+    return d_values, d_values.astype(BF16), d_gain
+
+
+def pack_kernel(*refs):
+    parts, out_ref = refs[:-1], refs[-1]
+    slim = parts[0].shape[1]
+    half = len(parts) // 2
+    for i, part in enumerate(parts):
+        side = i // half
+        out_ref[i % half, :, side * slim : (side + 1) * slim] = part[...]
+
+
+def pack_pairs(parts):
+    depth, slim = parts[0].shape
+    return pl.pallas_call(
+        pack_kernel,
+        out_shape=sized((len(parts) // 2, depth, 2 * slim), BF16),
+        name="pack_pairs",
+    )(*parts)
+
+
+def join_kernel(*refs):
+    parts, (moved_ref, out_ref) = refs[:-2], refs[-2:]
+    slim = parts[0].shape[1]
+    half = len(parts) // 2
+    for i, part in enumerate(parts):
+        side = i // half
+        out_ref[i, :, :slim] = part[...]
+        out_ref[i, :, slim:] = moved_ref[i % half, :, side * slim : (side + 1) * slim]
+
+
+def join_slices(parts, moved):
+    depth, slim = parts[0].shape
+    return pl.pallas_call(
+        join_kernel,
+        out_shape=sized((len(parts), depth, 2 * slim), BF16),
+        name="join_slices",
+    )(*parts, moved)
 
 
 def swap(values, step):
@@ -841,64 +887,12 @@
         far = received.astype(own.dtype)
         return jnp.stack([jnp.where(lower, own, far), jnp.where(lower, far, own)])
 
-    gain_size = gain_self.shape[0]
-    gains = lax.all_gather(
-        jnp.stack([gain_self, gain_cross, gain_mlp, gain_exit]), "batch", axis=1, tiled=True
-    )
-    gain_self, gain_cross, gain_mlp, gain_exit = (gains[i].astype(F32) for i in range(4))
-    attention = [q_self, k_self, v_self, o_self, q_cross, k_cross, v_cross, o_cross]
-    depth, slim = q_self.shape
-    packed = [jnp.concatenate(attention[i : i + 2], axis=1) for i in range(0, 8, 2)]
-    moved = swap(jnp.stack(packed), 2)
-    w_both = jnp.stack(
-        [
-            jnp.concatenate([own, moved[i // 2, :, i % 2 * slim : (i % 2 + 1) * slim]], axis=1)
-            for i, own in enumerate(attention)
-        ]
-    )
-    w_both = gather_batch(after(w_both, gains), 1)
-    own_rows_in = of_pair(hidden_in)
-    second = swap(after(of_other(hidden_in), moved), 2)
-    pieces = [own_rows_in, second, swap(own_rows_in, 1), swap(second, 1)]
-    mlp_part = both_slices(after(jnp.stack([mlp_gate, mlp_up, mlp_down]), second))
-    memory_pieces = pair_rows(after(memory, (pieces[2], pieces[3], mlp_part)))
-
     pair_tgt = jnp.where(lower, tgt_len[0], tgt_len[1])
     pair_src = jnp.where(lower, src_len[0], src_len[1])
     self_scal = jnp.stack(others + [pair_tgt]).astype(jnp.int32)
     cross_scal = jnp.stack(others + [pair_src]).astype(jnp.int32)
 
-    residual = jnp.concatenate(pieces[:2], axis=0).astype(F32)
-    q_one, k_one, v_one, mixed_one, lse_one, rows_one, own_terms, other_terms = self_forward(
-        self_scal, pieces, gain_self[None], w_both
-    )
-    memory_rows = jnp.concatenate(memory_pieces, axis=0)
-    w_mlp = gather_batch(after(mlp_part, (w_both, pieces, memory_pieces[1])), 1)
-    k_two = mm(memory_rows, w_both[5]).astype(BF16)
-    v_two = mm(memory_rows, w_both[6]).astype(BF16)
-    own_terms = after(own_terms, (k_two, v_two))
-    residual_one = residual + own_terms + swap(other_terms, 1).astype(F32)
-
-    normed_two, inverse_two = norm_rows(residual_one, gain_cross)
-    own_two = normed_two.astype(BF16)
-    rows_two = (own_two, swap(own_two, 1))
-    q_two, mixed_two, lse_two, own_terms, other_terms = cross_forward(
-        cross_scal, *rows_two, w_both, k_two, v_two
-    )
-    table = gather_batch(after(embed_table, (w_mlp, rows_two[1])), 0)
-    residual_two = residual_one + own_terms + swap(other_terms, 1).astype(F32)
-
-    normed_three, inverse_three = norm_rows(residual_two, gain_mlp)
-    own_three = normed_three.astype(BF16)
-    rows_three = (own_three, swap(own_three, 1))
-    gate, up_proj, hidden, own_terms, other_terms = mlp_forward(self_scal, *rows_three, w_mlp)
-    residual_three = residual_two + own_terms + swap(other_terms, 1).astype(F32)
-    finished = residual_three.astype(BF16)
-
-    normed_four, inverse_four = norm_rows(residual_three, gain_exit)
-    own_four = normed_four.astype(BF16)
-    near_four = jnp.concatenate([own_four, swap(own_four, 1)], axis=0)
-    far_four = (swap(own_four, 2), swap(own_four, 3))
+    half_rows = 2 * own_rows
     slot_blocks = [
         (of, other)
         for of, order in ((pair, others), (1 - pair, [others[i] for i in (1, 0, 3, 2)]))
@@ -923,13 +917,66 @@
 
     info = jnp.stack([row_scale, valid, local_ids.astype(F32)])
     info = jnp.concatenate([info, jnp.zeros((TURNED - 3, info.shape[1]), F32)])
-    half_rows = 2 * own_rows
+    near_ids, far_ids = local_ids[:half_rows, None], local_ids[half_rows:, None]
+
+    gain_size = gain_self.shape[0]
+    gains = lax.all_gather(
+        jnp.stack([gain_self, gain_cross, gain_mlp, gain_exit]), "batch", axis=1, tiled=True
+    )
+    attention = [q_self, k_self, v_self, o_self, q_cross, k_cross, v_cross, o_cross]
+    slim = q_self.shape[1]
+    moved = swap(pack_pairs(attention), 2)
+    w_both, gains, self_scal, cross_scal = lax.optimization_barrier(
+        (join_slices(attention, moved), gains.astype(F32), self_scal, cross_scal)
+    )
+    w_both = gather_batch(w_both, 1)
+    gain_self, gain_cross, gain_mlp, gain_exit = (gains[i] for i in range(4))
+    own_rows_in = of_pair(hidden_in)
+    second = swap(after(of_other(hidden_in), moved), 2)
+    pieces = [own_rows_in, second, swap(own_rows_in, 1), swap(second, 1)]
+    mlp_part = both_slices(after(jnp.stack([mlp_gate, mlp_up, mlp_down]), moved))
+    memory_pieces = pair_rows(after(memory, second))
+
+    residual = jnp.concatenate(pieces[:2], axis=0).astype(F32)
+    w_mlp = gather_batch(after(mlp_part, (w_both, pieces, memory_pieces[1])), 1)
+    q_one, k_one, v_one, mixed_one, lse_one, rows_one, own_terms, other_terms = self_forward(
+        self_scal, pieces, gain_self[None], w_both
+    )
+    memory_rows = jnp.concatenate(memory_pieces, axis=0)
+    k_two = mm(memory_rows, w_both[5]).astype(BF16)
+    v_two = mm(memory_rows, w_both[6]).astype(BF16)
+    own_terms = after(own_terms, (k_two, v_two))
+    residual_one = residual + own_terms + swap(other_terms, 1).astype(F32)
+
+    normed_two, inverse_two = norm_rows(residual_one, gain_cross)
+    own_two = normed_two.astype(BF16)
+    rows_two = (own_two, swap(own_two, 1))
+    q_two, mixed_two, lse_two, own_terms, other_terms = cross_forward(
+        cross_scal, *rows_two, w_both, k_two, v_two
+    )
+    table = gather_batch(after(embed_table, (w_mlp, rows_two[1])), 0)
+    residual_two = residual_one + own_terms + swap(other_terms, 1).astype(F32)
+
+    normed_three, inverse_three = norm_rows(residual_two, gain_mlp)
+    own_three = normed_three.astype(BF16)
+    other_three, info, near_ids, far_ids = lax.optimization_barrier(
+        (swap(own_three, 1), info, near_ids, far_ids)
+    )
+    rows_three = (own_three, other_three)
+    gate, up_proj, hidden, own_terms, other_terms = mlp_forward(self_scal, *rows_three, w_mlp)
+    residual_three = residual_two + own_terms + swap(other_terms, 1).astype(F32)
+    finished = residual_three.astype(BF16)
+
+    normed_four, inverse_four = norm_rows(residual_three, gain_exit)
+    own_four = normed_four.astype(BF16)
+    near_four = jnp.concatenate([own_four, swap(own_four, 1)], axis=0)
+    far_four = (swap(own_four, 2), swap(own_four, 3))
     near_prob, near_stats, near_turned = head_forward(
-        near_four, table, local_ids[:half_rows, None], logit_scale
+        near_four, table, near_ids, logit_scale
     )
     far_four = jnp.concatenate(after(far_four, near_turned), axis=0)
     far_prob, far_stats, far_turned = head_forward(
-        far_four, table, local_ids[half_rows:, None], logit_scale
+        far_four, table, far_ids, logit_scale
     )
     mine = jnp.concatenate([near_turned, far_turned], axis=1)
     finished = after(finished, near_turned)
@@ -942,25 +989,26 @@
     pair_loss = pair_sums / tgt_len.astype(F32)
 
     table_terms = table_grad(
-        (near_four, near_prob, after(near_coef, finished_far)), (far_four, far_prob, far_coef)
+        (near_four, near_prob, near_coef), (far_four, far_prob, far_coef)
     )
     embed_sum = scatter_batch(table_terms, 0)
     far_two, far_three = rows_grad(table, far_prob, after(far_coef, table_terms), BF16)
-    d_own, near_one = rows_grad(table, near_prob, after(near_coef, far_two), F32)
-    far_two = swap(far_two, 2)
-    d_four = d_own + swap(after(near_one, far_two), 1).astype(F32)
-    d_four += far_two.astype(F32) + swap(far_three, 3).astype(F32)
-    d_residual, exit_grad = norm_back(residual_three, inverse_four, gain_exit, d_four)
-
-    own_branch = d_residual.astype(BF16)
+    far_three = swap(far_three, 1)
+    d_own, near_one = rows_grad(table, near_prob, after(near_coef, (far_two, finished_far)), F32)
+    far_two = far_two.astype(F32) + after(far_three, near_one).astype(F32)
+    received = (swap(near_one, 1), swap(far_two.astype(BF16), 2))
+    d_residual, own_branch, exit_grad = step_back(
+        residual_three, inverse_four, gain_exit, d_own, received, None
+    )
+
     branch_three = (own_branch, swap(own_branch, 1))
     d_gate, d_up, own_terms, other_terms = mlp_back(self_scal, *branch_three, w_mlp, gate, up_proj)
     mlp_terms = mlp_grads(self_scal, rows_three, branch_three, d_gate, d_up, hidden)
-    d_rows = own_terms + after(swap(other_terms, 1), mlp_terms).astype(F32)
-    d_input, mlp_grad = norm_back(residual_two, inverse_three, gain_mlp, d_rows)
-    d_residual = d_residual + d_input
-
-    own_branch = d_residual.astype(BF16)
+    received = (after(swap(other_terms, 1), mlp_terms),)
+    d_residual, own_branch, mlp_grad = step_back(
+        residual_two, inverse_three, gain_mlp, own_terms, received, d_residual
+    )
+
     branch_two = (own_branch, after(swap(own_branch, 1), embed_sum))
     mlp_scattered = scatter_batch(after(mlp_terms, branch_two[1]), 1)
     mlp_here, mlp_moved = own_slice(mlp_scattered)
@@ -969,13 +1017,13 @@
         cross_scal, *branch_two, w_both, q_two, k_two, v_two, lse_two
     )
     cross_terms = cross_grads(
-        self_scal, rows_two, branch_two, memory_rows, (dq_two, dk_two, dv_two, mixed_two)
-    )
-    d_rows = own_terms + after(swap(other_terms, 1), cross_terms).astype(F32)
-    d_input, cross_grad = norm_back(residual_one, inverse_two, gain_cross, d_rows)
-    d_residual = d_residual + d_input
-
-    own_branch = d_residual.astype(BF16)
+        self_scal, rows_two, branch_two, memory_pieces, (dq_two, dk_two, dv_two, mixed_two)
+    )
+    received = (after(swap(other_terms, 1), cross_terms),)
+    d_residual, own_branch, cross_grad = step_back(
+        residual_one, inverse_two, gain_cross, own_terms, received, d_residual
+    )
+
     memory_terms = mm_nt(dk_two, w_both[5]) + mm_nt(dv_two, w_both[6])
     branch_one = (own_branch, after(swap(own_branch, 1), memory_terms))
     half = memory_terms.shape[0] // 2
@@ -994,15 +1042,16 @@
     )
     last_sum = scatter_batch(last_grads, 1)
     memory_far = swap(memory_own[half // 2 :].astype(BF16), 2)
+    gain_grads = jnp.stack([self_grad[0], cross_grad, mlp_grad, exit_grad])
+    gain_grads = total_of_all(after(gain_grads, last_grads))
+    memory_far = after(memory_far, gain_grads)
     memory_grad = placed(memory_own[: half // 2], memory_far)
-    received = after(swap(other_terms, 1), (last_grads, mlp_moved))
-    d_rows = own_terms + received.astype(F32)
-    d_input, _ = norm_back(residual, norm_rows(residual, 1.0)[1], gain_self, d_rows)
-    d_residual = d_residual + d_input
+    received = (after(swap(other_terms, 1), (last_grads, mlp_moved)),)
+    d_residual, _, _ = step_back(
+        residual, norm_rows(residual, 1.0)[1], gain_self, own_terms, received, d_residual
+    )
     hidden_far = swap(after(d_residual[block:].astype(BF16), memory_far), 2)
     hidden_grad = placed(d_residual[:block], hidden_far)
-    gain_grads = jnp.stack([self_grad[0], cross_grad, mlp_grad, exit_grad])
-    gain_grads = total_of_all(after(gain_grads, received))
     gain_sums = lax.dynamic_slice_in_dim(
         gain_grads, lax.axis_index("batch") * gain_size, gain_size, axis=1
     )

time: 522 us -> 501 us (0.960)
  waiting for transfers between devices: 196 us -> 157 us
  starting transfers between devices: 45.5 us -> 63.2 us
  other arithmetic: 39.2 us -> 32 us
    ppermute x34, waiting for transfers between devices: 186 us -> 150 us  [swap(): return lax.ppermute(values, 'mp', [(i, i ^ step) for i in range(4)])]
    ppermute x34, starting transfers between devices: 40 us -> 56.6 us  [swap(): return lax.ppermute(values, 'mp', [(i, i ^ step) for i in range(4)])]
    ppermute x5, waiting for transfers between devices: 8.84 us -> 3.14 us  [total_of_all(): moved = lax.ppermute(values, axis, [(i, i ^ step) for i in range(size)])]
    unnamed x8 -> x1, other arithmetic: 6.17 us -> 0.72 us
  transfers between devices with their start and end apart: 45 -> 45, of which waited for: 30 -> 25; matrix products, arithmetic and copies ran while one was open for 10% -> 12% of each run, Pallas kernels for 26% -> 27%
where the time goes in v3:
time: 501 us; the launch traced here: 495 us
  Pallas kernels  181 us (36%)
  waiting for transfers between devices  157 us (31%)
  starting transfers between devices  63.2 us (13%)
  other arithmetic  32 us (6%)
  local copies, waits for them, and re-layouts  25 us (5%)
  between operations  17.8 us (4%)
  matrix products  10.4 us (2%)
  blocking collectives  8.9 us (2%)
    ppermute x34, waiting for transfers between devices, swap(): return lax.ppermute(values, 'mp', [(i, i ^ step) for i in range(4)])  150 us
    pallas_call x8, Pallas kernels, sublayer(): pl.pallas_call(kernel, out_shape=outs, grid_spec=pltpu.PrefetchScalarGrid...  88.3 us
    ppermute x34, starting transfers between devices, swap(): return lax.ppermute(values, 'mp', [(i, i ^ step) for i in range(4)])  56.6 us
    pallas_call x2, Pallas kernels, rows_grad(): pl.pallas_call(functools.partial(rows_grad_kernel, vocab), out_shape=(siz...  30.3 us
    pallas_call x2, Pallas kernels, head_forward(): pl.pallas_call(functools.partial(head_kernel, vocab, scale), out_shape=(j...  26.9 us
    pallas_call x1, Pallas kernels, table_grad(): pl.pallas_call(functools.partial(table_grad_kernel, vocab), out_shape=siz...  21.7 us
  transfers between devices with their start and end apart: 45, of which 25 were waited for; matrix products, arithmetic and copies ran while one was open for 12% of the time, Pallas kernels for 27%

profile of v3, /device:TPU:0, one launch (start us, length us, event | category | flops | bytes accessed | tf_op | source)
XLA Modules:
  0.0 494.8 jit_solution(18281476488863958196)
XLA Ops:
  20.4 8.9 %all-gather = bf16[8,96,4]{1,2,0:T(4,128)(2,1)S(1)} all-gather(bf16[1,96,4]{1,2,0:T(4,128)(2,1)S(1)} %maximum_bitcast_fusion), channel_id=1, replica_groups=mesh['batch'=8,'mp'=4] {'batch'}, dimensions={0}, use_global_device_ids=true | all-gather | bytes 6912 | tf_op jit(solution)/shard_map/all_gather | solution.py:923
  36.5 16.1 %collective-permute-done.1.refs_1_.refs_8_ = bf16[128,768]{1,0:T(8,128)(2,1)S(1)} collective-permute-done((bf16[128,768]{1,0:T(8,128)(2,1)S(1)}, bf16[128,768]{1,0:T(8,128)(2,1)S(1)}, u32[]{:S(2)}, u32[]{:S(2)}) %collective-permute-start.1) | collective-permute-done | bytes 196640 | tf_op jit(solution)/shard_map/ppermute | solution.py:808
  54.9 12.6 %collective-permute-done.11 = bf16[3,96,512]{2,1,0:T(8,128)(2,1)S(1)} collective-permute-done((bf16[3,96,512]{2,1,0:T(8,128)(2,1)S(1)}, bf16[3,96,512]{2,1,0:T(8,128)(2,1)S(1)}, u32[]{:S(2)}, u32[]{:S(2)}) %collective-permute-start.11) | collective-permute-done | bytes 294944 | tf_op jit(solution)/shard_map/ppermute | solution.py:808
  78.2 10.4 %self_forward.1 = (bf16[512,384]{1,0:T(8,128)(2,1)}, bf16[512,384]{1,0:T(8,128)(2,1)}, bf16[512,384]{1,0:T(8,128)(2,1)}, bf16[512,384]{1,0:T(8,128)(2,1)}, f32[5...) custom-call(s32[5]{0:T(128)} %stack.162.scal_ref, ...), custom_call_target="tpu_custom_call" | custom-call | flops 2013265920 | bytes 7864320 | tf_op jit(solution)/shard_map/self_forward/pallas_call | solution.py:129
  104.7 9.3 %collective-permute-done.8.h_other_ref.h_other = bf16[256,768]{1,0:T(8,128)(2,1)S(1)} collective-permute-done((bf16[256,768]{1,0:T(8,128)(2,1)S(1)}, bf16[256,768]{1,0:T(8,128)(2,1)S(1)}, u32[]{:S(2)}, u32[]{:S(2)}) %collective-permute-start.8) | collective-permute-done | bytes 393248 | tf_op jit(solution)/shard_map/ppermute | solution.py:808
  119.0 12.7 %cross_forward.1 = (bf16[512,384]{1,0:T(8,128)(2,1)}, bf16[512,384]{1,0:T(8,128)(2,1)}, f32[512,384]{1,0:T(8,128)}, f32[256,768]{1,0:T(8,128)}, bf16[256,768]{1,0:T(8,128)(2,1)}) custom-call(s32[5]{0:T(128)} %stack.164.scal_ref, bf16[256,768]{1,0:T(8,128)(2,1)} %copy-done.17, bf16[256,768]{1,0:T(8,128)(2,1)} %copy-done.30, ...), custom_call_target="tpu_custom_call" | custom-call | flops 2214592512 | bytes 8650752 | tf_op jit(solution)/shard_map/cross_forward/pallas_call | solution.py:129
  132.1 9.4 %collective-permute-done.9 = bf16[256,768]{1,0:T(8,128)(2,1)S(1)} collective-permute-done((bf16[256,768]{1,0:T(8,128)(2,1)}, bf16[256,768]{1,0:T(8,128)(2,1)S(1)}, u32[]{:S(2)}, u32[]{:S(2)}) %collective-permute-start.9) | collective-permute-done | bytes 393248 | tf_op jit(solution)/shard_map/ppermute | solution.py:808
  154.0 8.5 %mlp_forward.1 = (f32[512,1024]{1,0:T(8,128)}, f32[512,1024]{1,0:T(8,128)}, bf16[512,1024]{1,0:T(8,128)(2,1)}, f32[256,768]{1,0:T(8,128)}, bf16[256,768]{1,0:T(8,128)(2,1)}) custom-call(s32[5]{0:T(128)} %stack.162.scal_ref, bf16[256,768]{1,0:T(8,128)(2,1)} %copy-done.18, bf16[256,768]{1,0:T(8,128)(2,1)} %copy-done.31, ...), custom_call_target="tpu_custom_call" | custom-call | flops 2415919104 | bytes 11927552 | tf_op jit(solution)/shard_map/mlp_forward/pallas_call | solution.py:129
  180.1 7.8 %collective-permute-done.13 = bf16[256,768]{1,0:T(8,128)(2,1)} collective-permute-done((bf16[256,768]{1,0:T(8,128)(2,1)S(1)}, bf16[256,768]{1,0:T(8,128)(2,1)}, u32[]{:S(2)}, u32[]{:S(2)}) %collective-permute-start.13) | collective-permute-done | bytes 393248 | tf_op jit(solution)/shard_map/ppermute | solution.py:808
  189.8 13.4 %head_forward.2 = (bf16[512,8032]{1,0:T(8,128)(2,1)}, f32[512,128]{1,0:T(8,128)}, f32[8,512]{1,0:T(8,128)}) custom-call(bf16[512,768]{1,0:T(8,128)(2,1)} %pad_maximum_fusion.2.rows_ref.near_rows_ref, bf16[768,8032]{1,0:T(8,128)(2,1)} %all-gather.9.cloned.1.call-done.table_ref, s32[512,1]{1,0:T(8,128)} %copy.55.ids_ref), custom_call_target="tpu_custom_call" | custom-call | flops 6316621824 | bytes 21348352 | tf_op jit(solution)/shard_map/head_forward/pallas_call | solution.py:568
  208.2 13.5 %head_forward.3 = (bf16[512,8032]{1,0:T(8,128)(2,1)}, f32[512,128]{1,0:T(8,128)}, f32[8,512]{1,0:T(8,128)}) custom-call(bf16[512,768]{1,0:T(8,128)(2,1)} %copy-done.36, bf16[768,8032]{1,0:T(8,128)(2,1)} %all-gather.9.cloned.1.call-done.table_ref, s32[512,1]{1,0:T(8,128)} %copy.56.ids_ref), custom_call_target="tpu_custom_call" | custom-call | flops 6316621824 | bytes 21348352 | tf_op jit(solution)/shard_map/head_forward/pallas_call | solution.py:568
  237.9 21.7 %table_grad.1 = bf16[768,8032]{1,0:T(8,128)(2,1)} custom-call(bf16[512,768]{1,0:T(8,128)(2,1)} %pad_maximum_fusion.2.rows_ref.near_rows_ref, bf16[512,8032]{1,0:T(8,128)(2,1)} %get-tuple-element.125.near_prob_ref.prob_ref, f32[512,128]{1,0:T(8,128)} %get-tuple-element.131.near_coef_ref.coef_ref, bf16[512,768]{1,0:T(8,128)(2,1)} %copy-done.36, ...), custom_call_target="tpu_custom_call" | custom-call | flops 12633243648 | bytes 30359552 | tf_op jit(solution)/shard_map/table_grad/pallas_call | solution.py:723
  259.9 15.2 %rows_grad.2 = (bf16[256,768]{1,0:T(8,128)(2,1)}, bf16[256,768]{1,0:T(8,128)(2,1)}) custom-call(bf16[768,8032]{1,0:T(8,128)(2,1)} %all-gather.9.cloned.1.call-done.table_ref, bf16[512,8032]{1,0:T(8,128)(2,1)} %get-tuple-element.127.far_prob_ref.prob_ref, f32[512,128]{1,0:T(8,128)} %get-tuple-element.129.far_coef_ref.coef_ref), custom_call_target="tpu_custom_call" | custom-call | flops 6316621824 | bytes 22134784 | tf_op jit(solution)/shard_map/rows_grad/pallas_call | solution.py:689
  277.0 15.1 %rows_grad.3 = (f32[256,768]{1,0:T(8,128)}, bf16[256,768]{1,0:T(8,128)(2,1)}) custom-call(bf16[768,8032]{1,0:T(8,128)(2,1)} %all-gather.9.cloned.1.call-done.table_ref, bf16[512,8032]{1,0:T(8,128)(2,1)} %get-tuple-element.125.near_prob_ref.prob_ref, f32[512,128]{1,0:T(8,128)} %get-tuple-element.131.near_coef_ref.coef_ref), custom_call_target="tpu_custom_call" | custom-call | flops 6316621824 | bytes 22134784 | tf_op jit(solution)/shard_map/rows_grad/pallas_call | solution.py:689
  294.6 11.7 %collective-permute-done.20 = bf16[256,768]{1,0:T(8,128)(2,1)S(1)} collective-permute-done((bf16[256,768]{1,0:T(8,128)(2,1)}, bf16[256,768]{1,0:T(8,128)(2,1)S(1)}, u32[]{:S(2)}, u32[]{:S(2)}) %collective-permute-start.20) | collective-permute-done | bytes 393248 | tf_op jit(solution)/shard_map/ppermute | solution.py:808
  310.8 7.5 %collective-permute-done.23.e_other_ref = bf16[256,768]{1,0:T(8,128)(2,1)S(1)} collective-permute-done((bf16[256,768]{1,0:T(8,128)(2,1)S(1)}, bf16[256,768]{1,0:T(8,128)(2,1)S(1)}, u32[]{:S(2)}, u32[]{:S(2)}) %collective-permute-start.23) | collective-permute-done | bytes 393248 | tf_op jit(solution)/shard_map/ppermute | solution.py:808
  319.1 10.1 %mlp_back.1 = (bf16[512,1024]{1,0:T(8,128)(2,1)}, bf16[512,1024]{1,0:T(8,128)(2,1)}, f32[256,768]{1,0:T(8,128)}, bf16[256,768]{1,0:T(8,128)(2,1)}) custom-call(s32[5]{0:T(128)} %stack.162.scal_ref, bf16[256,768]{1,0:T(8,128)(2,1)} %copy-done, bf16[256,768]{1,0:T(8,128)(2,1)} %copy-done.13, bf16[3,768,1024]{2,1,0:T(8,128)(2,1)} %all-gather.7.cloned.1.call-done.w_ref, ...), custom_call_target="tpu_custom_call" | custom-call | flops 2415919104 | bytes 12976128 | tf_op jit(solution)/shard_map/mlp_back/pallas_call | solution.py:129
  329.7 7.6 %mlp_grads.1 = bf16[3,768,1024]{2,1,0:T(8,128)(2,1)} custom-call(s32[5]{0:T(128)} %stack.162.scal_ref, bf16[256,768]{1,0:T(8,128)(2,1)} %copy-done.18, bf16[256,768]{1,0:T(8,128)(2,1)} %copy-done.31, bf16[256,768]{1,0:T(8,128)(2,1)} %copy-done, bf16[256,768]{1,0:T(8,128)(2,1)} %copy-done.13, bf16[512,1024]{1,0:T(8,128)(2,1)} %get-tuple-element.140.d_gate_ref, ...), custom_call_target="tpu_custom_call" | custom-call | flops 2415919104 | bytes 9437184 | tf_op jit(solution)/shard_map/mlp_grads/pallas_call | solution.py:129
  350.5 16.5 %cross_back.1 = (bf16[512,384]{1,0:T(8,128)(2,1)}, bf16[1024,384]{1,0:T(8,128)(2,1)}, bf16[1024,384]{1,0:T(8,128)(2,1)}, f32[256,768]{1,0:T(8,128)}, bf16[256,768]{1,0:T(8,128)(2,1)}) custom-call(s32[5]{0:T(128)} %stack.164.scal_ref, bf16[256,768]{1,0:T(8,128)(2,1)} %copy-done.14, bf16[256,768]{1,0:T(8,128)(2,1)} %copy-done.32, ...), custom_call_target="tpu_custom_call" | custom-call | flops 4630511616 | bytes 10223616 | tf_op jit(solution)/shard_map/cross_back/pallas_call | solution.py:129
  368.7 8.5 %cross_grads.1.rest_ref = bf16[8,768,384]{2,1,0:T(8,128)(2,1)} custom-call(s32[5]{0:T(128)} %stack.162.scal_ref, bf16[256,768]{1,0:T(8,128)(2,1)} %copy-done.17, bf16[256,768]{1,0:T(8,128)(2,1)} %copy-done.30, bf16[256,768]{1,0:T(8,128)(2,1)} %copy-done.14, bf16[256,768]{1,0:T(8,128)(2,1)} %copy-done.32, bf16[256,768]{1,0:T(8,128)(2,1)} %copy-done.16, ...), custom_call_target="tpu_custom_call" | custom-call | flops 1811939328 | bytes 6291456 | tf_op jit(solution)/shard_map/cross_grads/pallas_call | solution.py:129
  391.5 14.0 %self_back.1 = (bf16[512,384]{1,0:T(8,128)(2,1)}, bf16[512,384]{1,0:T(8,128)(2,1)}, bf16[512,384]{1,0:T(8,128)(2,1)}, f32[256,768]{1,0:T(8,128)}, bf16[256,768]{1,0:T(8,128)(2,1)}, /*index=5*/f32[8,768]{1,0:T(8,128)}) custom-call(s32[5]{0:T(128)} %stack.162.scal_ref, bf16[256,768]{1,0:T(8,128)(2,1)} %copy-done.15, bf16[256,768]{1,0:T(8,128)(2,1)} %copy-done.33, ...), custom_call_target="tpu_custom_call" | custom-call | flops 3221225472 | bytes 10223616 | tf_op jit(solution)/shard_map/self_back/pallas_call | solution.py:129
  438.7 11.6 %collective-permute-start.30 = (bf16[3,96,512]{2,1,0:T(8,128)(2,1)S(1)}, bf16[3,96,512]{2,1,0:T(8,128)(2,1)S(1)}, u32[]{:S(2)}, u32[]{:S(2)}) collective-permute-start(bf16[3,96,512]{2,1,0:T(8,128)(2,1)S(1)} %slice.223), channel_id=1, source_target_pairs={{0,2},{1,3},{2,0},{3,1},{4,6},{5,7},{6,4},{7,5},{8,10},{9,11},{10,... | collective-permute-start | bytes 884744 | tf_op jit(solution)/shard_map/ppermute | solution.py:808
  452.3 9.0 %collective-permute-done.28 = bf16[256,768]{1,0:T(8,128)(2,1)S(1)} collective-permute-done((bf16[256,768]{1,0:T(8,128)(2,1)S(1)}, bf16[256,768]{1,0:T(8,128)(2,1)S(1)}, u32[]{:S(2)}, u32[]{:S(2)}) %collective-permute-start.28) | collective-permute-done | bytes 393248 | tf_op jit(solution)/shard_map/ppermute | solution.py:808
  474.9 11.8 %collective-permute-done.38 = bf16[4,96,384]{2,1,0:T(8,128)(2,1)S(1)} collective-permute-done((bf16[4,96,384]{2,1,0:T(8,128)(2,1)S(1)}, bf16[4,96,384]{2,1,0:T(8,128)(2,1)S(1)}, u32[]{:S(2)}, u32[]{:S(2)}) %collective-permute-start.38) | collective-permute-done | bytes 294944 | tf_op jit(solution)/shard_map/ppermute | solution.py:808
  (324 shorter events, 194.1 us)
Async XLA Ops:
  7.2 68.2 %all-gather.5.cloned.1.call-start = ((), (), s32[]{:S(2)}) async-start(), calls=%async_computation.3 | async-start | bytes 5308416 | tf_op jit(solution)/shard_map/all_gather | solution.py:821
  9.2 20.3 %collective-permute-start = (bf16[4,96,384]{2,1,0:T(8,128)(2,1)}, bf16[4,96,384]{2,1,0:T(8,128)(2,1)S(1)}, u32[]{:S(2)}, u32[]{:S(2)}) collective-permute-start(bf16[4,96,384]{2,1,0:T(8,128)(2,1)} %pack_pairs.1), channel_id=1, source_target_pairs={{0,2},{1,3},{2,0},{3,1},{4,6},{5,7},{6,4},{7,5},{8,10},{9,11},{10,... | collective-permute-start | bytes 884744 | tf_op jit(solution)/shard_map/ppermute | solution.py:808
  32.3 81.7 %all-gather.7.cloned.1.call-start = ((), (), s32[]{:S(2)}) async-start(), calls=%async_computation.4 | async-start | bytes 5308416 | tf_op jit(solution)/shard_map/all_gather | solution.py:821
  33.4 19.2 %collective-permute-start.1 = (bf16[128,768]{1,0:T(8,128)(2,1)S(1)}, bf16[128,768]{1,0:T(8,128)(2,1)S(1)}, u32[]{:S(2)}, u32[]{:S(2)}) collective-permute-start(bf16[128,768]{1,0:T(8,128)(2,1)S(1)} %get-tuple-element.97), channel_id=1, source_target_pairs={{0,2},{1,3},{2,0},{3,1},{4,6},{5,7},{6,4},{7,5},{8,10},{9,11},{10,... | collective-permute-start | bytes 589832 | tf_op jit(solution)/shard_map/ppermute | solution.py:808
  33.8 33.6 %collective-permute-start.11 = (bf16[3,96,512]{2,1,0:T(8,128)(2,1)S(1)}, bf16[3,96,512]{2,1,0:T(8,128)(2,1)S(1)}, u32[]{:S(2)}, u32[]{:S(2)}) collective-permute-start(bf16[3,96,512]{2,1,0:T(8,128)(2,1)S(1)} %pad_maximum_fusion.7), channel_id=1, source_target_pairs={{0,2},{1,3},{2,0},{3,1},{4,6},{5,7},{6,4},{7,5},{8,10},{9,11},{10,... | collective-permute-start | bytes 884744 | tf_op jit(solution)/shard_map/ppermute | solution.py:808
  52.7 22.7 %collective-permute-start.4 = (bf16[256,768]{1,0:T(8,128)(2,1)S(1)}, bf16[256,768]{1,0:T(8,128)(2,1)S(1)}, u32[]{:S(2)}, u32[]{:S(2)}) collective-permute-start(bf16[256,768]{1,0:T(8,128)(2,1)S(1)} %get-tuple-element.208), channel_id=1, source_target_pairs={{0,2},{1,3},{2,0},{3,1},{4,6},{5,7},{6,4},{7,5},{8,10},{9,11},{10,... | collective-permute-start | bytes 1179656 | tf_op jit(solution)/shard_map/ppermute | solution.py:808
  52.8 15.6 %collective-permute-start.2 = (bf16[128,768]{1,0:T(8,128)(2,1)S(1)}, bf16[128,768]{1,0:T(8,128)(2,1)S(1)}, u32[]{:S(2)}, u32[]{:S(2)}) collective-permute-start(bf16[128,768]{1,0:T(8,128)(2,1)S(1)} %get-tuple-element.225.refs_0_.refs_7_), channel_id=1, source_target_pairs={{0,1},{1,0},{2,3},{3,2},{4,5},{5,4},{6,7},{7,6},{8,9},{9,8},{10,11... | collective-permute-start | bytes 589832 | tf_op jit(solution)/shard_map/ppermute | solution.py:808
  54.0 21.4 %collective-permute-start.3 = (bf16[128,768]{1,0:T(8,128)(2,1)S(1)}, bf16[128,768]{1,0:T(8,128)(2,1)S(1)}, u32[]{:S(2)}, u32[]{:S(2)}) collective-permute-start(bf16[128,768]{1,0:T(8,128)(2,1)S(1)} %collective-permute-done.1.refs_1_.refs_8_), channel_id=1, source_target_pairs={{0,1},{1,0},{2,3},{3,2},{4,5},{5,4},{6,7},{7,6},{8,9},{9,8},{10,11... | collective-permute-start | bytes 589832 | tf_op jit(solution)/shard_map/ppermute | solution.py:808
  75.4 114.4 %all-gather.9.cloned.1.call-start = ((), (), s32[]{:S(2)}) async-start(), calls=%async_computation.5 | async-start | bytes 13934592 | tf_op jit(solution)/shard_map/all_gather | solution.py:821
  75.6 20.5 %collective-permute-start.6 = (bf16[256,768]{1,0:T(8,128)(2,1)S(1)}, bf16[256,768]{1,0:T(8,128)(2,1)S(1)}, u32[]{:S(2)}, u32[]{:S(2)}) collective-permute-start(bf16[256,768]{1,0:T(8,128)(2,1)S(1)} %collective-permute-done.4.refs_1_), channel_id=1, source_target_pairs={{0,1},{1,0},{2,3},{3,2},{4,5},{5,4},{6,7},{7,6},{8,9},{9,8},{10,11... | collective-permute-start | bytes 1179656 | tf_op jit(solution)/shard_map/ppermute | solution.py:808
  114.0 235.8 %reduce-scatter.4.cloned.1.call-start = ((), (), s32[]{:S(2)}) async-start(), calls=%async_computation.6 | async-start | bytes 13934592 | tf_op jit(solution)/shard_map/reduce_scatter | solution.py:825
  177.4 28.8 %collective-permute-start.15 = (bf16[256,768]{1,0:T(8,128)(2,1)S(1)}, bf16[256,768]{1,0:T(8,128)(2,1)S(1)}, u32[]{:S(2)}, u32[]{:S(2)}) collective-permute-start(bf16[256,768]{1,0:T(8,128)(2,1)S(1)} %get-tuple-element.205), channel_id=1, source_target_pairs={{0,2},{1,3},{2,0},{3,1},{4,6},{5,7},{6,4},{7,5},{8,10},{9,11},{10,... | collective-permute-start | bytes 1179656 | tf_op jit(solution)/shard_map/ppermute | solution.py:808
  180.0 26.3 %collective-permute-start.16 = (bf16[256,768]{1,0:T(8,128)(2,1)S(1)}, bf16[256,768]{1,0:T(8,128)(2,1)}, u32[]{:S(2)}, u32[]{:S(2)}) collective-permute-start(bf16[256,768]{1,0:T(8,128)(2,1)S(1)} %get-tuple-element.205), channel_id=1, source_target_pairs={{0,3},{1,2},{2,1},{3,0},{4,7},{5,6},{6,5},{7,4},{8,11},{9,10},{10,... | collective-permute-start | bytes 1179656 | tf_op jit(solution)/shard_map/ppermute | solution.py:808
  259.6 148.6 %reduce-scatter.6.cloned.1.call-start = ((), (), s32[]{:S(2)}) async-start(), calls=%async_computation.7 | async-start | bytes 5308416 | tf_op jit(solution)/shard_map/reduce_scatter | solution.py:825
  259.7 17.3 %collective-permute-start.14 = (bf16[128,768]{1,0:T(8,128)(2,1)S(1)}, bf16[128,768]{1,0:T(8,128)(2,1)S(1)}, u32[]{:S(2)}, u32[]{:S(2)}) collective-permute-start(bf16[128,768]{1,0:T(8,128)(2,1)S(1)} %slice.186), channel_id=1, source_target_pairs={{0,2},{1,3},{2,0},{3,1},{4,6},{5,7},{6,4},{7,5},{8,10},{9,11},{10,... | collective-permute-start | bytes 589832 | tf_op jit(solution)/shard_map/ppermute | solution.py:808
  275.1 17.1 %collective-permute-start.21 = (bf16[256,768]{1,0:T(8,128)(2,1)}, bf16[256,768]{1,0:T(8,128)(2,1)S(1)}, u32[]{:S(2)}, u32[]{:S(2)}) collective-permute-start(bf16[256,768]{1,0:T(8,128)(2,1)} %get-tuple-element.134), channel_id=1, source_target_pairs={{0,1},{1,0},{2,3},{3,2},{4,5},{5,4},{6,7},{7,6},{8,9},{9,8},{10,11... | collective-permute-start | bytes 1179656 | tf_op jit(solution)/shard_map/ppermute | solution.py:808
  292.3 15.9 %collective-permute-start.22 = (bf16[256,768]{1,0:T(8,128)(2,1)S(1)}, bf16[256,768]{1,0:T(8,128)(2,1)S(1)}, u32[]{:S(2)}, u32[]{:S(2)}) collective-permute-start(bf16[256,768]{1,0:T(8,128)(2,1)S(1)} %add_convert_fusion), channel_id=1, source_target_pairs={{0,2},{1,3},{2,0},{3,1},{4,6},{5,7},{6,4},{7,5},{8,10},{9,11},{10,... | collective-permute-start | bytes 1179656 | tf_op jit(solution)/shard_map/ppermute | solution.py:808
  349.8 119.6 %reduce-scatter.8.cloned.1.call-start = ((), (), s32[]{:S(2)}) async-start(), calls=%async_computation.8 | async-start | bytes 5308416 | tf_op jit(solution)/shard_map/reduce_scatter | solution.py:825
  390.8 17.4 %collective-permute-start.29 = (bf16[512,768]{1,0:T(8,128)(2,1)S(1)}, bf16[512,768]{1,0:T(8,128)(2,1)}, u32[]{:S(2)}, u32[]{:S(2)}) collective-permute-start(bf16[512,768]{1,0:T(8,128)(2,1)S(1)} %slice.296), channel_id=1, source_target_pairs={{0,1},{1,0},{2,3},{3,2},{4,5},{5,4},{6,7},{7,6},{8,9},{9,8},{10,11... | collective-permute-start | bytes 2359304 | tf_op jit(solution)/shard_map/ppermute | solution.py:808
  427.7 22.6 %collective-permute-start.31 = (bf16[256,768]{1,0:T(8,128)(2,1)S(1)}, bf16[256,768]{1,0:T(8,128)(2,1)S(1)}, u32[]{:S(2)}, u32[]{:S(2)}) collective-permute-start(bf16[256,768]{1,0:T(8,128)(2,1)S(1)} %slice.297), channel_id=1, source_target_pairs={{0,2},{1,3},{2,0},{3,1},{4,6},{5,7},{6,4},{7,5},{8,10},{9,11},{10,... | collective-permute-start | bytes 1179656 | tf_op jit(solution)/shard_map/ppermute | solution.py:808
  432.9 17.4 %collective-permute-start.36 = (f32[4,768]{1,0:T(4,128)S(1)}, f32[4,768]{1,0:T(4,128)S(1)}, u32[]{:S(2)}, u32[]{:S(2)}) collective-permute-start(f32[4,768]{1,0:T(4,128)S(1)} %add.228), channel_id=1, source_target_pairs={{0,16},{4,20},{8,24},{12,28},{16,0},{20,4},{24,8},{28,12},{1,17},{... | collective-permute-start | bytes 36872 | tf_op jit(solution)/shard_map/ppermute | solution.py:815
  436.8 24.5 %collective-permute-start.28 = (bf16[256,768]{1,0:T(8,128)(2,1)S(1)}, bf16[256,768]{1,0:T(8,128)(2,1)S(1)}, u32[]{:S(2)}, u32[]{:S(2)}) collective-permute-start(bf16[256,768]{1,0:T(8,128)(2,1)S(1)} %copy-done.60), channel_id=1, source_target_pairs={{0,1},{1,0},{2,3},{3,2},{4,5},{5,4},{6,7},{7,6},{8,9},{9,8},{10,11... | collective-permute-start | bytes 1179656 | tf_op jit(solution)/shard_map/ppermute | solution.py:808
  438.7 22.6 %collective-permute-start.30 = (bf16[3,96,512]{2,1,0:T(8,128)(2,1)S(1)}, bf16[3,96,512]{2,1,0:T(8,128)(2,1)S(1)}, u32[]{:S(2)}, u32[]{:S(2)}) collective-permute-start(bf16[3,96,512]{2,1,0:T(8,128)(2,1)S(1)} %slice.223), channel_id=1, source_target_pairs={{0,2},{1,3},{2,0},{3,1},{4,6},{5,7},{6,4},{7,5},{8,10},{9,11},{10,... | collective-permute-start | bytes 884744 | tf_op jit(solution)/shard_map/ppermute | solution.py:808
  470.7 16.0 %collective-permute-start.38 = (bf16[4,96,384]{2,1,0:T(8,128)(2,1)S(1)}, bf16[4,96,384]{2,1,0:T(8,128)(2,1)S(1)}, u32[]{:S(2)}, u32[]{:S(2)}) collective-permute-start(bf16[4,96,384]{2,1,0:T(8,128)(2,1)S(1)} %pad_maximum_fusion.8), channel_id=1, source_target_pairs={{0,2},{1,3},{2,0},{3,1},{4,6},{5,7},{6,4},{7,5},{8,10},{9,11},{10,... | collective-permute-start | bytes 884744 | tf_op jit(solution)/shard_map/ppermute | solution.py:808
  (86 other events, 999.4 us)
Sparse Core Ops, SparseCore 0:
  32.4 37.4 all-gather.4
  75.6 36.8 all-gather.6
  114.3 71.2 all-gather.8
  259.7 89.7 reduce-scatter.3
  353.2 53.8 reduce-scatter.5
  415.3 53.9 reduce-scatter.7

commit v4 on v3

--- a/solution.py
+++ b/solution.py
@@ -13,17 +13,17 @@
 MASKED_OUT = -1000000000.0
 GELU_SCALE = 0.7978845608028654
 VMEM_LIMIT = 56 * 1024 * 1024
+HEAD_LIMIT = 56 * 1024 * 1024
+GRAD_BLOCK = 512
 VOCAB_BLOCK = 2048
-HIDDEN_BLOCK = 256
+HIDDEN_BLOCK = 512
 LOG2_E = 1.4426950408889634
 BF16 = jnp.bfloat16
 F32 = jnp.float32
 
 
-def params():
-    return pltpu.CompilerParams(
-        dimension_semantics=("arbitrary",), vmem_limit_bytes=VMEM_LIMIT
-    )
+def params(limit=VMEM_LIMIT):
+    return pltpu.CompilerParams(dimension_semantics=("arbitrary",), vmem_limit_bytes=limit)
 
 
 def mm(a, b):
@@ -526,7 +526,7 @@
     return jnp.where(column < vocab, 0.0, MASKED_OUT)
 
 
-def head_kernel(vocab, scale, rows_ref, table_ref, ids_ref, prob_ref, stat_ref, turned_ref):
+def head_kernel(vocab, scale, own_ref, other_ref, table_ref, ids_ref, prob_ref, stat_ref, turned_ref):
     step = pl.program_id(0)
     block = table_ref.shape[1]
     table = table_ref[...]
@@ -534,9 +534,11 @@
     bias = column_bias(vocab, step, block)
     column = lax.broadcasted_iota(jnp.int32, (1, block), 1)
     lane = lax.broadcasted_iota(jnp.int32, (chunk, LANES), 1)
-    for start in range(0, rows_ref.shape[0], chunk):
+    half = own_ref.shape[0]
+    for start in range(0, 2 * half, chunk):
         part = pl.ds(start, chunk)
-        products = mm(rows_ref[part, :], table) + bias
+        rows_ref = own_ref if start < half else other_ref
+        products = mm(rows_ref[pl.ds(start % half, chunk), :], table) + bias
         highest = jnp.max(products, -1, keepdims=True)
         raised = jnp.exp2((products - highest) * (scale * LOG2_E))
         prob_ref[part, :] = raised.astype(BF16)
@@ -562,35 +564,36 @@
 
 
 def head_forward(rows, table, ids, scale):
-    count, width = rows.shape
-    vocab = table.shape[1]
+    half, width = rows[0].shape
+    count, vocab = 2 * half, table.shape[1]
     steps = pl.cdiv(vocab, VOCAB_BLOCK)
     return pl.pallas_call(
         functools.partial(head_kernel, vocab, scale),
         out_shape=(
-            jax.ShapeDtypeStruct((count, vocab), BF16),
+            jax.ShapeDtypeStruct((count, steps * VOCAB_BLOCK), BF16),
             jax.ShapeDtypeStruct((count, LANES), F32),
             jax.ShapeDtypeStruct((TURNED, count), F32),
         ),
         grid=(steps,),
         in_specs=[
-            pl.BlockSpec((count, width), lambda j: (0, 0)),
+            whole((half, width)),
+            whole((half, width)),
             pl.BlockSpec((width, VOCAB_BLOCK), lambda j: (0, j)),
             pl.BlockSpec((count, 1), lambda j: (0, 0)),
         ],
         out_specs=(
-            pl.BlockSpec((count, VOCAB_BLOCK), lambda j: (0, j)),
+            columns(count, VOCAB_BLOCK),
             pl.BlockSpec((count, LANES), lambda j: (0, 0)),
             pl.BlockSpec((TURNED, count), lambda j: (0, 0)),
         ),
-        compiler_params=params(),
+        compiler_params=params(HEAD_LIMIT),
         cost_estimate=pl.CostEstimate(
             flops=2 * count * width * vocab,
             transcendentals=count * vocab,
             bytes_accessed=2 * (count + width) * vocab + 2 * count * width,
         ),
         name="head_forward",
-    )(rows, table, ids)
+    )(*rows, table, ids)
 
 
 def combine_kernel(near_stat_ref, far_stat_ref, *refs):
@@ -630,7 +633,7 @@
             sized((half, LANES), F32),
             sized((TURNED, 2 * half), F32),
         ),
-        compiler_params=pltpu.CompilerParams(vmem_limit_bytes=VMEM_LIMIT),
+        compiler_params=pltpu.CompilerParams(vmem_limit_bytes=HEAD_LIMIT),
         cost_estimate=pl.CostEstimate(
             flops=20 * half * LANES,
             transcendentals=2 * half * LANES,
@@ -640,24 +643,19 @@
     )(near_stats, far_stats, *shares, info)
 
 
-def logit_grads(vocab, step, part, prob_ref, coef_ref):
-    block = prob_ref.shape[1]
-    coef = coef_ref[part, :]
+def row_coefs(step, coef_ref):
+    coef = coef_ref[...]
     lane = lax.broadcasted_iota(jnp.int32, coef.shape, 1)
     factor = jnp.sum(jnp.where(lane == step, coef, 0.0), -1, keepdims=True)
-    weight = coef[:, WEIGHT_LANE : WEIGHT_LANE + 1]
-    target = coef[:, ID_LANE : ID_LANE + 1].astype(jnp.int32) - step * block
-    column = lax.broadcasted_iota(jnp.int32, (1, block), 1)
-    inside = column < vocab - step * block
-    prob = prob_ref[part, :].astype(F32)
-    grads = prob * factor - jnp.where(column == target, weight, 0.0)
-    return jnp.where(inside, grads, 0.0).astype(BF16)
-
-
-def table_block(vocab, step, table_ref):
-    table = table_ref[...]
-    column = lax.broadcasted_iota(jnp.int32, (1, table.shape[1]), 1) + step * table.shape[1]
-    return jnp.where(column < vocab, table, jnp.zeros_like(table))
+    target = coef[:, ID_LANE : ID_LANE + 1].astype(jnp.int32)
+    return factor, coef[:, WEIGHT_LANE : WEIGHT_LANE + 1], target - step * VOCAB_BLOCK
+
+
+def logit_grads(start, prob_ref, coefs):
+    factor, weight, target = coefs
+    column = lax.broadcasted_iota(jnp.int32, (1, GRAD_BLOCK), 1) + start
+    prob = prob_ref[:, start : start + GRAD_BLOCK].astype(F32)
+    return (prob * factor - jnp.where(column == target, weight, 0.0)).astype(BF16)
 
 
 def add_up(step, out_ref, terms):
@@ -672,8 +670,14 @@
 
 def rows_grad_kernel(vocab, table_ref, prob_ref, coef_ref, first_ref, second_ref, total):
     step = pl.program_id(0)
-    grads = logit_grads(vocab, step, slice(None), prob_ref, coef_ref)
-    add_up(step, total, mm_nt(grads, table_block(vocab, step, table_ref)))
+    coefs = row_coefs(step, coef_ref)
+    terms = 0.0
+    for start in range(0, VOCAB_BLOCK, GRAD_BLOCK):
+        table = table_ref[:, start : start + GRAD_BLOCK]
+        column = lax.broadcasted_iota(jnp.int32, (1, GRAD_BLOCK), 1) + start
+        table = jnp.where(column < vocab - step * VOCAB_BLOCK, table, jnp.zeros_like(table))
+        terms += mm_nt(logit_grads(start, prob_ref, coefs), table)
+    add_up(step, total, terms)
 
     @pl.when(step == pl.num_programs(0) - 1)
     def _():
@@ -683,8 +687,8 @@
 
 
 def rows_grad(table, prob, coef, dtype):
-    width = table.shape[0]
-    count, vocab = prob.shape
+    width, vocab = table.shape
+    count = prob.shape[0]
     half = whole((count // 2, width))
     return pl.pallas_call(
         functools.partial(rows_grad_kernel, vocab),
@@ -697,7 +701,7 @@
         ],
         out_specs=(half, half),
         scratch_shapes=[pltpu.VMEM((count, width), F32)],
-        compiler_params=params(),
+        compiler_params=params(HEAD_LIMIT),
         cost_estimate=pl.CostEstimate(
             flops=2 * count * width * vocab,
             transcendentals=0,
@@ -708,25 +712,32 @@
 
 
 def table_grad_kernel(
-    vocab, near_rows_ref, near_prob_ref, near_coef_ref, far_rows_ref, far_prob_ref, far_coef_ref, out_ref
+    near_own, near_other, near_prob_ref, near_coef_ref,
+    far_own, far_other, far_prob_ref, far_coef_ref, out_ref,
 ):
     step = pl.program_id(0)
-    near = logit_grads(vocab, step, slice(None), near_prob_ref, near_coef_ref)
-    far = logit_grads(vocab, step, slice(None), far_prob_ref, far_coef_ref)
-    out_ref[...] = (mm_tn(near_rows_ref[...], near) + mm_tn(far_rows_ref[...], far)).astype(BF16)
-
-
-def table_grad(near, far):
-    count, width = near[0].shape
-    vocab = near[1].shape[1]
-    specs = [whole((count, width)), columns(count, VOCAB_BLOCK), whole((count, LANES))]
+    near_coefs, far_coefs = row_coefs(step, near_coef_ref), row_coefs(step, far_coef_ref)
+    for start in range(0, VOCAB_BLOCK, GRAD_BLOCK):
+        near = logit_grads(start, near_prob_ref, near_coefs)
+        far = logit_grads(start, far_prob_ref, far_coefs)
+        half = near_own.shape[0]
+        terms = mm_tn(near_own[...], near[:half]) + mm_tn(near_other[...], near[half:])
+        terms += mm_tn(far_own[...], far[:half]) + mm_tn(far_other[...], far[half:])
+        out_ref[:, start : start + GRAD_BLOCK] = terms.astype(BF16)
+
+
+def table_grad(vocab, near, far):
+    half, width = near[0].shape
+    count = 2 * half
+    specs = [whole((half, width))] * 2
+    specs += [columns(count, VOCAB_BLOCK), whole((count, LANES))]
     return pl.pallas_call(
-        functools.partial(table_grad_kernel, vocab),
+        table_grad_kernel,
         out_shape=sized((width, vocab), BF16),
         grid=(pl.cdiv(vocab, VOCAB_BLOCK),),
         in_specs=specs * 2,
         out_specs=columns(width, VOCAB_BLOCK),
-        compiler_params=params(),
+        compiler_params=params(HEAD_LIMIT),
         cost_estimate=pl.CostEstimate(
             flops=4 * count * width * vocab,
             transcendentals=0,
@@ -878,11 +889,6 @@
     def of_other(values):
         return jnp.where(lower, values[1], values[0])
 
-    def pair_rows(values):
-        mine, other = of_pair(values), of_other(values)
-        second = swap(other, 2)
-        return [mine, second, swap(mine, 1), swap(second, 1)]
-
     def placed(own, received):
         far = received.astype(own.dtype)
         return jnp.stack([jnp.where(lower, own, far), jnp.where(lower, far, own)])
@@ -935,7 +941,10 @@
     second = swap(after(of_other(hidden_in), moved), 2)
     pieces = [own_rows_in, second, swap(own_rows_in, 1), swap(second, 1)]
     mlp_part = both_slices(after(jnp.stack([mlp_gate, mlp_up, mlp_down]), moved))
-    memory_pieces = pair_rows(after(memory, second))
+    memory_own = of_pair(memory)
+    memory_second = swap(after(of_other(memory), second), 2)
+    memory_pieces = [memory_own, memory_second, swap(after(memory_own, pieces[3]), 1)]
+    memory_pieces += [swap(memory_second, 1)]
 
     residual = jnp.concatenate(pieces[:2], axis=0).astype(F32)
     w_mlp = gather_batch(after(mlp_part, (w_both, pieces, memory_pieces[1])), 1)
@@ -969,27 +978,27 @@
 
     normed_four, inverse_four = norm_rows(residual_three, gain_exit)
     own_four = normed_four.astype(BF16)
-    near_four = jnp.concatenate([own_four, swap(own_four, 1)], axis=0)
+    near_four = (own_four, swap(own_four, 1))
     far_four = (swap(own_four, 2), swap(own_four, 3))
     near_prob, near_stats, near_turned = head_forward(
         near_four, table, near_ids, logit_scale
     )
-    far_four = jnp.concatenate(after(far_four, near_turned), axis=0)
+    far_four = after(far_four, near_turned)
     far_prob, far_stats, far_turned = head_forward(
         far_four, table, far_ids, logit_scale
     )
     mine = jnp.concatenate([near_turned, far_turned], axis=1)
-    finished = after(finished, near_turned)
+    shares = [mine] + [swap(mine, step) for step in (1, 2, 3)]
+    near_coef, far_coef, losses = combine(near_stats, far_stats, shares, info)
+    finished = after(finished, near_coef)
     finished_far = swap(finished[block:], 2)
     block_out = placed(finished[:block], finished_far)
-    shares = [mine] + [swap(mine, step) for step in (1, 2, 3)]
-    near_coef, far_coef, losses = combine(near_stats, far_stats, shares, info)
     half_sums = jnp.sum(losses[0].reshape(2, half_rows), -1)
     pair_sums = jnp.where(lower, half_sums, half_sums[::-1])
     pair_loss = pair_sums / tgt_len.astype(F32)
 
     table_terms = table_grad(
-        (near_four, near_prob, near_coef), (far_four, far_prob, far_coef)
+        vocab, (*near_four, near_prob, near_coef), (*far_four, far_prob, far_coef)
     )
     embed_sum = scatter_batch(table_terms, 0)
     far_two, far_three = rows_grad(table, far_prob, after(far_coef, table_terms), BF16)

time: 501 us -> 498 us (level)
  waiting for transfers between devices: 157 us -> 164 us
    ppermute x34, waiting for transfers between devices: 150 us -> 156 us  [swap(): return lax.ppermute(values, 'mp', [(i, i ^ step) for i in range(4)])]
  transfers between devices with their start and end apart: 45 -> 45, of which waited for: 25 -> 28; matrix products, arithmetic and copies ran while one was open for 12% -> 11% of each run, Pallas kernels for 27% -> 26%
where the time goes in v4:
time: 498 us; the launch traced here: 492 us
  Pallas kernels  176 us (35%)
  waiting for transfers between devices  164 us (33%)
  starting transfers between devices  62.7 us (13%)
  other arithmetic  29.5 us (6%)
  local copies, waits for them, and re-layouts  22.2 us (4%)
  between operations  17.8 us (4%)
  matrix products  10.4 us (2%)
  blocking collectives  8.9 us (2%)
    ppermute x34, waiting for transfers between devices, swap(): return lax.ppermute(values, 'mp', [(i, i ^ step) for i in range(4)])  156 us
    pallas_call x8, Pallas kernels, sublayer(): pl.pallas_call(kernel, out_shape=outs, grid_spec=pltpu.PrefetchScalarGrid...  86.4 us
    ppermute x34, starting transfers between devices, swap(): return lax.ppermute(values, 'mp', [(i, i ^ step) for i in range(4)])  56.9 us
    pallas_call x2, Pallas kernels, rows_grad(): pl.pallas_call(functools.partial(rows_grad_kernel, vocab), out_shape=(siz...  28.1 us
    pallas_call x2, Pallas kernels, head_forward(): pl.pallas_call(functools.partial(head_kernel, vocab, scale), out_shape=(j...  26.8 us
    pallas_call x1, Pallas kernels, table_grad(): pl.pallas_call(table_grad_kernel, out_shape=sized((width, vocab), BF16),...  21.6 us
  transfers between devices with their start and end apart: 45, of which 28 were waited for; matrix products, arithmetic and copies ran while one was open for 11% of the time, Pallas kernels for 26%

profile of v4, /device:TPU:0, one launch (start us, length us, event | category | flops | bytes accessed | tf_op | source)
XLA Modules:
  0.0 491.6 jit_solution(245129284807301410)
XLA Ops:
  20.3 8.9 %all-gather = bf16[8,96,4]{1,2,0:T(4,128)(2,1)S(1)} all-gather(bf16[1,96,4]{1,2,0:T(4,128)(2,1)S(1)} %maximum_bitcast_fusion), channel_id=1, replica_groups=mesh['batch'=8,'mp'=4] {'batch'}, dimensions={0}, use_global_device_ids=true | all-gather | bytes 6912 | tf_op jit(solution)/shard_map/all_gather | solution.py:929
  36.4 16.2 %collective-permute-done.1.refs_1_.refs_8_ = bf16[128,768]{1,0:T(8,128)(2,1)S(1)} collective-permute-done((bf16[128,768]{1,0:T(8,128)(2,1)S(1)}, bf16[128,768]{1,0:T(8,128)(2,1)S(1)}, u32[]{:S(2)}, u32[]{:S(2)}) %collective-permute-start.1) | collective-permute-done | bytes 196640 | tf_op jit(solution)/shard_map/ppermute | solution.py:819
  54.6 12.8 %collective-permute-done.11 = bf16[3,96,512]{2,1,0:T(8,128)(2,1)S(1)} collective-permute-done((bf16[3,96,512]{2,1,0:T(8,128)(2,1)S(1)}, bf16[3,96,512]{2,1,0:T(8,128)(2,1)S(1)}, u32[]{:S(2)}, u32[]{:S(2)}) %collective-permute-start.11) | collective-permute-done | bytes 294944 | tf_op jit(solution)/shard_map/ppermute | solution.py:819
  78.1 10.4 %self_forward.1 = (bf16[512,384]{1,0:T(8,128)(2,1)}, bf16[512,384]{1,0:T(8,128)(2,1)}, bf16[512,384]{1,0:T(8,128)(2,1)}, bf16[512,384]{1,0:T(8,128)(2,1)}, f32[5...) custom-call(s32[5]{0:T(128)} %stack.162.scal_ref, ...), custom_call_target="tpu_custom_call" | custom-call | flops 2013265920 | bytes 7864320 | tf_op jit(solution)/shard_map/self_forward/pallas_call | solution.py:129
  104.6 9.3 %collective-permute-done.8.h_other_ref.h_other = bf16[256,768]{1,0:T(8,128)(2,1)S(1)} collective-permute-done((bf16[256,768]{1,0:T(8,128)(2,1)S(1)}, bf16[256,768]{1,0:T(8,128)(2,1)S(1)}, u32[]{:S(2)}, u32[]{:S(2)}) %collective-permute-start.8) | collective-permute-done | bytes 393248 | tf_op jit(solution)/shard_map/ppermute | solution.py:819
  118.8 12.7 %cross_forward.1 = (bf16[512,384]{1,0:T(8,128)(2,1)}, bf16[512,384]{1,0:T(8,128)(2,1)}, f32[512,384]{1,0:T(8,128)}, f32[256,768]{1,0:T(8,128)}, bf16[256,768]{1,0:T(8,128)(2,1)}) custom-call(s32[5]{0:T(128)} %stack.164.scal_ref, bf16[256,768]{1,0:T(8,128)(2,1)} %copy-done.17, bf16[256,768]{1,0:T(8,128)(2,1)} %copy-done.30, ...), custom_call_target="tpu_custom_call" | custom-call | flops 2214592512 | bytes 8650752 | tf_op jit(solution)/shard_map/cross_forward/pallas_call | solution.py:129
  132.0 9.4 %collective-permute-done.9 = bf16[256,768]{1,0:T(8,128)(2,1)S(1)} collective-permute-done((bf16[256,768]{1,0:T(8,128)(2,1)}, bf16[256,768]{1,0:T(8,128)(2,1)S(1)}, u32[]{:S(2)}, u32[]{:S(2)}) %collective-permute-start.9) | collective-permute-done | bytes 393248 | tf_op jit(solution)/shard_map/ppermute | solution.py:819
  153.9 7.8 %mlp_forward.1 = (f32[512,1024]{1,0:T(8,128)}, f32[512,1024]{1,0:T(8,128)}, bf16[512,1024]{1,0:T(8,128)(2,1)}, f32[256,768]{1,0:T(8,128)}, bf16[256,768]{1,0:T(8,128)(2,1)}) custom-call(s32[5]{0:T(128)} %stack.162.scal_ref, bf16[256,768]{1,0:T(8,128)(2,1)} %copy-done.18, bf16[256,768]{1,0:T(8,128)(2,1)} %copy-done.31, ...), custom_call_target="tpu_custom_call" | custom-call | flops 2415919104 | bytes 11927552 | tf_op jit(solution)/shard_map/mlp_forward/pallas_call | solution.py:129
  178.7 7.9 %collective-permute-done.13.other_ref.near_other = bf16[256,768]{1,0:T(8,128)(2,1)} collective-permute-done((bf16[256,768]{1,0:T(8,128)(2,1)S(1)}, bf16[256,768]{1,0:T(8,128)(2,1)}, u32[]{:S(2)}, u32[]{:S(2)}) %collective-permute-start.13) | collective-permute-done | bytes 393248 | tf_op jit(solution)/shard_map/ppermute | solution.py:819
  186.5 13.4 %head_forward.2 = (bf16[512,8192]{1,0:T(8,128)(2,1)}, f32[512,128]{1,0:T(8,128)}, f32[8,512]{1,0:T(8,128)}) custom-call(bf16[256,768]{1,0:T(8,128)(2,1)} %copy-done.35, bf16[256,768]{1,0:T(8,128)(2,1)} %collective-permute-done.13.other_ref.near_other, bf16[768,8032]{1,0:T(8,128)(2,1)} %all-gather.9.cloned.1.call-done.table_ref, s32[512,1]{1,0:T(8,128)} %copy.55.ids_ref), custom_call_target="tpu_custom_call" | custom-call | flops 6316621824 | bytes 21348352 | tf_op jit(solution)/shard_map/head_forward/pallas_call | solution.py:570
  205.2 13.4 %head_forward.3 = (bf16[512,8192]{1,0:T(8,128)(2,1)}, f32[512,128]{1,0:T(8,128)}, f32[8,512]{1,0:T(8,128)}) custom-call(bf16[256,768]{1,0:T(8,128)(2,1)} %collective-permute-done.14.own_ref.far_own, bf16[256,768]{1,0:T(8,128)(2,1)} %collective-permute-done.15.other_ref.far_other, bf16[768,8032]{1,0:T(8,128)(2,1)} %all-gather.9.cloned.1.call-done.table_ref, ...), custom_call_target="tpu_custom_call" | custom-call | flops 6316621824 | bytes 21348352 | tf_op jit(solution)/shard_map/head_forward/pallas_call | solution.py:570
  234.7 21.6 %table_grad.1 = bf16[768,8032]{1,0:T(8,128)(2,1)} custom-call(bf16[256,768]{1,0:T(8,128)(2,1)} %copy-done.35, bf16[256,768]{1,0:T(8,128)(2,1)} %collective-permute-done.13.other_ref.near_other, bf16[512,8192]{1,0:T(8,128)(2,1)} %get-tuple-element.128.near_prob_ref.prob_ref, f32[512,128]{1,0:T(8,128)} %get-tuple-element.133.near_coef_ref.coef_ref, ...), custom_call_target="tpu_custom_call" | custom-call | flops 12633243648 | bytes 30359552 | tf_op jit(solution)/shard_map/table_grad/pallas_call | solution.py:734
  256.6 14.5 %rows_grad.2 = (bf16[256,768]{1,0:T(8,128)(2,1)}, bf16[256,768]{1,0:T(8,128)(2,1)}) custom-call(bf16[768,8032]{1,0:T(8,128)(2,1)} %all-gather.9.cloned.1.call-done.table_ref, bf16[512,8192]{1,0:T(8,128)(2,1)} %get-tuple-element.129.far_prob_ref.prob_ref, f32[512,128]{1,0:T(8,128)} %get-tuple-element.131.far_coef_ref.coef_ref), custom_call_target="tpu_custom_call" | custom-call | flops 6316621824 | bytes 22134784 | tf_op jit(solution)/shard_map/rows_grad/pallas_call | solution.py:693
  273.1 13.6 %rows_grad.3 = (f32[256,768]{1,0:T(8,128)}, bf16[256,768]{1,0:T(8,128)(2,1)}) custom-call(bf16[768,8032]{1,0:T(8,128)(2,1)} %all-gather.9.cloned.1.call-done.table_ref, bf16[512,8192]{1,0:T(8,128)(2,1)} %get-tuple-element.128.near_prob_ref.prob_ref, f32[512,128]{1,0:T(8,128)} %get-tuple-element.133.near_coef_ref.coef_ref), custom_call_target="tpu_custom_call" | custom-call | flops 6316621824 | bytes 22134784 | tf_op jit(solution)/shard_map/rows_grad/pallas_call | solution.py:693
  289.9 12.3 %collective-permute-done.20 = bf16[256,768]{1,0:T(8,128)(2,1)S(1)} collective-permute-done((bf16[256,768]{1,0:T(8,128)(2,1)}, bf16[256,768]{1,0:T(8,128)(2,1)S(1)}, u32[]{:S(2)}, u32[]{:S(2)}) %collective-permute-start.20) | collective-permute-done | bytes 393248 | tf_op jit(solution)/shard_map/ppermute | solution.py:819
  306.3 8.1 %collective-permute-done.23.e_other_ref = bf16[256,768]{1,0:T(8,128)(2,1)S(1)} collective-permute-done((bf16[256,768]{1,0:T(8,128)(2,1)S(1)}, bf16[256,768]{1,0:T(8,128)(2,1)S(1)}, u32[]{:S(2)}, u32[]{:S(2)}) %collective-permute-start.23) | collective-permute-done | bytes 393248 | tf_op jit(solution)/shard_map/ppermute | solution.py:819
  315.1 9.4 %mlp_back.1 = (bf16[512,1024]{1,0:T(8,128)(2,1)}, bf16[512,1024]{1,0:T(8,128)(2,1)}, f32[256,768]{1,0:T(8,128)}, bf16[256,768]{1,0:T(8,128)(2,1)}) custom-call(s32[5]{0:T(128)} %stack.162.scal_ref, bf16[256,768]{1,0:T(8,128)(2,1)} %copy-done, bf16[256,768]{1,0:T(8,128)(2,1)} %copy-done.13, bf16[3,768,1024]{2,1,0:T(8,128)(2,1)} %all-gather.7.cloned.1.call-done.w_ref, ...), custom_call_target="tpu_custom_call" | custom-call | flops 2415919104 | bytes 12976128 | tf_op jit(solution)/shard_map/mlp_back/pallas_call | solution.py:129
  346.3 16.2 %cross_back.1 = (bf16[512,384]{1,0:T(8,128)(2,1)}, bf16[1024,384]{1,0:T(8,128)(2,1)}, bf16[1024,384]{1,0:T(8,128)(2,1)}, f32[256,768]{1,0:T(8,128)}, bf16[256,768]{1,0:T(8,128)(2,1)}) custom-call(s32[5]{0:T(128)} %stack.164.scal_ref, bf16[256,768]{1,0:T(8,128)(2,1)} %copy-done.14, bf16[256,768]{1,0:T(8,128)(2,1)} %copy-done.32, ...), custom_call_target="tpu_custom_call" | custom-call | flops 4630511616 | bytes 10223616 | tf_op jit(solution)/shard_map/cross_back/pallas_call | solution.py:129
  364.1 8.4 %cross_grads.1.rest_ref = bf16[8,768,384]{2,1,0:T(8,128)(2,1)} custom-call(s32[5]{0:T(128)} %stack.162.scal_ref, bf16[256,768]{1,0:T(8,128)(2,1)} %copy-done.17, bf16[256,768]{1,0:T(8,128)(2,1)} %copy-done.30, bf16[256,768]{1,0:T(8,128)(2,1)} %copy-done.14, bf16[256,768]{1,0:T(8,128)(2,1)} %copy-done.32, bf16[256,768]{1,0:T(8,128)(2,1)} %copy-done.16, ...), custom_call_target="tpu_custom_call" | custom-call | flops 1811939328 | bytes 6291456 | tf_op jit(solution)/shard_map/cross_grads/pallas_call | solution.py:129
  379.3 7.9 %collective-permute-done.27.refs_1_.e_other = bf16[256,768]{1,0:T(8,128)(2,1)S(1)} collective-permute-done((bf16[256,768]{1,0:T(8,128)(2,1)S(1)}, bf16[256,768]{1,0:T(8,128)(2,1)S(1)}, u32[]{:S(2)}, u32[]{:S(2)}) %collective-permute-start.27) | collective-permute-done | bytes 393248 | tf_op jit(solution)/shard_map/ppermute | solution.py:819
  387.9 14.0 %self_back.1 = (bf16[512,384]{1,0:T(8,128)(2,1)}, bf16[512,384]{1,0:T(8,128)(2,1)}, bf16[512,384]{1,0:T(8,128)(2,1)}, f32[256,768]{1,0:T(8,128)}, bf16[256,768]{1,0:T(8,128)(2,1)}, /*index=5*/f32[8,768]{1,0:T(8,128)}) custom-call(s32[5]{0:T(128)} %stack.162.scal_ref, bf16[256,768]{1,0:T(8,128)(2,1)} %copy-done.15, bf16[256,768]{1,0:T(8,128)(2,1)} %copy-done.33, ...), custom_call_target="tpu_custom_call" | custom-call | flops 3221225472 | bytes 10223616 | tf_op jit(solution)/shard_map/self_back/pallas_call | solution.py:129
  435.6 11.4 %collective-permute-start.30 = (bf16[3,96,512]{2,1,0:T(8,128)(2,1)S(1)}, bf16[3,96,512]{2,1,0:T(8,128)(2,1)S(1)}, u32[]{:S(2)}, u32[]{:S(2)}) collective-permute-start(bf16[3,96,512]{2,1,0:T(8,128)(2,1)S(1)} %slice.223), channel_id=1, source_target_pairs={{0,2},{1,3},{2,0},{3,1},{4,6},{5,7},{6,4},{7,5},{8,10},{9,11},{10,... | collective-permute-start | bytes 884744 | tf_op jit(solution)/shard_map/ppermute | solution.py:819
  449.0 9.1 %collective-permute-done.28 = bf16[256,768]{1,0:T(8,128)(2,1)S(1)} collective-permute-done((bf16[256,768]{1,0:T(8,128)(2,1)S(1)}, bf16[256,768]{1,0:T(8,128)(2,1)S(1)}, u32[]{:S(2)}, u32[]{:S(2)}) %collective-permute-start.28) | collective-permute-done | bytes 393248 | tf_op jit(solution)/shard_map/ppermute | solution.py:819
  471.7 11.8 %collective-permute-done.38 = bf16[4,96,384]{2,1,0:T(8,128)(2,1)S(1)} collective-permute-done((bf16[4,96,384]{2,1,0:T(8,128)(2,1)S(1)}, bf16[4,96,384]{2,1,0:T(8,128)(2,1)S(1)}, u32[]{:S(2)}, u32[]{:S(2)}) %collective-permute-start.38) | collective-permute-done | bytes 294944 | tf_op jit(solution)/shard_map/ppermute | solution.py:819
  (315 shorter events, 193.3 us)
Async XLA Ops:
  7.2 68.1 %all-gather.5.cloned.1.call-start = ((), (), s32[]{:S(2)}) async-start(), calls=%async_computation.3 | async-start | bytes 5308416 | tf_op jit(solution)/shard_map/all_gather | solution.py:832
  9.1 20.2 %collective-permute-start = (bf16[4,96,384]{2,1,0:T(8,128)(2,1)}, bf16[4,96,384]{2,1,0:T(8,128)(2,1)S(1)}, u32[]{:S(2)}, u32[]{:S(2)}) collective-permute-start(bf16[4,96,384]{2,1,0:T(8,128)(2,1)} %pack_pairs.1), channel_id=1, source_target_pairs={{0,2},{1,3},{2,0},{3,1},{4,6},{5,7},{6,4},{7,5},{8,10},{9,11},{10,... | collective-permute-start | bytes 884744 | tf_op jit(solution)/shard_map/ppermute | solution.py:819
  32.2 81.7 %all-gather.7.cloned.1.call-start = ((), (), s32[]{:S(2)}) async-start(), calls=%async_computation.4 | async-start | bytes 5308416 | tf_op jit(solution)/shard_map/all_gather | solution.py:832
  33.3 19.2 %collective-permute-start.1 = (bf16[128,768]{1,0:T(8,128)(2,1)S(1)}, bf16[128,768]{1,0:T(8,128)(2,1)S(1)}, u32[]{:S(2)}, u32[]{:S(2)}) collective-permute-start(bf16[128,768]{1,0:T(8,128)(2,1)S(1)} %get-tuple-element.98), channel_id=1, source_target_pairs={{0,2},{1,3},{2,0},{3,1},{4,6},{5,7},{6,4},{7,5},{8,10},{9,11},{10,... | collective-permute-start | bytes 589832 | tf_op jit(solution)/shard_map/ppermute | solution.py:819
  33.7 33.7 %collective-permute-start.11 = (bf16[3,96,512]{2,1,0:T(8,128)(2,1)S(1)}, bf16[3,96,512]{2,1,0:T(8,128)(2,1)S(1)}, u32[]{:S(2)}, u32[]{:S(2)}) collective-permute-start(bf16[3,96,512]{2,1,0:T(8,128)(2,1)S(1)} %pad_maximum_fusion.6), channel_id=1, source_target_pairs={{0,2},{1,3},{2,0},{3,1},{4,6},{5,7},{6,4},{7,5},{8,10},{9,11},{10,... | collective-permute-start | bytes 884744 | tf_op jit(solution)/shard_map/ppermute | solution.py:819
  52.6 22.8 %collective-permute-start.4 = (bf16[256,768]{1,0:T(8,128)(2,1)S(1)}, bf16[256,768]{1,0:T(8,128)(2,1)S(1)}, u32[]{:S(2)}, u32[]{:S(2)}) collective-permute-start(bf16[256,768]{1,0:T(8,128)(2,1)S(1)} %get-tuple-element.103), channel_id=1, source_target_pairs={{0,2},{1,3},{2,0},{3,1},{4,6},{5,7},{6,4},{7,5},{8,10},{9,11},{10,... | collective-permute-start | bytes 1179656 | tf_op jit(solution)/shard_map/ppermute | solution.py:819
  52.6 15.7 %collective-permute-start.2 = (bf16[128,768]{1,0:T(8,128)(2,1)S(1)}, bf16[128,768]{1,0:T(8,128)(2,1)S(1)}, u32[]{:S(2)}, u32[]{:S(2)}) collective-permute-start(bf16[128,768]{1,0:T(8,128)(2,1)S(1)} %get-tuple-element.227.refs_0_.refs_7_), channel_id=1, source_target_pairs={{0,1},{1,0},{2,3},{3,2},{4,5},{5,4},{6,7},{7,6},{8,9},{9,8},{10,11... | collective-permute-start | bytes 589832 | tf_op jit(solution)/shard_map/ppermute | solution.py:819
  53.8 21.5 %collective-permute-start.3 = (bf16[128,768]{1,0:T(8,128)(2,1)S(1)}, bf16[128,768]{1,0:T(8,128)(2,1)S(1)}, u32[]{:S(2)}, u32[]{:S(2)}) collective-permute-start(bf16[128,768]{1,0:T(8,128)(2,1)S(1)} %collective-permute-done.1.refs_1_.refs_8_), channel_id=1, source_target_pairs={{0,1},{1,0},{2,3},{3,2},{4,5},{5,4},{6,7},{7,6},{8,9},{9,8},{10,11... | collective-permute-start | bytes 589832 | tf_op jit(solution)/shard_map/ppermute | solution.py:819
  75.4 111.2 %all-gather.9.cloned.1.call-start = ((), (), s32[]{:S(2)}) async-start(), calls=%async_computation.5 | async-start | bytes 13934592 | tf_op jit(solution)/shard_map/all_gather | solution.py:832
  75.5 20.5 %collective-permute-start.6 = (bf16[256,768]{1,0:T(8,128)(2,1)S(1)}, bf16[256,768]{1,0:T(8,128)(2,1)S(1)}, u32[]{:S(2)}, u32[]{:S(2)}) collective-permute-start(bf16[256,768]{1,0:T(8,128)(2,1)S(1)} %collective-permute-done.4.refs_1_), channel_id=1, source_target_pairs={{0,1},{1,0},{2,3},{3,2},{4,5},{5,4},{6,7},{7,6},{8,9},{9,8},{10,11... | collective-permute-start | bytes 1179656 | tf_op jit(solution)/shard_map/ppermute | solution.py:819
  113.9 232.3 %reduce-scatter.4.cloned.1.call-start = ((), (), s32[]{:S(2)}) async-start(), calls=%async_computation.6 | async-start | bytes 13934592 | tf_op jit(solution)/shard_map/reduce_scatter | solution.py:836
  176.0 29.1 %collective-permute-start.14 = (bf16[256,768]{1,0:T(8,128)(2,1)S(1)}, bf16[256,768]{1,0:T(8,128)(2,1)}, u32[]{:S(2)}, u32[]{:S(2)}) collective-permute-start(bf16[256,768]{1,0:T(8,128)(2,1)S(1)} %get-tuple-element.207.own_ref.near_own), channel_id=1, source_target_pairs={{0,2},{1,3},{2,0},{3,1},{4,6},{5,7},{6,4},{7,5},{8,10},{9,11},{10,... | collective-permute-start | bytes 1179656 | tf_op jit(solution)/shard_map/ppermute | solution.py:819
  178.5 26.6 %collective-permute-start.15 = (bf16[256,768]{1,0:T(8,128)(2,1)S(1)}, bf16[256,768]{1,0:T(8,128)(2,1)}, u32[]{:S(2)}, u32[]{:S(2)}) collective-permute-start(bf16[256,768]{1,0:T(8,128)(2,1)S(1)} %get-tuple-element.207.own_ref.near_own), channel_id=1, source_target_pairs={{0,3},{1,2},{2,1},{3,0},{4,7},{5,6},{6,5},{7,4},{8,11},{9,10},{10,... | collective-permute-start | bytes 1179656 | tf_op jit(solution)/shard_map/ppermute | solution.py:819
  256.3 149.4 %reduce-scatter.6.cloned.1.call-start = ((), (), s32[]{:S(2)}) async-start(), calls=%async_computation.7 | async-start | bytes 5308416 | tf_op jit(solution)/shard_map/reduce_scatter | solution.py:836
  256.4 16.7 %collective-permute-start.19 = (bf16[128,768]{1,0:T(8,128)(2,1)S(1)}, bf16[128,768]{1,0:T(8,128)(2,1)S(1)}, u32[]{:S(2)}, u32[]{:S(2)}) collective-permute-start(bf16[128,768]{1,0:T(8,128)(2,1)S(1)} %slice.186), channel_id=1, source_target_pairs={{0,2},{1,3},{2,0},{3,1},{4,6},{5,7},{6,4},{7,5},{8,10},{9,11},{10,... | collective-permute-start | bytes 589832 | tf_op jit(solution)/shard_map/ppermute | solution.py:819
  271.2 15.9 %collective-permute-start.21 = (bf16[256,768]{1,0:T(8,128)(2,1)}, bf16[256,768]{1,0:T(8,128)(2,1)S(1)}, u32[]{:S(2)}, u32[]{:S(2)}) collective-permute-start(bf16[256,768]{1,0:T(8,128)(2,1)} %get-tuple-element.136), channel_id=1, source_target_pairs={{0,1},{1,0},{2,3},{3,2},{4,5},{5,4},{6,7},{7,6},{8,9},{9,8},{10,11... | collective-permute-start | bytes 1179656 | tf_op jit(solution)/shard_map/ppermute | solution.py:819
  287.2 16.4 %collective-permute-start.22 = (bf16[256,768]{1,0:T(8,128)(2,1)S(1)}, bf16[256,768]{1,0:T(8,128)(2,1)S(1)}, u32[]{:S(2)}, u32[]{:S(2)}) collective-permute-start(bf16[256,768]{1,0:T(8,128)(2,1)S(1)} %add_convert_fusion), channel_id=1, source_target_pairs={{0,2},{1,3},{2,0},{3,1},{4,6},{5,7},{6,4},{7,5},{8,10},{9,11},{10,... | collective-permute-start | bytes 1179656 | tf_op jit(solution)/shard_map/ppermute | solution.py:819
  346.2 119.9 %reduce-scatter.8.cloned.1.call-start = ((), (), s32[]{:S(2)}) async-start(), calls=%async_computation.8 | async-start | bytes 5308416 | tf_op jit(solution)/shard_map/reduce_scatter | solution.py:836
  387.2 18.5 %collective-permute-start.29 = (bf16[512,768]{1,0:T(8,128)(2,1)S(1)}, bf16[512,768]{1,0:T(8,128)(2,1)}, u32[]{:S(2)}, u32[]{:S(2)}) collective-permute-start(bf16[512,768]{1,0:T(8,128)(2,1)S(1)} %slice.296), channel_id=1, source_target_pairs={{0,1},{1,0},{2,3},{3,2},{4,5},{5,4},{6,7},{7,6},{8,9},{9,8},{10,11... | collective-permute-start | bytes 2359304 | tf_op jit(solution)/shard_map/ppermute | solution.py:819
  424.3 22.7 %collective-permute-start.31 = (bf16[256,768]{1,0:T(8,128)(2,1)S(1)}, bf16[256,768]{1,0:T(8,128)(2,1)S(1)}, u32[]{:S(2)}, u32[]{:S(2)}) collective-permute-start(bf16[256,768]{1,0:T(8,128)(2,1)S(1)} %slice.297), channel_id=1, source_target_pairs={{0,2},{1,3},{2,0},{3,1},{4,6},{5,7},{6,4},{7,5},{8,10},{9,11},{10,... | collective-permute-start | bytes 1179656 | tf_op jit(solution)/shard_map/ppermute | solution.py:819
  430.0 17.0 %collective-permute-start.36 = (f32[4,768]{1,0:T(4,128)S(1)}, f32[4,768]{1,0:T(4,128)S(1)}, u32[]{:S(2)}, u32[]{:S(2)}) collective-permute-start(f32[4,768]{1,0:T(4,128)S(1)} %add.228), channel_id=1, source_target_pairs={{0,16},{4,20},{8,24},{12,28},{16,0},{20,4},{24,8},{28,12},{1,17},{... | collective-permute-start | bytes 36872 | tf_op jit(solution)/shard_map/ppermute | solution.py:826
  434.0 24.1 %collective-permute-start.28 = (bf16[256,768]{1,0:T(8,128)(2,1)S(1)}, bf16[256,768]{1,0:T(8,128)(2,1)S(1)}, u32[]{:S(2)}, u32[]{:S(2)}) collective-permute-start(bf16[256,768]{1,0:T(8,128)(2,1)S(1)} %copy-done.57), channel_id=1, source_target_pairs={{0,1},{1,0},{2,3},{3,2},{4,5},{5,4},{6,7},{7,6},{8,9},{9,8},{10,11... | collective-permute-start | bytes 1179656 | tf_op jit(solution)/shard_map/ppermute | solution.py:819
  435.6 22.5 %collective-permute-start.30 = (bf16[3,96,512]{2,1,0:T(8,128)(2,1)S(1)}, bf16[3,96,512]{2,1,0:T(8,128)(2,1)S(1)}, u32[]{:S(2)}, u32[]{:S(2)}) collective-permute-start(bf16[3,96,512]{2,1,0:T(8,128)(2,1)S(1)} %slice.223), channel_id=1, source_target_pairs={{0,2},{1,3},{2,0},{3,1},{4,6},{5,7},{6,4},{7,5},{8,10},{9,11},{10,... | collective-permute-start | bytes 884744 | tf_op jit(solution)/shard_map/ppermute | solution.py:819
  467.5 16.0 %collective-permute-start.38 = (bf16[4,96,384]{2,1,0:T(8,128)(2,1)S(1)}, bf16[4,96,384]{2,1,0:T(8,128)(2,1)S(1)}, u32[]{:S(2)}, u32[]{:S(2)}) collective-permute-start(bf16[4,96,384]{2,1,0:T(8,128)(2,1)S(1)} %pad_maximum_fusion.7), channel_id=1, source_target_pairs={{0,2},{1,3},{2,0},{3,1},{4,6},{5,7},{6,4},{7,5},{8,10},{9,11},{10,... | collective-permute-start | bytes 884744 | tf_op jit(solution)/shard_map/ppermute | solution.py:819
  (83 other events, 1170.0 us)
Sparse Core Ops, SparseCore 0:
  32.3 37.4 all-gather.4
  75.5 36.8 all-gather.6
  114.3 71.3 all-gather.8
  256.4 89.6 reduce-scatter.3
  349.9 53.8 reduce-scatter.5
  412.8 53.1 reduce-scatter.7

commit v5 on v4

--- a/solution.py
+++ b/solution.py
@@ -959,7 +959,10 @@
 
     normed_two, inverse_two = norm_rows(residual_one, gain_cross)
     own_two = normed_two.astype(BF16)
-    rows_two = (own_two, swap(own_two, 1))
+    other_two, info, near_ids, far_ids = lax.optimization_barrier(
+        (swap(own_two, 1), info, near_ids, far_ids)
+    )
+    rows_two = (own_two, other_two)
     q_two, mixed_two, lse_two, own_terms, other_terms = cross_forward(
         cross_scal, *rows_two, w_both, k_two, v_two
     )
@@ -968,10 +971,7 @@
 
     normed_three, inverse_three = norm_rows(residual_two, gain_mlp)
     own_three = normed_three.astype(BF16)
-    other_three, info, near_ids, far_ids = lax.optimization_barrier(
-        (swap(own_three, 1), info, near_ids, far_ids)
-    )
-    rows_three = (own_three, other_three)
+    rows_three = (own_three, swap(own_three, 1))
     gate, up_proj, hidden, own_terms, other_terms = mlp_forward(self_scal, *rows_three, w_mlp)
     residual_three = residual_two + own_terms + swap(other_terms, 1).astype(F32)
     finished = residual_three.astype(BF16)

time: 498 us -> 493 us (0.990)
  waiting for transfers between devices: 164 us -> 159 us
    ppermute x34, waiting for transfers between devices: 156 us -> 145 us  [swap(): return lax.ppermute(values, 'mp', [(i, i ^ step) for i in range(4)])]
    all_gather x3, waiting for transfers between devices: 0.02 us -> 7.62 us  [gather_batch(): return lax.all_gather(values, 'batch', axis=axis, tiled=True)]
  transfers between devices with their start and end apart: 45 -> 45, of which waited for: 28 -> 25; matrix products, arithmetic and copies ran while one was open for 11% -> 11% of each run, Pallas kernels for 26% -> 26%
where the time goes in v5:
time: 493 us; the launch traced here: 487 us
  Pallas kernels  177 us (36%)
  waiting for transfers between devices  159 us (32%)
  starting transfers between devices  61.4 us (12%)
  other arithmetic  29.4 us (6%)
  local copies, waits for them, and re-layouts  23.1 us (5%)
  between operations  17.8 us (4%)
  matrix products  10.3 us (2%)
  blocking collectives  8.9 us (2%)
    ppermute x34, waiting for transfers between devices, swap(): return lax.ppermute(values, 'mp', [(i, i ^ step) for i in range(4)])  145 us
    pallas_call x8, Pallas kernels, sublayer(): pl.pallas_call(kernel, out_shape=outs, grid_spec=pltpu.PrefetchScalarGrid...  86.4 us
    ppermute x34, starting transfers between devices, swap(): return lax.ppermute(values, 'mp', [(i, i ^ step) for i in range(4)])  54.3 us
    pallas_call x2, Pallas kernels, rows_grad(): pl.pallas_call(functools.partial(rows_grad_kernel, vocab), out_shape=(siz...  28.2 us
    pallas_call x2, Pallas kernels, head_forward(): pl.pallas_call(functools.partial(head_kernel, vocab, scale), out_shape=(j...  26.8 us
    pallas_call x1, Pallas kernels, table_grad(): pl.pallas_call(table_grad_kernel, out_shape=sized((width, vocab), BF16),...  21.7 us
  transfers between devices with their start and end apart: 45, of which 25 were waited for; matrix products, arithmetic and copies ran while one was open for 11% of the time, Pallas kernels for 26%

profile of v5, /device:TPU:0, one launch (start us, length us, event | category | flops | bytes accessed | tf_op | source)
XLA Modules:
  0.0 487.0 jit_solution(5861583389248430899)
XLA Ops:
  20.3 8.9 %all-gather = bf16[8,96,4]{1,2,0:T(4,128)(2,1)S(1)} all-gather(bf16[1,96,4]{1,2,0:T(4,128)(2,1)S(1)} %maximum_bitcast_fusion), channel_id=1, replica_groups=mesh['batch'=8,'mp'=4] {'batch'}, dimensions={0}, use_global_device_ids=true | all-gather | bytes 6912 | tf_op jit(solution)/shard_map/all_gather | solution.py:929
  36.4 16.2 %collective-permute-done.1.refs_1_.refs_8_ = bf16[128,768]{1,0:T(8,128)(2,1)S(1)} collective-permute-done((bf16[128,768]{1,0:T(8,128)(2,1)S(1)}, bf16[128,768]{1,0:T(8,128)(2,1)S(1)}, u32[]{:S(2)}, u32[]{:S(2)}) %collective-permute-start.1) | collective-permute-done | bytes 196640 | tf_op jit(solution)/shard_map/ppermute | solution.py:819
  54.6 12.8 %collective-permute-done.11 = bf16[3,96,512]{2,1,0:T(8,128)(2,1)S(1)} collective-permute-done((bf16[3,96,512]{2,1,0:T(8,128)(2,1)S(1)}, bf16[3,96,512]{2,1,0:T(8,128)(2,1)S(1)}, u32[]{:S(2)}, u32[]{:S(2)}) %collective-permute-start.11) | collective-permute-done | bytes 294944 | tf_op jit(solution)/shard_map/ppermute | solution.py:819
  82.8 10.4 %self_forward.1 = (bf16[512,384]{1,0:T(8,128)(2,1)}, bf16[512,384]{1,0:T(8,128)(2,1)}, bf16[512,384]{1,0:T(8,128)(2,1)}, bf16[512,384]{1,0:T(8,128)(2,1)}, f32[5...) custom-call(s32[5]{0:T(128)} %stack.162.scal_ref, ...), custom_call_target="tpu_custom_call" | custom-call | flops 2013265920 | bytes 7864320 | tf_op jit(solution)/shard_map/self_forward/pallas_call | solution.py:129
  109.9 8.6 %collective-permute-done.8.h_other_ref.h_other = bf16[256,768]{1,0:T(8,128)(2,1)S(1)} collective-permute-done((bf16[256,768]{1,0:T(8,128)(2,1)S(1)}, bf16[256,768]{1,0:T(8,128)(2,1)S(1)}, u32[]{:S(2)}, u32[]{:S(2)}) %collective-permute-start.8) | collective-permute-done | bytes 393248 | tf_op jit(solution)/shard_map/ppermute | solution.py:819
  119.3 12.5 %cross_forward.1 = (bf16[512,384]{1,0:T(8,128)(2,1)}, bf16[512,384]{1,0:T(8,128)(2,1)}, f32[512,384]{1,0:T(8,128)}, f32[256,768]{1,0:T(8,128)}, bf16[256,768]{1,0:T(8,128)(2,1)}) custom-call(s32[5]{0:T(128)} %stack.164.scal_ref, bf16[256,768]{1,0:T(8,128)(2,1)} %copy-done.17, bf16[256,768]{1,0:T(8,128)(2,1)} %copy-done.30, ...), custom_call_target="tpu_custom_call" | custom-call | flops 2214592512 | bytes 8650752 | tf_op jit(solution)/shard_map/cross_forward/pallas_call | solution.py:129
  132.4 8.3 %collective-permute-done.9 = bf16[256,768]{1,0:T(8,128)(2,1)S(1)} collective-permute-done((bf16[256,768]{1,0:T(8,128)(2,1)}, bf16[256,768]{1,0:T(8,128)(2,1)S(1)}, u32[]{:S(2)}, u32[]{:S(2)}) %collective-permute-start.9) | collective-permute-done | bytes 393248 | tf_op jit(solution)/shard_map/ppermute | solution.py:819
  151.3 8.5 %mlp_forward.1 = (f32[512,1024]{1,0:T(8,128)}, f32[512,1024]{1,0:T(8,128)}, bf16[512,1024]{1,0:T(8,128)(2,1)}, f32[256,768]{1,0:T(8,128)}, bf16[256,768]{1,0:T(8,128)(2,1)}) custom-call(s32[5]{0:T(128)} %stack.162.scal_ref, bf16[256,768]{1,0:T(8,128)(2,1)} %copy-done.18, bf16[256,768]{1,0:T(8,128)(2,1)} %copy-done.31, ...), custom_call_target="tpu_custom_call" | custom-call | flops 2415919104 | bytes 11927552 | tf_op jit(solution)/shard_map/mlp_forward/pallas_call | solution.py:129
  161.3 7.7 %collective-permute-done.12 = bf16[256,768]{1,0:T(8,128)(2,1)S(1)} collective-permute-done((bf16[256,768]{1,0:T(8,128)(2,1)}, bf16[256,768]{1,0:T(8,128)(2,1)S(1)}, u32[]{:S(2)}, u32[]{:S(2)}) %collective-permute-start.12) | collective-permute-done | bytes 393248 | tf_op jit(solution)/shard_map/ppermute | solution.py:819
  181.5 7.6 %all-gather.9.cloned.1.call-done.table_ref = bf16[768,8032]{1,0:T(8,128)(2,1)} async-done(((bf16[96,8032]{1,0:T(8,128)(2,1)}), bf16[768,8032]{1,0:T(8,128)(2,1)}) %all-gather.9.cloned.1.call-update) | async-done | bytes 12337168 | tf_op jit(solution)/shard_map/all_gather | solution.py:832
  189.1 13.4 %head_forward.2 = (bf16[512,8192]{1,0:T(8,128)(2,1)}, f32[512,128]{1,0:T(8,128)}, f32[8,512]{1,0:T(8,128)}) custom-call(bf16[256,768]{1,0:T(8,128)(2,1)} %copy-done.35, bf16[256,768]{1,0:T(8,128)(2,1)} %collective-permute-done.13.other_ref.near_other, bf16[768,8032]{1,0:T(8,128)(2,1)} %all-gather.9.cloned.1.call-done.table_ref, s32[512,1]{1,0:T(8,128)} %copy.55.ids_ref), custom_call_target="tpu_custom_call" | custom-call | flops 6316621824 | bytes 21348352 | tf_op jit(solution)/shard_map/head_forward/pallas_call | solution.py:570
  203.2 13.4 %head_forward.3 = (bf16[512,8192]{1,0:T(8,128)(2,1)}, f32[512,128]{1,0:T(8,128)}, f32[8,512]{1,0:T(8,128)}) custom-call(bf16[256,768]{1,0:T(8,128)(2,1)} %collective-permute-done.14.own_ref.far_own, bf16[256,768]{1,0:T(8,128)(2,1)} %collective-permute-done.15.other_ref.far_other, bf16[768,8032]{1,0:T(8,128)(2,1)} %all-gather.9.cloned.1.call-done.table_ref, ...), custom_call_target="tpu_custom_call" | custom-call | flops 6316621824 | bytes 21348352 | tf_op jit(solution)/shard_map/head_forward/pallas_call | solution.py:570
  230.4 21.7 %table_grad.1 = bf16[768,8032]{1,0:T(8,128)(2,1)} custom-call(bf16[256,768]{1,0:T(8,128)(2,1)} %copy-done.35, bf16[256,768]{1,0:T(8,128)(2,1)} %collective-permute-done.13.other_ref.near_other, bf16[512,8192]{1,0:T(8,128)(2,1)} %get-tuple-element.128.near_prob_ref.prob_ref, f32[512,128]{1,0:T(8,128)} %get-tuple-element.133.near_coef_ref.coef_ref, ...), custom_call_target="tpu_custom_call" | custom-call | flops 12633243648 | bytes 30359552 | tf_op jit(solution)/shard_map/table_grad/pallas_call | solution.py:734
  252.3 14.6 %rows_grad.2 = (bf16[256,768]{1,0:T(8,128)(2,1)}, bf16[256,768]{1,0:T(8,128)(2,1)}) custom-call(bf16[768,8032]{1,0:T(8,128)(2,1)} %all-gather.9.cloned.1.call-done.table_ref, bf16[512,8192]{1,0:T(8,128)(2,1)} %get-tuple-element.129.far_prob_ref.prob_ref, f32[512,128]{1,0:T(8,128)} %get-tuple-element.131.far_coef_ref.coef_ref), custom_call_target="tpu_custom_call" | custom-call | flops 6316621824 | bytes 22134784 | tf_op jit(solution)/shard_map/rows_grad/pallas_call | solution.py:693
  268.9 13.6 %rows_grad.3 = (f32[256,768]{1,0:T(8,128)}, bf16[256,768]{1,0:T(8,128)(2,1)}) custom-call(bf16[768,8032]{1,0:T(8,128)(2,1)} %all-gather.9.cloned.1.call-done.table_ref, bf16[512,8192]{1,0:T(8,128)(2,1)} %get-tuple-element.128.near_prob_ref.prob_ref, f32[512,128]{1,0:T(8,128)} %get-tuple-element.133.near_coef_ref.coef_ref), custom_call_target="tpu_custom_call" | custom-call | flops 6316621824 | bytes 22134784 | tf_op jit(solution)/shard_map/rows_grad/pallas_call | solution.py:693
  285.6 13.6 %collective-permute-done.20 = bf16[256,768]{1,0:T(8,128)(2,1)S(1)} collective-permute-done((bf16[256,768]{1,0:T(8,128)(2,1)}, bf16[256,768]{1,0:T(8,128)(2,1)S(1)}, u32[]{:S(2)}, u32[]{:S(2)}) %collective-permute-start.20) | collective-permute-done | bytes 393248 | tf_op jit(solution)/shard_map/ppermute | solution.py:819
  304.5 7.4 %collective-permute-done.23.e_other_ref = bf16[256,768]{1,0:T(8,128)(2,1)S(1)} collective-permute-done((bf16[256,768]{1,0:T(8,128)(2,1)S(1)}, bf16[256,768]{1,0:T(8,128)(2,1)S(1)}, u32[]{:S(2)}, u32[]{:S(2)}) %collective-permute-start.23) | collective-permute-done | bytes 393248 | tf_op jit(solution)/shard_map/ppermute | solution.py:819
  312.6 9.4 %mlp_back.1 = (bf16[512,1024]{1,0:T(8,128)(2,1)}, bf16[512,1024]{1,0:T(8,128)(2,1)}, f32[256,768]{1,0:T(8,128)}, bf16[256,768]{1,0:T(8,128)(2,1)}) custom-call(s32[5]{0:T(128)} %stack.162.scal_ref, bf16[256,768]{1,0:T(8,128)(2,1)} %copy-done, bf16[256,768]{1,0:T(8,128)(2,1)} %copy-done.13, bf16[3,768,1024]{2,1,0:T(8,128)(2,1)} %all-gather.7.cloned.1.call-done.w_ref, ...), custom_call_target="tpu_custom_call" | custom-call | flops 2415919104 | bytes 12976128 | tf_op jit(solution)/shard_map/mlp_back/pallas_call | solution.py:129
  344.7 16.2 %cross_back.1 = (bf16[512,384]{1,0:T(8,128)(2,1)}, bf16[1024,384]{1,0:T(8,128)(2,1)}, bf16[1024,384]{1,0:T(8,128)(2,1)}, f32[256,768]{1,0:T(8,128)}, bf16[256,768]{1,0:T(8,128)(2,1)}) custom-call(s32[5]{0:T(128)} %stack.164.scal_ref, bf16[256,768]{1,0:T(8,128)(2,1)} %copy-done.14, bf16[256,768]{1,0:T(8,128)(2,1)} %copy-done.32, ...), custom_call_target="tpu_custom_call" | custom-call | flops 4630511616 | bytes 10223616 | tf_op jit(solution)/shard_map/cross_back/pallas_call | solution.py:129
  361.5 8.4 %cross_grads.1.rest_ref = bf16[8,768,384]{2,1,0:T(8,128)(2,1)} custom-call(s32[5]{0:T(128)} %stack.162.scal_ref, bf16[256,768]{1,0:T(8,128)(2,1)} %copy-done.17, bf16[256,768]{1,0:T(8,128)(2,1)} %copy-done.30, bf16[256,768]{1,0:T(8,128)(2,1)} %copy-done.14, bf16[256,768]{1,0:T(8,128)(2,1)} %copy-done.32, bf16[256,768]{1,0:T(8,128)(2,1)} %copy-done.16, ...), custom_call_target="tpu_custom_call" | custom-call | flops 1811939328 | bytes 6291456 | tf_op jit(solution)/shard_map/cross_grads/pallas_call | solution.py:129
  383.7 14.1 %self_back.1 = (bf16[512,384]{1,0:T(8,128)(2,1)}, bf16[512,384]{1,0:T(8,128)(2,1)}, bf16[512,384]{1,0:T(8,128)(2,1)}, f32[256,768]{1,0:T(8,128)}, bf16[256,768]{1,0:T(8,128)(2,1)}, /*index=5*/f32[8,768]{1,0:T(8,128)}) custom-call(s32[5]{0:T(128)} %stack.162.scal_ref, bf16[256,768]{1,0:T(8,128)(2,1)} %copy-done.15, bf16[256,768]{1,0:T(8,128)(2,1)} %copy-done.33, ...), custom_call_target="tpu_custom_call" | custom-call | flops 3221225472 | bytes 10223616 | tf_op jit(solution)/shard_map/self_back/pallas_call | solution.py:129
  430.7 11.4 %collective-permute-start.30 = (bf16[3,96,512]{2,1,0:T(8,128)(2,1)S(1)}, bf16[3,96,512]{2,1,0:T(8,128)(2,1)S(1)}, u32[]{:S(2)}, u32[]{:S(2)}) collective-permute-start(bf16[3,96,512]{2,1,0:T(8,128)(2,1)S(1)} %slice.223), channel_id=1, source_target_pairs={{0,2},{1,3},{2,0},{3,1},{4,6},{5,7},{6,4},{7,5},{8,10},{9,11},{10,... | collective-permute-start | bytes 884744 | tf_op jit(solution)/shard_map/ppermute | solution.py:819
  444.1 9.5 %collective-permute-done.28 = bf16[256,768]{1,0:T(8,128)(2,1)S(1)} collective-permute-done((bf16[256,768]{1,0:T(8,128)(2,1)S(1)}, bf16[256,768]{1,0:T(8,128)(2,1)S(1)}, u32[]{:S(2)}, u32[]{:S(2)}) %collective-permute-start.28) | collective-permute-done | bytes 393248 | tf_op jit(solution)/shard_map/ppermute | solution.py:819
  467.5 11.4 %collective-permute-done.38 = bf16[4,96,384]{2,1,0:T(8,128)(2,1)S(1)} collective-permute-done((bf16[4,96,384]{2,1,0:T(8,128)(2,1)S(1)}, bf16[4,96,384]{2,1,0:T(8,128)(2,1)S(1)}, u32[]{:S(2)}, u32[]{:S(2)}) %collective-permute-start.38) | collective-permute-done | bytes 294944 | tf_op jit(solution)/shard_map/ppermute | solution.py:819
  (315 shorter events, 189.8 us)
Async XLA Ops:
  7.2 68.1 %all-gather.5.cloned.1.call-start = ((), (), s32[]{:S(2)}) async-start(), calls=%async_computation.3 | async-start | bytes 5308416 | tf_op jit(solution)/shard_map/all_gather | solution.py:832
  9.1 20.2 %collective-permute-start = (bf16[4,96,384]{2,1,0:T(8,128)(2,1)}, bf16[4,96,384]{2,1,0:T(8,128)(2,1)S(1)}, u32[]{:S(2)}, u32[]{:S(2)}) collective-permute-start(bf16[4,96,384]{2,1,0:T(8,128)(2,1)} %pack_pairs.1), channel_id=1, source_target_pairs={{0,2},{1,3},{2,0},{3,1},{4,6},{5,7},{6,4},{7,5},{8,10},{9,11},{10,... | collective-permute-start | bytes 884744 | tf_op jit(solution)/shard_map/ppermute | solution.py:819
  32.2 86.3 %all-gather.7.cloned.1.call-start = ((), (), s32[]{:S(2)}) async-start(), calls=%async_computation.4 | async-start | bytes 5308416 | tf_op jit(solution)/shard_map/all_gather | solution.py:832
  33.4 19.2 %collective-permute-start.1 = (bf16[128,768]{1,0:T(8,128)(2,1)S(1)}, bf16[128,768]{1,0:T(8,128)(2,1)S(1)}, u32[]{:S(2)}, u32[]{:S(2)}) collective-permute-start(bf16[128,768]{1,0:T(8,128)(2,1)S(1)} %get-tuple-element.98), channel_id=1, source_target_pairs={{0,2},{1,3},{2,0},{3,1},{4,6},{5,7},{6,4},{7,5},{8,10},{9,11},{10,... | collective-permute-start | bytes 589832 | tf_op jit(solution)/shard_map/ppermute | solution.py:819
  33.8 33.7 %collective-permute-start.11 = (bf16[3,96,512]{2,1,0:T(8,128)(2,1)S(1)}, bf16[3,96,512]{2,1,0:T(8,128)(2,1)S(1)}, u32[]{:S(2)}, u32[]{:S(2)}) collective-permute-start(bf16[3,96,512]{2,1,0:T(8,128)(2,1)S(1)} %pad_maximum_fusion.6), channel_id=1, source_target_pairs={{0,2},{1,3},{2,0},{3,1},{4,6},{5,7},{6,4},{7,5},{8,10},{9,11},{10,... | collective-permute-start | bytes 884744 | tf_op jit(solution)/shard_map/ppermute | solution.py:819
  52.6 22.8 %collective-permute-start.4 = (bf16[256,768]{1,0:T(8,128)(2,1)S(1)}, bf16[256,768]{1,0:T(8,128)(2,1)S(1)}, u32[]{:S(2)}, u32[]{:S(2)}) collective-permute-start(bf16[256,768]{1,0:T(8,128)(2,1)S(1)} %get-tuple-element.103), channel_id=1, source_target_pairs={{0,2},{1,3},{2,0},{3,1},{4,6},{5,7},{6,4},{7,5},{8,10},{9,11},{10,... | collective-permute-start | bytes 1179656 | tf_op jit(solution)/shard_map/ppermute | solution.py:819
  53.8 21.5 %collective-permute-start.3 = (bf16[128,768]{1,0:T(8,128)(2,1)S(1)}, bf16[128,768]{1,0:T(8,128)(2,1)S(1)}, u32[]{:S(2)}, u32[]{:S(2)}) collective-permute-start(bf16[128,768]{1,0:T(8,128)(2,1)S(1)} %collective-permute-done.1.refs_1_.refs_8_), channel_id=1, source_target_pairs={{0,1},{1,0},{2,3},{3,2},{4,5},{5,4},{6,7},{7,6},{8,9},{9,8},{10,11... | collective-permute-start | bytes 589832 | tf_op jit(solution)/shard_map/ppermute | solution.py:819
  75.4 113.7 %all-gather.9.cloned.1.call-start = ((), (), s32[]{:S(2)}) async-start(), calls=%async_computation.5 | async-start | bytes 13934592 | tf_op jit(solution)/shard_map/all_gather | solution.py:832
  80.1 20.5 %collective-permute-start.6 = (bf16[256,768]{1,0:T(8,128)(2,1)S(1)}, bf16[256,768]{1,0:T(8,128)(2,1)S(1)}, u32[]{:S(2)}, u32[]{:S(2)}) collective-permute-start(bf16[256,768]{1,0:T(8,128)(2,1)S(1)} %collective-permute-done.4.refs_1_), channel_id=1, source_target_pairs={{0,1},{1,0},{2,3},{3,2},{4,5},{5,4},{6,7},{7,6},{8,9},{9,8},{10,11... | collective-permute-start | bytes 1179656 | tf_op jit(solution)/shard_map/ppermute | solution.py:819
  118.5 225.4 %reduce-scatter.4.cloned.1.call-start = ((), (), s32[]{:S(2)}) async-start(), calls=%async_computation.6 | async-start | bytes 13934592 | tf_op jit(solution)/shard_map/reduce_scatter | solution.py:836
  173.4 29.8 %collective-permute-start.14 = (bf16[256,768]{1,0:T(8,128)(2,1)S(1)}, bf16[256,768]{1,0:T(8,128)(2,1)}, u32[]{:S(2)}, u32[]{:S(2)}) collective-permute-start(bf16[256,768]{1,0:T(8,128)(2,1)S(1)} %get-tuple-element.207.own_ref.near_own), channel_id=1, source_target_pairs={{0,2},{1,3},{2,0},{3,1},{4,6},{5,7},{6,4},{7,5},{8,10},{9,11},{10,... | collective-permute-start | bytes 1179656 | tf_op jit(solution)/shard_map/ppermute | solution.py:819
  176.4 26.8 %collective-permute-start.15 = (bf16[256,768]{1,0:T(8,128)(2,1)S(1)}, bf16[256,768]{1,0:T(8,128)(2,1)}, u32[]{:S(2)}, u32[]{:S(2)}) collective-permute-start(bf16[256,768]{1,0:T(8,128)(2,1)S(1)} %get-tuple-element.207.own_ref.near_own), channel_id=1, source_target_pairs={{0,3},{1,2},{2,1},{3,0},{4,7},{5,6},{6,5},{7,4},{8,11},{9,10},{10,... | collective-permute-start | bytes 1179656 | tf_op jit(solution)/shard_map/ppermute | solution.py:819
  252.1 147.6 %reduce-scatter.6.cloned.1.call-start = ((), (), s32[]{:S(2)}) async-start(), calls=%async_computation.7 | async-start | bytes 5308416 | tf_op jit(solution)/shard_map/reduce_scatter | solution.py:836
  252.2 16.7 %collective-permute-start.19 = (bf16[128,768]{1,0:T(8,128)(2,1)S(1)}, bf16[128,768]{1,0:T(8,128)(2,1)S(1)}, u32[]{:S(2)}, u32[]{:S(2)}) collective-permute-start(bf16[128,768]{1,0:T(8,128)(2,1)S(1)} %slice.186), channel_id=1, source_target_pairs={{0,2},{1,3},{2,0},{3,1},{4,6},{5,7},{6,4},{7,5},{8,10},{9,11},{10,... | collective-permute-start | bytes 589832 | tf_op jit(solution)/shard_map/ppermute | solution.py:819
  266.9 15.9 %collective-permute-start.21 = (bf16[256,768]{1,0:T(8,128)(2,1)}, bf16[256,768]{1,0:T(8,128)(2,1)S(1)}, u32[]{:S(2)}, u32[]{:S(2)}) collective-permute-start(bf16[256,768]{1,0:T(8,128)(2,1)} %get-tuple-element.136), channel_id=1, source_target_pairs={{0,1},{1,0},{2,3},{3,2},{4,5},{5,4},{6,7},{7,6},{8,9},{9,8},{10,11... | collective-permute-start | bytes 1179656 | tf_op jit(solution)/shard_map/ppermute | solution.py:819
  282.5 16.7 %collective-permute-start.20 = (bf16[256,768]{1,0:T(8,128)(2,1)}, bf16[256,768]{1,0:T(8,128)(2,1)S(1)}, u32[]{:S(2)}, u32[]{:S(2)}) collective-permute-start(bf16[256,768]{1,0:T(8,128)(2,1)} %get-tuple-element.135), channel_id=1, source_target_pairs={{0,1},{1,0},{2,3},{3,2},{4,5},{5,4},{6,7},{7,6},{8,9},{9,8},{10,11... | collective-permute-start | bytes 1179656 | tf_op jit(solution)/shard_map/ppermute | solution.py:819
  282.9 18.9 %collective-permute-start.22 = (bf16[256,768]{1,0:T(8,128)(2,1)S(1)}, bf16[256,768]{1,0:T(8,128)(2,1)S(1)}, u32[]{:S(2)}, u32[]{:S(2)}) collective-permute-start(bf16[256,768]{1,0:T(8,128)(2,1)S(1)} %add_convert_fusion), channel_id=1, source_target_pairs={{0,2},{1,3},{2,0},{3,1},{4,6},{5,7},{6,4},{7,5},{8,10},{9,11},{10,... | collective-permute-start | bytes 1179656 | tf_op jit(solution)/shard_map/ppermute | solution.py:819
  343.9 117.2 %reduce-scatter.8.cloned.1.call-start = ((), (), s32[]{:S(2)}) async-start(), calls=%async_computation.8 | async-start | bytes 5308416 | tf_op jit(solution)/shard_map/reduce_scatter | solution.py:836
  382.9 16.8 %collective-permute-start.29 = (bf16[512,768]{1,0:T(8,128)(2,1)S(1)}, bf16[512,768]{1,0:T(8,128)(2,1)}, u32[]{:S(2)}, u32[]{:S(2)}) collective-permute-start(bf16[512,768]{1,0:T(8,128)(2,1)S(1)} %slice.296), channel_id=1, source_target_pairs={{0,1},{1,0},{2,3},{3,2},{4,5},{5,4},{6,7},{7,6},{8,9},{9,8},{10,11... | collective-permute-start | bytes 2359304 | tf_op jit(solution)/shard_map/ppermute | solution.py:819
  419.5 22.6 %collective-permute-start.31 = (bf16[256,768]{1,0:T(8,128)(2,1)S(1)}, bf16[256,768]{1,0:T(8,128)(2,1)S(1)}, u32[]{:S(2)}, u32[]{:S(2)}) collective-permute-start(bf16[256,768]{1,0:T(8,128)(2,1)S(1)} %slice.297), channel_id=1, source_target_pairs={{0,2},{1,3},{2,0},{3,1},{4,6},{5,7},{6,4},{7,5},{8,10},{9,11},{10,... | collective-permute-start | bytes 1179656 | tf_op jit(solution)/shard_map/ppermute | solution.py:819
  425.0 17.1 %collective-permute-start.36 = (f32[4,768]{1,0:T(4,128)S(1)}, f32[4,768]{1,0:T(4,128)S(1)}, u32[]{:S(2)}, u32[]{:S(2)}) collective-permute-start(f32[4,768]{1,0:T(4,128)S(1)} %add.228), channel_id=1, source_target_pairs={{0,16},{4,20},{8,24},{12,28},{16,0},{20,4},{24,8},{28,12},{1,17},{... | collective-permute-start | bytes 36872 | tf_op jit(solution)/shard_map/ppermute | solution.py:826
  429.1 24.6 %collective-permute-start.28 = (bf16[256,768]{1,0:T(8,128)(2,1)S(1)}, bf16[256,768]{1,0:T(8,128)(2,1)S(1)}, u32[]{:S(2)}, u32[]{:S(2)}) collective-permute-start(bf16[256,768]{1,0:T(8,128)(2,1)S(1)} %copy-done.57), channel_id=1, source_target_pairs={{0,1},{1,0},{2,3},{3,2},{4,5},{5,4},{6,7},{7,6},{8,9},{9,8},{10,11... | collective-permute-start | bytes 1179656 | tf_op jit(solution)/shard_map/ppermute | solution.py:819
  430.7 22.9 %collective-permute-start.30 = (bf16[3,96,512]{2,1,0:T(8,128)(2,1)S(1)}, bf16[3,96,512]{2,1,0:T(8,128)(2,1)S(1)}, u32[]{:S(2)}, u32[]{:S(2)}) collective-permute-start(bf16[3,96,512]{2,1,0:T(8,128)(2,1)S(1)} %slice.223), channel_id=1, source_target_pairs={{0,2},{1,3},{2,0},{3,1},{4,6},{5,7},{6,4},{7,5},{8,10},{9,11},{10,... | collective-permute-start | bytes 884744 | tf_op jit(solution)/shard_map/ppermute | solution.py:819
  462.6 16.3 %collective-permute-start.38 = (bf16[4,96,384]{2,1,0:T(8,128)(2,1)S(1)}, bf16[4,96,384]{2,1,0:T(8,128)(2,1)S(1)}, u32[]{:S(2)}, u32[]{:S(2)}) collective-permute-start(bf16[4,96,384]{2,1,0:T(8,128)(2,1)S(1)} %pad_maximum_fusion.7), channel_id=1, source_target_pairs={{0,2},{1,3},{2,0},{3,1},{4,6},{5,7},{6,4},{7,5},{8,10},{9,11},{10,... | collective-permute-start | bytes 884744 | tf_op jit(solution)/shard_map/ppermute | solution.py:819
  (83 other events, 1284.3 us)
Sparse Core Ops, SparseCore 0:
  32.3 37.4 all-gather.4
  75.5 36.8 all-gather.6
  118.7 70.3 all-gather.8
  252.3 89.4 reduce-scatter.3
  345.5 53.8 reduce-scatter.5
  406.9 54.2 reduce-scatter.7
